TPU v7x, 32 devices: a whole 2x2x4 slice. The times are simulated.
32 devices in a mesh: ctx: 4 (over x, core), wsh: 8 (over z, y).
Axes of the slice: x: 2, y: 2, z: 4, core: 2. Of those that a mesh axis runs over, the one named last changes fastest.
Arguments:
- inputs: bfloat16 [8, 1024, 1024], P('wsh', 'ctx'), may hold values from -6 to 6
- enc_states: bfloat16 [8, 512, 1024], P('wsh', 'ctx'), may hold values from -6 to 6
- cotangent: bfloat16 [8, 1024, 1024], P('wsh', 'ctx'), may hold values from -6 to 6
- slot_order: int32 [8, 1024], P('wsh'), may hold values from 0 to 1023, each once within a row
- seq_lengths: int32 [8, 8], P('wsh'), may hold values from 1 to 512, 1024 in all within a row
- enc_lengths: int32 [8, 8], P('wsh'), may hold values from 1 to 256, 512 in all within a row
- self_query: bfloat16 [1024, 1024], P('wsh'), may hold values from -0.1875 to 0.1875
- self_key: bfloat16 [1024, 1024], P('wsh'), may hold values from -0.1875 to 0.1875
- self_value: bfloat16 [1024, 1024], P('wsh'), may hold values from -0.1875 to 0.1875
- self_out: bfloat16 [1024, 1024], P('wsh'), may hold values from -1 to 1
- cross_query: bfloat16 [1024, 1024], P('wsh'), may hold values from -0.1875 to 0.1875
- cross_key: bfloat16 [1024, 1024], P('wsh'), may hold values from -0.1875 to 0.1875
- cross_value: bfloat16 [1024, 1024], P('wsh'), may hold values from -0.1875 to 0.1875
- cross_out: bfloat16 [1024, 1024], P('wsh'), may hold values from -1 to 1
- feed_in: bfloat16 [1024, 4096], P('wsh'), may hold values from -0.1875 to 0.1875
- feed_out: bfloat16 [4096, 1024], P('wsh'), may hold values from -0.09375 to 0.09375
- norm_gains: bfloat16 [1024, 4], P('wsh'), may hold values from 0.5 to 1.5
- norm_shifts: bfloat16 [1024, 4], P('wsh'), may hold values from -1 to 1
Outputs:
- output: float32 [8, 1024, 1024], P('wsh', 'ctx')
- input_grad: float32 [8, 1024, 1024], P('wsh', 'ctx')
- enc_grad: float32 [8, 512, 1024], P('wsh', 'ctx')
- self_query_grad: float32 [1024, 1024], P('wsh')
- self_key_grad: float32 [1024, 1024], P('wsh')
- self_value_grad: float32 [1024, 1024], P('wsh')
- self_out_grad: float32 [1024, 1024], P('wsh')
- cross_query_grad: float32 [1024, 1024], P('wsh')
- cross_key_grad: float32 [1024, 1024], P('wsh')
- cross_value_grad: float32 [1024, 1024], P('wsh')
- cross_out_grad: float32 [1024, 1024], P('wsh')
- feed_in_grad: float32 [1024, 4096], P('wsh')
- feed_out_grad: float32 [4096, 1024], P('wsh')
- gain_grad: float32 [1024, 4], P('wsh')
- shift_grad: float32 [1024, 4], P('wsh')
Inputs may be any that keep to these rules, and one draw needn't show every extreme that they name: Each row of slot_order is a permutation of 0 to 1023. `seq_lengths`: each row sums to 1024. `enc_lengths`: each row sums to 512.
All inputs are finite; a program needn't handle non-finite values.
Results may differ from a plain program's by a relative error of at most 0.023.
Values may be sent and summed in bfloat16 or wider, within the bound.
No kernel may reach another device: no remote copies, remote signals or barrier semaphores. Data moves between devices by JAX's collectives and lax.ppermute only.
A program may use at most 256 MiB of HBM per device.

v0:
```python
import functools

import jax
import jax.numpy as jnp
from jax import lax
from jax.experimental import pallas as pl
from jax.experimental.pallas import tpu as pltpu
from jax.sharding import PartitionSpec as P

HEAD = 64
BF = jnp.bfloat16
F32 = jnp.float32


def dot(left, right):
    return jnp.dot(left, right, preferred_element_type=F32)


def dot_left(left, right):
    return lax.dot_general(left, right, (((0,), (0,)), ((), ())), preferred_element_type=F32)


def dot_right(left, right):
    return lax.dot_general(left, right, (((1,), (1,)), ((), ())), preferred_element_type=F32)


def swap(value, axis, bit):
    size = lax.axis_size(axis)
    return lax.ppermute(value, axis, [(i, i ^ bit) for i in range(size)])


def gather_ctx(own):
    size = lax.axis_size("ctx")
    blocks = {0: own}
    bit = size // 2
    while bit:
        for index in sorted(blocks):
            blocks[index | bit] = swap(blocks[index], "ctx", bit)
        bit //= 2
    return [blocks[index] for index in range(size)]


def scatter_ctx(blocks):
    blocks = dict(enumerate(blocks))
    size, bit = len(blocks), 1
    while bit < size:
        for index in sorted(blocks, reverse=True):
            if index & bit:
                arrived = swap(blocks.pop(index).astype(BF), "ctx", bit)
                blocks[index ^ bit] = blocks[index ^ bit] + arrived.astype(F32)
        bit *= 2
    return blocks[0]


def halves(blocks):
    middle = len(blocks) // 2
    return (jnp.concatenate(blocks[:middle], 0), jnp.concatenate(blocks[middle:], 0))


def scatter_halves(low, high, rows):
    count = low.shape[0] // rows
    cut = [low[i * rows : (i + 1) * rows] for i in range(count)]
    return scatter_ctx(cut + [high[i * rows : (i + 1) * rows] for i in range(count)])


def norm_parts(values):
    center = values - jnp.mean(values, axis=-1, keepdims=True)
    rate = lax.rsqrt(jnp.mean(center * center, axis=-1, keepdims=True) + 1e-05)
    return center * rate, rate


def norm_back(hat, rate, gain, grad):
    scaled = grad * gain
    inner = jnp.mean(scaled * hat, axis=-1, keepdims=True)
    result = rate * (scaled - jnp.mean(scaled, axis=-1, keepdims=True) - hat * inner)
    return result, jnp.sum(grad * hat, axis=0), jnp.sum(grad, axis=0)


def gelu_back(values, grad):
    unused, pullback = jax.vjp(lambda u: jax.nn.gelu(u, approximate=True), values)
    return pullback(grad)[0]


def split_heads(block, heads, head):
    wide = block.astype(F32)
    lane = lax.broadcasted_iota(jnp.int32, wide.shape, 1) // head
    parts = [jnp.where(lane == h, wide, 0.0).astype(BF) for h in range(heads)]
    return jnp.concatenate(parts, 0)


def spread(row, heads):
    return jnp.concatenate([row] * heads, 1)


def allowed_keys(first, chunk, low, high):
    index = first + lax.broadcasted_iota(jnp.int32, (chunk, low.shape[1]), 0)
    return (index >= low) & (index < high)


def forward_kernel(meta, q_ref, k_ref, v_ref, rows_ref, o_ref, lse_ref, top, total, mixed, *, heads, head, chunk, count, offset):
    block = pl.program_id(0) + offset
    queries = q_ref.shape[0]
    split = split_heads(q_ref[...].astype(F32) * 0.125, heads, head)
    low = spread(rows_ref[0, 0:1, :], heads)
    high = spread(rows_ref[0, 1:2, :], heads)
    top[...] = jnp.full_like(top, -1e30)
    total[...] = jnp.zeros_like(total)
    mixed[...] = jnp.zeros_like(mixed)

    def step(index, carry):
        start = pl.multiple_of((index ^ meta[0]) * chunk, chunk)
        keys = k_ref[pl.ds(start, chunk), :]
        values = jnp.transpose(v_ref[pl.ds(start, chunk), :])
        scores = dot_right(keys, split)
        scores = jnp.where(allowed_keys(index * chunk, chunk, low, high), scores, -1e30)
        before = top[...]
        now = jnp.maximum(before, jnp.max(scores, axis=0, keepdims=True))
        decay = jnp.exp(before - now)
        weight = jnp.exp(scores - now)
        top[...] = now
        total[...] = total[...] * decay + jnp.sum(weight, axis=0, keepdims=True)
        weight = weight.astype(BF)
        for h in range(heads):
            rows, cols = slice(h * head, (h + 1) * head), slice(h * queries, (h + 1) * queries)
            mixed[rows, :] = mixed[rows, :] * decay[:, cols] + dot(values[rows, :], weight[:, cols])
        return carry

    lax.fori_loop(meta[1 + block], meta[1 + count + block], step, 0)
    amount = total[...]
    for h in range(heads):
        rows, cols = slice(h * head, (h + 1) * head), slice(h * queries, (h + 1) * queries)
        mixed[rows, :] = mixed[rows, :] / amount[:, cols]
    o_ref[...] = jnp.transpose(mixed[...]).astype(BF)
    lse_ref[0] = top[...] + jnp.log(amount)


def backward_kernel(meta, q_ref, g_ref, o_ref, lse_ref, rows_ref, k_ref, v_ref, dq_ref, dk_ref, dv_ref, dq_sum, *, heads, head, chunk, count, offset):
    block = pl.program_id(0) + offset
    queries = q_ref.shape[0]

    @pl.when(pl.program_id(0) == 0)
    def _():
        dk_ref[...] = jnp.zeros_like(dk_ref)
        dv_ref[...] = jnp.zeros_like(dv_ref)

    split = split_heads(q_ref[...].astype(F32) * 0.125, heads, head)
    grads = split_heads(g_ref[...], heads, head)
    low = spread(rows_ref[0, 0:1, :], heads)
    high = spread(rows_ref[0, 1:2, :], heads)
    lse = lse_ref[0]
    product = jnp.transpose(g_ref[...].astype(F32) * o_ref[...].astype(F32))
    inner = jnp.concatenate(
        [jnp.sum(product[h * head : (h + 1) * head], axis=0, keepdims=True) for h in range(heads)], 1
    )
    dq_sum[...] = jnp.zeros_like(dq_sum)

    def step(index, carry):
        start = pl.multiple_of((index ^ meta[0]) * chunk, chunk)
        keys = k_ref[pl.ds(start, chunk), :]
        scores = dot_right(keys, split)
        scores = jnp.where(allowed_keys(index * chunk, chunk, low, high), scores, -1e30)
        weight = jnp.exp(scores - lse)
        slope = dot_right(v_ref[pl.ds(start, chunk), :], grads)
        slope = (weight * (slope - inner)).astype(BF)
        dv_ref[pl.ds(start, chunk), :] += dot(weight.astype(BF), grads)
        dk_ref[pl.ds(start, chunk), :] += dot(slope, split)
        turned = jnp.transpose(keys)
        for h in range(heads):
            rows, cols = slice(h * head, (h + 1) * head), slice(h * queries, (h + 1) * queries)
            dq_sum[rows, :] += dot(turned[rows, :], slope[:, cols])
        return carry

    lax.fori_loop(meta[1 + block], meta[1 + count + block], step, 0)
    dq_ref[...] = (jnp.transpose(dq_sum[...]) * 0.125).astype(BF)


class Attention:
    def __init__(self, low, high, tile, chunk, flip):
        self.tile, self.chunk = tile, chunk
        self.count = low.shape[0] // tile
        low, high = low.reshape(self.count, tile), high.reshape(self.count, tile)
        self.rows = jnp.stack([low, high], 1)
        first, last = jnp.min(low, 1) // chunk, (jnp.max(high, 1) - 1) // chunk + 1
        self.meta = jnp.concatenate([flip.reshape(1), first, last]).astype(jnp.int32)

    def specs(self, width, heads, offset, queries_at):
        tile = self.tile
        tall = pl.BlockSpec((tile, width), lambda i, m: (i + queries_at, 0))
        rows = pl.BlockSpec((1, 2, tile), lambda i, m: (i + offset, 0, 0))
        return tall, rows

    def forward(self, queries, keys, values, offset, steps, queries_at):
        width, heads = queries.shape[1], queries.shape[1] // HEAD
        tall, rows = self.specs(width, heads, offset, queries_at)
        whole = pl.BlockSpec(keys.shape, lambda i, m: (0, 0))
        lanes = heads * self.tile
        body = functools.partial(
            forward_kernel, heads=heads, head=HEAD, chunk=self.chunk, count=self.count, offset=offset
        )
        pairs = steps * self.tile * keys.shape[0] * heads
        return pl.pallas_call(
            body,
            grid_spec=pltpu.PrefetchScalarGridSpec(
                num_scalar_prefetch=1,
                grid=(steps,),
                in_specs=[tall, whole, whole, rows],
                out_specs=[
                    pl.BlockSpec((self.tile, width), lambda i, m: (i, 0)),
                    pl.BlockSpec((1, 1, lanes), lambda i, m: (i, 0, 0)),
                ],
                scratch_shapes=[
                    pltpu.VMEM((1, lanes), F32),
                    pltpu.VMEM((1, lanes), F32),
                    pltpu.VMEM((width, self.tile), F32),
                ],
            ),
            out_shape=[
                jax.ShapeDtypeStruct((steps * self.tile, width), BF),
                jax.ShapeDtypeStruct((steps, 1, lanes), F32),
            ],
            cost_estimate=pl.CostEstimate(flops=pairs * 256, transcendentals=pairs // 2, bytes_accessed=2 << 20),
            compiler_params=pltpu.CompilerParams(vmem_limit_bytes=24 << 20),
        )(self.meta, queries, keys, values, self.rows)

    def backward(self, queries, grads, mixed, lse, keys, values, offset, steps, queries_at):
        width, heads = queries.shape[1], queries.shape[1] // HEAD
        tall, rows = self.specs(width, heads, offset, queries_at)
        near = pl.BlockSpec((self.tile, width), lambda i, m: (i, 0))
        whole = pl.BlockSpec(keys.shape, lambda i, m: (0, 0))
        lanes = heads * self.tile
        body = functools.partial(
            backward_kernel, heads=heads, head=HEAD, chunk=self.chunk, count=self.count, offset=offset
        )
        pairs = steps * self.tile * keys.shape[0] * heads
        return pl.pallas_call(
            body,
            grid_spec=pltpu.PrefetchScalarGridSpec(
                num_scalar_prefetch=1,
                grid=(steps,),
                in_specs=[tall, near, near, pl.BlockSpec((1, 1, lanes), lambda i, m: (i, 0, 0)), rows, whole, whole],
                out_specs=[near, whole, whole],
                scratch_shapes=[pltpu.VMEM((width, self.tile), F32)],
            ),
            out_shape=[
                jax.ShapeDtypeStruct((steps * self.tile, width), BF),
                jax.ShapeDtypeStruct(keys.shape, F32),
                jax.ShapeDtypeStruct(keys.shape, F32),
            ],
            cost_estimate=pl.CostEstimate(flops=pairs * 640, transcendentals=pairs // 2, bytes_accessed=4 << 20),
            compiler_params=pltpu.CompilerParams(vmem_limit_bytes=32 << 20),
        )(self.meta, queries, grads, mixed, lse, self.rows, keys, values)


def gather_wsh(part):
    return lax.all_gather(part, "wsh", axis=0, tiled=True)


def scatter_wsh(whole):
    return lax.psum_scatter(whole.astype(BF), "wsh", scatter_dimension=0, tiled=True)


def piece_moves(groups, size):
    return [((g % size) * groups + g // size, g) for g in range(groups * size)]


def plain_body(
    inputs,
    enc_states,
    cotangent,
    slot_order,
    seq_lengths,
    enc_lengths,
    self_query,
    self_key,
    self_value,
    self_out,
    cross_query,
    cross_key,
    cross_value,
    cross_out,
    feed_in,
    feed_out,
    norm_gains,
    norm_shifts,
):
    size, groups = lax.axis_size("ctx"), lax.axis_size("wsh")
    mine, row = lax.axis_index("ctx"), lax.axis_index("wsh")
    slots = inputs.shape[1]
    total = slots * size
    enc_slots = enc_states.shape[1]
    width = inputs.shape[2]
    rows = self_query.shape[0]
    cols = width // size
    piece = rows // size
    ff_cols = feed_in.shape[1] // size
    ff_rows = feed_out.shape[0] // size

    def columns(matrix):
        return lax.dynamic_slice_in_dim(matrix, mine * cols, cols, 1)

    norms = jnp.concatenate([norm_gains, norm_shifts, jnp.zeros((rows, 120), BF)], 1)
    self_full = gather_wsh(jnp.concatenate([columns(self_query), columns(self_key), columns(self_value), norms], 1))
    q_full, k_full, v_full = (self_full[:, i * cols : (i + 1) * cols] for i in range(3))
    norm_rows = jnp.transpose(self_full[:, 3 * cols : 3 * cols + 8].astype(F32))
    gains, shifts = norm_rows[:4, None, :], norm_rows[4:, None, :]

    def out_piece(matrix):
        return lax.dynamic_slice_in_dim(matrix, mine * piece, piece, 0)

    pieces = jnp.concatenate([out_piece(self_out), out_piece(cross_out)], 0)
    pieces = lax.ppermute(pieces, ("ctx", "wsh"), piece_moves(groups, size))
    pieces = gather_wsh(pieces).reshape(groups, 2, piece, width)
    out_full, cross_o_full = pieces[:, 0].reshape(cols, width), pieces[:, 1].reshape(cols, width)
    cross_full = gather_wsh(jnp.concatenate([columns(cross_query), columns(cross_key), columns(cross_value)], 1))
    cq_full, ck_full, cv_full = (cross_full[:, i * cols : (i + 1) * cols] for i in range(3))
    first_part = lax.dynamic_slice_in_dim(feed_in.reshape(rows, groups, size, ff_rows), mine, 1, 2)
    second_part = lax.dynamic_slice_in_dim(feed_out, mine * ff_rows, ff_rows, 0)
    feed = jnp.concatenate([first_part.reshape(rows, ff_cols), second_part.reshape(rows, ff_cols)], 0)
    feed = gather_wsh(feed).reshape(groups, 2, rows, ff_cols)
    first_full = feed[:, 0].reshape(groups * rows, ff_cols)
    second_full = feed[:, 1].reshape(groups * ff_rows, width)

    relative = jnp.arange(size, dtype=jnp.int32) ^ mine
    order = jnp.take(slot_order[0].reshape(size, slots), relative, axis=0).reshape(total)
    place = (relative[:, None] * slots + jnp.arange(slots, dtype=jnp.int32)).reshape(total)
    lower = jnp.arange(seq_lengths.shape[1])
    lower = lower[None, :] <= lower[:, None]
    ends = jnp.sum(jnp.where(lower, seq_lengths[0][None, :], 0), 1)
    enc_ends = jnp.sum(jnp.where(lower, enc_lengths[0][None, :], 0), 1)
    passed = ends[None, :] <= place[:, None]
    starts = jnp.max(jnp.where(passed, ends[None, :], 0), 1)
    enc_from = jnp.max(jnp.where(passed, enc_ends[None, :], 0), 1)
    enc_to = jnp.min(jnp.where(passed, enc_slots * size, enc_ends[None, :]), 1)
    self_att = Attention(starts, place + 1, 256, 256, mine * (slots // 256))
    cross_att = Attention(enc_from, enc_to, 256, 128, mine * (enc_slots // 128))
    tiles = total // 256
    half = tiles // 2

    to_place = (order[None, :] == place[:, None]).astype(BF)
    to_slot = (order[:slots, None] == place[None, :]).astype(BF)
    tokens_all = jnp.concatenate(gather_ctx(inputs[0]), 0)
    tokens_all = dot(to_place, tokens_all)
    tokens = tokens_all[:slots]
    encoder = jnp.concatenate(gather_ctx(enc_states[0]), 0)
    outside = jnp.concatenate(gather_ctx(cotangent[0]), 0)
    outside = dot(to_place[:slots], outside)

    hat_all, unused = norm_parts(tokens_all)
    normed_one = (hat_all * gains[0] + shifts[0]).astype(BF)
    queries = dot(normed_one, q_full).astype(BF)
    keys = dot(normed_one, k_full).astype(BF)
    values = dot(normed_one, v_full).astype(BF)
    mixed_high, lse_high = self_att.forward(queries, keys, values, half, half, half)
    mixed_low, lse_low = self_att.forward(queries, keys, values, 0, half, 0)
    after_self = tokens + scatter_halves(dot(mixed_low, out_full), dot(mixed_high, out_full), slots)

    hat_two, rate_two = norm_parts(after_self)
    normed_two = halves(gather_ctx((hat_two * gains[1] + shifts[1]).astype(BF)))
    enc_keys = dot(encoder, ck_full).astype(BF)
    enc_values = dot(encoder, cv_full).astype(BF)
    queries_two = [dot(part, cq_full).astype(BF) for part in normed_two]
    mixed_two = [
        cross_att.forward(queries_two[side], enc_keys, enc_values, side * half, half, 0) for side in range(2)
    ]
    after_cross = after_self + scatter_halves(*(dot(part[0], cross_o_full) for part in mixed_two), slots)

    hat_three, rate_three = norm_parts(after_cross)
    normed_three = halves(gather_ctx((hat_three * gains[2] + shifts[2]).astype(BF)))
    pre_act = [dot(part, first_full) for part in normed_three]
    hidden = [jax.nn.gelu(part, approximate=True).astype(BF) for part in pre_act]
    after_ffn = after_cross + scatter_halves(*(dot(part, second_full) for part in hidden), slots)
    hat_four, rate_four = norm_parts(after_ffn)
    result = hat_four * gains[3] + shifts[3]
    result = jnp.concatenate(gather_ctx(result.astype(BF)), 0)
    result = dot(to_slot, result)

    grad_ffn, gain_three, shift_three = norm_back(hat_four, rate_four, gains[3], outside)
    grad_in = halves(gather_ctx(grad_ffn.astype(BF)))
    grad_pre = [
        gelu_back(part, dot_right(grad, second_full)).astype(BF)
        for part, grad in zip(pre_act, grad_in)
    ]
    arrived = scatter_halves(*(dot_right(grad, first_full) for grad in grad_pre), slots)
    norm_part, gain_two, shift_two = norm_back(hat_three, rate_three, gains[2], arrived)
    grad_cross = grad_ffn + norm_part
    grad_first = sum(dot_left(n, g) for n, g in zip(normed_three, grad_pre))
    grad_second = sum(dot_left(n, g) for n, g in zip(hidden, grad_in))
    feed_grads = jnp.concatenate(
        [
            grad_first.astype(BF).reshape(groups, rows, ff_cols),
            grad_second.astype(BF).reshape(groups, rows, ff_cols),
        ],
        1,
    )
    feed_grads = scatter_wsh(feed_grads.reshape(groups * 2 * rows, ff_cols))
    feed_grads = lax.all_gather(feed_grads, "ctx", axis=0).reshape(size, 2, rows, ff_cols)
    feed_in_grad = jnp.transpose(feed_grads[:, 0].reshape(size, rows, groups, ff_rows), (1, 2, 0, 3))
    feed_in_grad = feed_in_grad.reshape(rows, groups * size * ff_rows).astype(F32)
    feed_out_grad = feed_grads[:, 1].reshape(size * ff_rows, width).astype(F32)

    def share(query_grad, key_grad, value_grad, out_grad):
        packed = [
            query_grad.astype(BF),
            key_grad.astype(BF),
            value_grad.astype(BF),
            out_grad.astype(BF).reshape(groups * rows, cols),
        ]
        packed = scatter_wsh(jnp.concatenate(packed, 1))
        moved = packed[:, 3 * cols :].reshape(piece, width)
        moved = lax.ppermute(moved, ("ctx", "wsh"), [(b, a) for a, b in piece_moves(groups, size)])
        packed = jnp.concatenate([packed[:, : 3 * cols], moved.reshape(rows, cols)], 1)
        packed = lax.all_gather(packed, "ctx", axis=0)
        three = [
            jnp.transpose(packed[:, :, i * cols : (i + 1) * cols], (1, 0, 2)).reshape(rows, width).astype(F32)
            for i in range(3)
        ]
        return three + [packed[:, :, 3 * cols :].reshape(size, piece, width).reshape(rows, width).astype(F32)]

    grad_in = halves(gather_ctx(grad_cross.astype(BF)))
    grad_mixed = [dot_right(grad, cross_o_full).astype(BF) for grad in grad_in]
    back = [
        cross_att.backward(
            queries_two[side], grad_mixed[side], *mixed_two[side], enc_keys, enc_values, side * half, half, 0
        )
        for side in range(2)
    ]
    arrived = scatter_halves(*(dot_right(part[0], cq_full) for part in back), slots)
    norm_part, gain_one, shift_one = norm_back(hat_two, rate_two, gains[1], arrived)
    grad_self = grad_cross + norm_part
    grad_ek = (back[0][1] + back[1][1]).astype(BF)
    grad_ev = (back[0][2] + back[1][2]).astype(BF)
    enc_part = dot_right(grad_ek, ck_full) + dot_right(grad_ev, cv_full)
    enc_grad = scatter_ctx([enc_part[i * enc_slots : (i + 1) * enc_slots] for i in range(size)])
    cross_q_grad, cross_k_grad, cross_v_grad, cross_o_grad = share(
        sum(dot_left(n, part[0]) for n, part in zip(normed_two, back)),
        dot_left(encoder, grad_ek),
        dot_left(encoder, grad_ev),
        sum(dot_left(part[0], g) for part, g in zip(mixed_two, grad_in)),
    )

    grad_in = halves(gather_ctx(grad_self.astype(BF)))
    grad_mixed = [dot_right(grad, out_full).astype(BF) for grad in grad_in]
    back_low = self_att.backward(queries, grad_mixed[0], mixed_low, lse_low, keys, values, 0, half, 0)
    back_high = self_att.backward(queries, grad_mixed[1], mixed_high, lse_high, keys, values, half, half, half)
    grad_q = jnp.concatenate([back_low[0], back_high[0]], 0)
    grad_k = (back_low[1] + back_high[1]).astype(BF)
    grad_v = (back_low[2] + back_high[2]).astype(BF)
    arrived = dot_right(grad_q, q_full) + dot_right(grad_k, k_full) + dot_right(grad_v, v_full)
    arrived = scatter_ctx([arrived[i * slots : (i + 1) * slots] for i in range(size)])
    hat_one, rate_one = norm_parts(tokens)
    norm_part, gain_zero, shift_zero = norm_back(hat_one, rate_one, gains[0], arrived)
    input_grad = grad_self + norm_part
    input_grad = jnp.concatenate(gather_ctx(input_grad.astype(BF)), 0)
    input_grad = dot(to_slot, input_grad)
    query_grad, key_grad, value_grad, out_grad = share(
        dot_left(normed_one, grad_q),
        dot_left(normed_one, grad_k),
        dot_left(normed_one, grad_v),
        dot_left(mixed_low, grad_in[0]) + dot_left(mixed_high, grad_in[1]),
    )

    terms = jnp.stack(
        [gain_zero, gain_one, gain_two, gain_three, shift_zero, shift_one, shift_two, shift_three], 0
    )
    for axis, amount in (("ctx", size), ("wsh", groups)):
        bit = 1
        while bit < amount:
            terms = terms + swap(terms, axis, bit)
            bit *= 2
    terms = jnp.transpose(lax.dynamic_slice_in_dim(terms, row * rows, rows, 1))
    return (
        result[None],
        input_grad[None],
        enc_grad[None],
        query_grad,
        key_grad,
        value_grad,
        out_grad,
        cross_q_grad,
        cross_k_grad,
        cross_v_grad,
        cross_o_grad,
        feed_in_grad,
        feed_out_grad,
        terms[:, :4],
        terms[:, 4:],
    )


SMALL = pl.CostEstimate(flops=1 << 20, transcendentals=0, bytes_accessed=1 << 16)


def call(kernel, outs, scalars, *operands, scratch=(), aliases=None, vmem=12, space=pltpu.VMEM, out_space=pltpu.VMEM):
    specs = [pl.BlockSpec(memory_space=pltpu.SMEM)] * len(scalars)
    specs += [pl.BlockSpec(memory_space=space)] * len(operands)
    return pl.pallas_call(
        kernel,
        in_specs=specs,
        out_specs=[pl.BlockSpec(memory_space=out_space)] * len(outs),
        out_shape=[jax.ShapeDtypeStruct(shape, kind) for shape, kind in outs],
        scratch_shapes=list(scratch),
        input_output_aliases=aliases or {},
        cost_estimate=SMALL,
        compiler_params=pltpu.CompilerParams(vmem_limit_bytes=vmem << 20),
    )(*scalars, *operands)


def call_packing(kernel, outs, *operands):
    scratch = [pltpu.VMEM(operand.shape, operand.dtype) for operand in operands]
    count = len(operands)

    def fetching(*refs):
        sources, outs, held, done = refs[:count], refs[count : -count - 1], refs[-count - 1 : -1], refs[-1]
        copies = [pltpu.make_async_copy(sources[i], held[i], done.at[i]) for i in range(count)]
        for copy in copies:
            copy.start()
        for copy in copies:
            copy.wait()
        kernel(*held, *outs)

    operands = [pltpu.with_memory_space_constraint(operand, pltpu.HBM) for operand in operands]
    scratch.append(pltpu.SemaphoreType.DMA((count,)))
    return call(fetching, outs, (), *operands, scratch=scratch, space=pltpu.HBM)


def call_streaming(kernel, out, steps, *operands, vmem=20):
    shape, kind = out
    part = shape[0] // steps

    def streaming(*refs):
        *sources, out_ref, held, done = refs

        def copy(index):
            at = pl.ds(index * part, part)
            return pltpu.make_async_copy(held.at[at], out_ref.at[at], done.at[index])

        kernel(*sources, held, lambda index: copy(index).start())
        for index in range(steps):
            copy(index).wait()

    scratch = [pltpu.VMEM(shape, kind), pltpu.SemaphoreType.DMA((steps,))]
    return call(streaming, [out], (), *operands, scratch=scratch, vmem=vmem, out_space=pltpu.HBM)[0]


def one_hot(hit):
    return jnp.where(hit, 1.0, 0.0).astype(BF)


def ctx_part(size):
    return pl.ds(pl.multiple_of(lax.axis_index("ctx") * size, size), size)


def my_heads(matrix, size):
    cols = matrix.shape[1] // size
    heads = cols // HEAD
    span = HEAD * size
    source = lax.broadcasted_iota(jnp.int32, (span, cols), 0) - lax.axis_index("ctx") * HEAD
    target = lax.broadcasted_iota(jnp.int32, (span, cols), 1)
    total = None
    for head in range(heads):
        part = dot(matrix[:, head * span : (head + 1) * span], one_hot((source >= 0) & (source < HEAD) & (source == target - head * HEAD)))
        total = part if total is None else total + part
    return total.astype(BF)


def give_pieces_kernel(one, two, out_ref):
    piece = out_ref.shape[0] // 2
    start = pl.multiple_of((lax.axis_index("ctx") % 2) * 2 * piece + piece, piece)
    out_ref[:piece, :] = one[pl.ds(start, piece), :]
    out_ref[piece:, :] = two[pl.ds(start, piece), :]


def my_piece(matrix, given, which):
    piece = given.shape[0] // 2
    mine = lax.axis_index("ctx")
    start = pl.multiple_of((mine % 2) * 2 * piece, piece)
    own = matrix[pl.ds(start, piece), :].astype(F32)
    other = given[which * piece : (which + 1) * piece, :].astype(F32)
    same = lax.axis_index("wsh") % 2 == mine // 2
    return jnp.where(same, own, other).astype(BF)


def pack_kernel(wq, wk, wv, wo, given, *refs, size, which):
    *norm_refs, out_ref = refs
    rows, cols = wq.shape[0], out_ref.shape[1]
    for part, full in enumerate((wq, wk, wv)):
        out_ref[part * rows : (part + 1) * rows, :] = my_heads(full, size)
    taken = my_piece(wo, given, which)
    piece = taken.shape[0]
    for chunk in range(taken.shape[1] // cols):
        at = 3 * rows + chunk * piece
        out_ref[at : at + piece, :] = taken[:, chunk * cols : (chunk + 1) * cols]
    if norm_refs:
        gains, shifts = norm_refs
        norms = jnp.concatenate([gains[...], shifts[...]], 0).astype(F32)
        norms = jnp.concatenate([norms, jnp.zeros((8, rows), F32)], 0)
        norms = jnp.concatenate([norms, jnp.zeros((16, cols - rows), F32)], 1)
        out_ref[out_ref.shape[0] - 16 :, :] = norms.astype(BF)


def pack_feed_kernel(first, second, out_ref, groups, size):
    rows, width = first.shape[0], first.shape[1] // groups
    cols = width // size
    mine = lax.axis_index("ctx")
    for group in range(groups):
        at = pl.ds(pl.multiple_of(group * width + mine * cols, cols), cols)
        out_ref[:rows, group * cols : (group + 1) * cols] = first[:, at]
    out_ref[rows:, :] = second[ctx_part(cols), :]


def sort_kernel(order_ref, *refs, size):
    sources, (hat_ref, own_ref) = refs[:size], refs[size:]
    slots = sources[0].shape[0]
    mine = lax.axis_index("ctx")

    def block(index, carry):
        base = (mine ^ index) * slots
        total = jnp.zeros(own_ref.shape, F32)
        for source in range(size):
            order = order_ref[:, source * slots : (source + 1) * slots]
            place = base + lax.broadcasted_iota(jnp.int32, (slots, slots), 0)
            total += dot(one_hot(order == place), sources[source][...])

        @pl.when(index == 0)
        def _():
            own_ref[...] = total

        hat, unused = norm_parts(total)
        hat_ref[pl.ds(pl.multiple_of(index * slots, slots), slots), :] = hat
        return carry

    lax.fori_loop(0, size, block, 0)


def pick_kernel(order_ref, *refs, size):
    sources, out_ref = refs[:size], refs[size]
    slots = sources[0].shape[0]
    base = lax.axis_index("ctx") * slots
    total = jnp.zeros(out_ref.shape, F32)
    for source in range(size):
        order = order_ref[:, source * slots : (source + 1) * slots]
        place = base + lax.broadcasted_iota(jnp.int32, (slots, slots), 0)
        total += dot(one_hot(order == place), sources[source][...])
    out_ref[...] = total


def unsort_kernel(order_ref, *refs, size):
    sources, out_ref = refs[:size], refs[size]
    slots = sources[0].shape[0]
    mine = lax.axis_index("ctx")
    total = jnp.zeros(out_ref.shape, F32)
    for source in range(size):
        place = (mine ^ source) * slots + lax.broadcasted_iota(jnp.int32, (slots, slots), 1)
        total += dot(one_hot(order_ref[...] == place), sources[source][...])
    out_ref[...] = total


def wsh_rows(index, rows):
    target = (lax.axis_index("wsh") ^ index) * rows
    return pl.ds(pl.multiple_of(target, rows), rows)


def piece_rows(index, piece):
    target = lax.axis_index("wsh") ^ index ^ (lax.axis_index("ctx") // 2)
    return pl.ds(pl.multiple_of(target * piece, piece), piece)


def place_attention(blocks, wq, wk, wv, wo, rows, piece):
    for index, block in enumerate(blocks):
        for part, full in enumerate((wq, wk, wv)):
            full[wsh_rows(index, rows), :] = block[part * rows : (part + 1) * rows, :]
        cols = block.shape[1]
        for chunk in range(wo.shape[1] // cols):
            at = 3 * rows + chunk * piece
            wo[piece_rows(index, piece), chunk * cols : (chunk + 1) * cols] = block[at : at + piece, :]


def project_kernel(hat_ref, *refs, groups, rows, piece):
    blocks = refs[:groups]
    wq, wk, wv, wo, norms, normed_ref, q_ref, k_ref, v_ref = refs[groups:]
    place_attention(blocks, wq, wk, wv, wo, rows, piece)
    for index, block in enumerate(blocks):
        last = block.shape[0] - 16
        norms[:, wsh_rows(index, rows)] = block[last:, :rows].astype(F32)[:8]
    tile = 256

    def step(index, carry):
        at = pl.ds(pl.multiple_of(index * tile, tile), tile)
        normed = (hat_ref[at, :] * norms[0:1, :] + norms[4:5, :]).astype(BF)
        normed_ref[at, :] = normed
        for full, out in ((wq, q_ref), (wk, k_ref), (wv, v_ref)):
            out[at, :] = dot(normed, full[...]).astype(BF)
        return carry

    lax.fori_loop(0, hat_ref.shape[0] // tile, step, 0)


def cross_prepare_kernel(blocks, *refs, size, rows, piece):
    encoder = refs[:size]
    wq, wk, wv, wo, key_ref, value_ref = refs[size:]
    groups, cols = blocks.shape[0], blocks.shape[2]
    for index in range(groups):
        for part, full in enumerate((wq, wk, wv)):
            full[index * rows : (index + 1) * rows, :] = blocks[index, part * rows : (part + 1) * rows, :]
        target = (index ^ (lax.axis_index("ctx") // 2)) * piece
        there = pl.ds(pl.multiple_of(target, piece), piece)
        for chunk in range(wo.shape[1] // cols):
            at = 3 * rows + chunk * piece
            wo[there, chunk * cols : (chunk + 1) * cols] = blocks[index, at : at + piece, :]
    slots = encoder[0].shape[0]
    for index, part in enumerate(encoder):
        at = slice(index * slots, (index + 1) * slots)
        key_ref[at, :] = dot(part[...], wk[...]).astype(BF)
        value_ref[at, :] = dot(part[...], wv[...]).astype(BF)


def attend(split, low, high, first, last, flip, k_ref, v_ref, top, total, mixed, heads, chunk):
    tile = mixed.shape[1]
    top[...] = jnp.full_like(top, -1e30)
    total[...] = jnp.zeros_like(total)
    mixed[...] = jnp.zeros_like(mixed)

    def step(index, carry):
        start = pl.multiple_of((index ^ flip) * chunk, chunk)
        keys = k_ref[pl.ds(start, chunk), :]
        values = jnp.transpose(v_ref[pl.ds(start, chunk), :])
        scores = dot_right(keys, split)
        scores = jnp.where(allowed_keys(index * chunk, chunk, low, high), scores, -1e30)
        before = top[...]
        now = jnp.maximum(before, jnp.max(scores, axis=0, keepdims=True))
        decay = jnp.exp(before - now)
        weight = jnp.exp(scores - now)
        top[...] = now
        total[...] = total[...] * decay + jnp.sum(weight, axis=0, keepdims=True)
        weight = weight.astype(BF)
        for h in range(heads):
            rows, cols = slice(h * HEAD, (h + 1) * HEAD), slice(h * tile, (h + 1) * tile)
            mixed[rows, :] = mixed[rows, :] * decay[:, cols] + dot(values[rows, :], weight[:, cols])
        return carry

    lax.fori_loop(first, last, step, 0)
    amount = total[...]
    for h in range(heads):
        rows, cols = slice(h * HEAD, (h + 1) * HEAD), slice(h * tile, (h + 1) * tile)
        mixed[rows, :] = mixed[rows, :] / amount[:, cols]
    return top[...] + jnp.log(amount)


def attend_forward_kernel(meta, *refs, own_queries, parts, offset, count, chunk):
    if own_queries:
        sources, wq = refs[:parts], refs[parts]
        k_ref, v_ref, rows_ref, wo, q_ref, mixed_ref, lse_ref = refs[parts + 1 : parts + 8]
        rest = refs[parts + 8 :]
        for index, source in enumerate(sources):
            slots = source.shape[0]
            q_ref[index * slots : (index + 1) * slots, :] = dot(source[...], wq[...]).astype(BF)
        shift = 0
    else:
        q_ref, k_ref, v_ref, rows_ref, wo, mixed_ref, lse_ref = refs[:7]
        rest = refs[7:]
        shift = offset
    outs, (top, total, mixed) = rest[:parts], rest[parts:]
    tile = mixed.shape[1]
    heads = q_ref.shape[1] // HEAD

    def block(index, carry):
        at = pl.ds(pl.multiple_of((index + shift) * tile, tile), tile)
        split = split_heads(q_ref[at, :].astype(F32) * 0.125, heads, HEAD)
        low = spread(rows_ref[index + offset, 0:1, :], heads)
        high = spread(rows_ref[index + offset, 1:2, :], heads)
        first, last = meta[1 + index + offset], meta[1 + count + index + offset]
        lse_ref[index] = attend(split, low, high, first, last, meta[0], k_ref, v_ref, top, total, mixed, heads, chunk)
        here = pl.ds(pl.multiple_of(index * tile, tile), tile)
        mixed_ref[here, :] = jnp.transpose(mixed[...]).astype(BF)
        return carry

    lax.fori_loop(0, mixed_ref.shape[0] // tile, block, 0)
    for index, out in enumerate(outs):
        slots = out.shape[0]
        out[...] = dot(mixed_ref[index * slots : (index + 1) * slots, :], wo[...]).astype(BF)


def attend_backward_kernel(meta, *refs, own_queries, parts, offset, count, chunk, fresh):
    sources = refs[:parts]
    q_ref, mixed_ref, lse_ref, rows_ref, k_ref, v_ref, wo = refs[parts : parts + 7]
    rest = refs[parts + 7 :]
    if own_queries:
        wq, rest = rest[0], rest[1:]
    if not fresh:
        rest = rest[3:]
    dq_ref, dk_ref, dv_ref, dwo_ref = rest[:4]
    outs = rest[4 : 4 + parts] if own_queries else ()
    grad_ref, dq_sum = rest[-2:]
    tile = dq_sum.shape[1]
    heads = q_ref.shape[1] // HEAD
    shift = 0 if own_queries else offset
    if fresh:
        dk_ref[...] = jnp.zeros_like(dk_ref)
        dv_ref[...] = jnp.zeros_like(dv_ref)
    change = None
    for index, source in enumerate(sources):
        slots = source.shape[0]
        at = slice(index * slots, (index + 1) * slots)
        grad_ref[at, :] = dot_right(source[...], wo[...]).astype(BF)
        part = dot_left(mixed_ref[at, :], source[...])
        change = part if change is None else change + part
    dwo_ref[...] = change if fresh else dwo_ref[...] + change

    def block(index, carry):
        at = pl.ds(pl.multiple_of((index + shift) * tile, tile), tile)
        here = pl.ds(pl.multiple_of(index * tile, tile), tile)
        split = split_heads(q_ref[at, :].astype(F32) * 0.125, heads, HEAD)
        grads = split_heads(grad_ref[here, :], heads, HEAD)
        low = spread(rows_ref[index + offset, 0:1, :], heads)
        high = spread(rows_ref[index + offset, 1:2, :], heads)
        lse = lse_ref[index]
        product = jnp.transpose(grad_ref[here, :].astype(F32) * mixed_ref[here, :].astype(F32))
        inner = jnp.concatenate(
            [jnp.sum(product[h * HEAD : (h + 1) * HEAD], axis=0, keepdims=True) for h in range(heads)], 1
        )
        dq_sum[...] = jnp.zeros_like(dq_sum)

        def step(number, carry):
            start = pl.multiple_of((number ^ meta[0]) * chunk, chunk)
            keys = k_ref[pl.ds(start, chunk), :]
            scores = dot_right(keys, split)
            scores = jnp.where(allowed_keys(number * chunk, chunk, low, high), scores, -1e30)
            weight = jnp.exp(scores - lse)
            slope = dot_right(v_ref[pl.ds(start, chunk), :], grads)
            slope = (weight * (slope - inner)).astype(BF)
            dv_ref[pl.ds(start, chunk), :] += dot(weight.astype(BF), grads)
            dk_ref[pl.ds(start, chunk), :] += dot(slope, split)
            turned = jnp.transpose(keys)
            for h in range(heads):
                rows, cols = slice(h * HEAD, (h + 1) * HEAD), slice(h * tile, (h + 1) * tile)
                dq_sum[rows, :] += dot(turned[rows, :], slope[:, cols])
            return carry

        lax.fori_loop(meta[1 + index + offset], meta[1 + count + index + offset], step, 0)
        dq_ref[here, :] = (jnp.transpose(dq_sum[...]) * 0.125).astype(BF)
        return carry

    lax.fori_loop(0, dq_ref.shape[0] // tile, block, 0)
    for index, out in enumerate(outs):
        slots = out.shape[0]
        out[...] = dot_right(dq_ref[index * slots : (index + 1) * slots, :], wq[...]).astype(BF)


def total_of(base, parts):
    value = base[...]
    for part in parts:
        value = value + part[...].astype(F32)
    return value


def norm_kernel(norms, base, *refs, which):
    parts, (sum_ref, normed_ref) = refs[:-2], refs[-2:]
    value = total_of(base, parts)
    sum_ref[...] = value
    hat, unused = norm_parts(value)
    normed_ref[...] = (hat * norms[which : which + 1, :] + norms[4 + which : 5 + which, :]).astype(BF)


def norm_back_kernel(norms, value_ref, grad_ref, *refs, which):
    parts, (out_ref, sent_ref, terms_ref) = refs[:-3], refs[-3:]
    hat, rate = norm_parts(value_ref[...])
    grad = parts[0][...].astype(F32)
    for part in parts[1:]:
        grad = grad + part[...].astype(F32)
    change, gain, shift = norm_back(hat, rate, norms[which : which + 1, :], grad)
    result = grad_ref[...] + change
    out_ref[...] = result
    sent_ref[...] = result.astype(BF)
    terms_ref[0:1, :] = gain[None]
    terms_ref[1:2, :] = shift[None]


def norm_turn_kernel(norms, base, outside, *refs):
    parts, (result_ref, out_ref, sent_ref, terms_ref) = refs[:-4], refs[-4:]
    hat, rate = norm_parts(total_of(base, parts))
    result_ref[...] = (hat * norms[3:4, :] + norms[7:8, :]).astype(BF)
    change, gain, shift = norm_back(hat, rate, norms[3:4, :], outside[...])
    out_ref[...] = change
    sent_ref[...] = change.astype(BF)
    terms_ref[0:1, :] = gain[None]
    terms_ref[1:2, :] = shift[None]


def feed_halves(feed):
    groups, rows, cols = feed.shape
    rows = rows // 2
    return feed[:, :rows, :].reshape(groups * rows, cols), feed[:, rows:, :].reshape(groups * rows, cols)


def feed_forward_kernel(*refs, parts):
    sources, (feed, hidden_ref, slope_ref), outs = refs[:parts], refs[parts : parts + 3], refs[parts + 3 :]
    rate = 0.7978845608028654
    first, second = feed_halves(feed)
    for index, (source, out) in enumerate(zip(sources, outs)):
        slots = source.shape[0]
        at = slice(index * slots, (index + 1) * slots)
        pre = dot(source[...], first)
        square = pre * pre
        bend = jnp.tanh(rate * pre * (1.0 + 0.044715 * square))
        half = 0.5 * (1.0 + bend)
        slope_ref[at, :] = (half + 0.5 * pre * (1.0 - bend * bend) * rate * (1.0 + 0.134145 * square)).astype(BF)
        hidden_ref[at, :] = (pre * half).astype(BF)
        out[...] = dot(hidden_ref[at, :], second).astype(BF)


def feed_backward_kernel(*refs, parts):
    sources, (feed, slope_ref, change_ref), outs = refs[:parts], refs[parts : parts + 3], refs[parts + 3 :]
    first, second = feed_halves(feed)
    for index, (source, out) in enumerate(zip(sources, outs)):
        slots = source.shape[0]
        at = slice(index * slots, (index + 1) * slots)
        change = dot_right(source[...], second) * slope_ref[at, :].astype(F32)
        change_ref[at, :] = change.astype(BF)
        out[...] = dot_right(change_ref[at, :], first).astype(BF)


def feed_grad_kernel(*refs, size, rows):
    normed, (change_low, change_high, hidden_low, hidden_high) = refs[:size], refs[size : size + 4]
    grads, (out_ref, send) = refs[size + 4 : 2 * size + 4], refs[-2:]
    middle, slots = size // 2, normed[0].shape[0]
    wide = 2 * rows

    def step(index, carry):
        lanes = pl.ds(pl.multiple_of(index * wide, wide), wide)
        first, second = None, None
        for block in range(size):
            side, at = block // middle, (block % middle) * slots
            change = (change_low, change_high)[side][at : at + slots, :]
            hidden = (hidden_low, hidden_high)[side][at : at + slots, lanes]
            one = dot_left(normed[block][:, lanes], change)
            two = dot_left(hidden, grads[block][...])
            first, second = (one, two) if first is None else (first + one, second + two)
        for part in range(2):
            at = slice(part * rows, (part + 1) * rows)
            out_ref[2 * index + part, 0:rows, :] = first[at, :].astype(BF)
            out_ref[2 * index + part, rows : 2 * rows, :] = second[at, :].astype(BF)
        send(index)
        return carry

    lax.fori_loop(0, out_ref.shape[0] // 2, step, 0)


def weight_grad_kernel(*refs, terms, odd, rows, piece, count):
    send = None
    if odd is None:
        *refs, send = refs
    operands, extra, out_ref = refs[:-2], refs[-2], refs[-1]
    height = out_ref.shape[0] // count
    cols = out_ref.shape[1]
    mine = lax.axis_index("wsh")

    def step(index, carry):
        relative = index ^ mine if odd is None else 2 * index + odd
        target = mine ^ relative
        lanes = pl.ds(pl.multiple_of(target * rows, rows), rows)
        for part in range(3):
            value = None
            for which, left, left_at, right, right_at, length in terms:
                if which == part:
                    one = dot_left(
                        operands[left][left_at : left_at + length, lanes],
                        operands[right][right_at : right_at + length, :].astype(BF),
                    )
                    value = one if value is None else value + one
            at = pl.ds(pl.multiple_of(index * height + part * rows, rows), rows)
            out_ref[at, :] = value.astype(out_ref.dtype)
        taken = piece_rows(relative, piece)
        for chunk in range(extra.shape[1] // cols):
            at = pl.ds(pl.multiple_of(index * height + 3 * rows + chunk * piece, piece), piece)
            out_ref[at, :] = extra[taken, chunk * cols : (chunk + 1) * cols].astype(out_ref.dtype)
        if send is not None:
            send(index)
        return carry

    lax.fori_loop(0, count, step, 0)


def sum_kernel(even, odd, terms, other_terms, *outs, rows, height):
    total = terms[...] + other_terms[...]
    for index, out in enumerate(outs):
        at = slice(index * height, (index + 1) * height)
        out[:height, :] = (even[at, :] + odd[at, :].astype(F32)).astype(out.dtype)
        lanes = (lax.axis_index("wsh") ^ (2 * index)) * rows
        taken = jnp.zeros((8, rows), F32)
        for block in range(total.shape[1] // rows):
            taken = jnp.where(lanes == block * rows, total[:, block * rows : (block + 1) * rows], taken)
        taken = jnp.concatenate([taken, jnp.zeros((8, rows), F32)], 0)
        taken = jnp.concatenate([taken, jnp.zeros((16, out.shape[1] - rows), F32)], 1)
        out[height:, :] = taken.astype(out.dtype)


def back_project_kernel(dq_ref, dk_ref, dv_ref, wq, wk, wv, *outs, first):
    for index, out in enumerate(outs):
        slots = out.shape[0]
        at = slice(index * slots, (index + 1) * slots)
        there = slice(first + index * slots, first + (index + 1) * slots)
        value = dot_right(dq_ref[at, :], wq[...])
        value += dot_right(dk_ref[there, :].astype(BF), wk[...])
        value += dot_right(dv_ref[there, :].astype(BF), wv[...])
        out[...] = value.astype(BF)


def encoder_grad_kernel(dk_ref, dv_ref, wk, wv, *outs):
    for index, out in enumerate(outs):
        slots = out.shape[0]
        at = slice(index * slots, (index + 1) * slots)
        value = dot_right(dk_ref[at, :].astype(BF), wk[...]) + dot_right(dv_ref[at, :].astype(BF), wv[...])
        out[...] = value.astype(BF)


def place_square_kernel(*refs, count, rows, piece):
    mine = lax.axis_index("ctx")
    threes, (near, other), outs = refs[:count], refs[count : count + 2], refs[count + 2 :]
    cols = threes[0].shape[1]
    if len(outs) > 4:
        last = [three[3 * rows :, :rows].astype(F32) for three in threes]
        outs[4][...] = sum(last)
    span = HEAD * count
    blocks = [three[...].astype(F32) for three in threes]
    for group in range(count):
        wanted = mine ^ group
        chosen = blocks[0]
        for index in range(1, count):
            chosen = jnp.where(wanted == index, blocks[index], chosen)
        for part in range(3):
            for head in range(cols // HEAD):
                at = head * span + group * HEAD
                outs[part][:, at : at + HEAD] = chosen[
                    part * rows : (part + 1) * rows, head * HEAD : (head + 1) * HEAD
                ]
    core = mine % 2
    for source, place in ((near, core), (other, 1 - core)):
        for half in range(2):
            row = pl.ds(pl.multiple_of((2 * place + half) * piece, piece), piece)
            for chunk in range(outs[3].shape[1] // cols):
                at = (half * (outs[3].shape[1] // cols) + chunk) * piece
                outs[3][row, chunk * cols : (chunk + 1) * cols] = source[at : at + piece, :].astype(F32)


def place_feed_kernel(*refs, count, groups, rows, cols):
    mine = lax.axis_index("ctx")
    first, second = refs[count:]
    for index in range(count):
        target = mine ^ index
        for group in range(groups):
            column = pl.ds(pl.multiple_of(group * count * cols + target * cols, cols), cols)
            first[:, column] = refs[index][:rows, group * cols : (group + 1) * cols].astype(F32)
        row = pl.ds(pl.multiple_of(target * cols, cols), cols)
        second[row, :] = refs[index][rows:, :].astype(F32)


def fold(near, sent):
    arrived = swap(sent, "ctx", 1)
    return near, arrived


def after(value, *others):
    return lax.optimization_barrier((value,) + others)[0]


def far_hop(parts):
    arrived = swap(parts[1], "ctx", 1)
    sent = (parts[0].astype(F32) + arrived.astype(F32)).astype(BF)
    return sent, swap(sent, "ctx", 2)


def spread_ctx(own):
    far = swap(own, "ctx", 2)
    near = swap(own, "ctx", 1)
    return [own, near, far, swap(far, "ctx", 1)]


def start_ctx(own):
    return [own, swap(own, "ctx", 1), swap(own, "ctx", 2)]


def finish_ctx(blocks, *before):
    far = after(blocks[2], *before)
    return blocks[:2] + [far, swap(far, "ctx", 1)]


def send_z(own):
    size = lax.axis_size("wsh")
    blocks = {0: own, 1: swap(own, "wsh", 1)}
    for bit in range(2, size, 2):
        blocks[bit] = swap(own, "wsh", bit)
    return blocks


def pass_y(blocks):
    size = lax.axis_size("wsh")
    for bit in range(2, size, 2):
        blocks[bit + 1] = swap(blocks[bit], "wsh", 1)
    return [blocks[bit] for bit in range(size)]


class Ranges:
    def __init__(self, low, high, tile, chunk, flip):
        self.tile, self.chunk, self.count = tile, chunk, low.shape[0] // tile
        low, high = low.reshape(self.count, tile), high.reshape(self.count, tile)
        self.rows = jnp.stack([low, high], 1)
        first, last = jnp.min(low, 1) // chunk, (jnp.max(high, 1) - 1) // chunk + 1
        self.meta = jnp.concatenate([flip.reshape(1), first, last]).astype(jnp.int32)


def fast_body(
    inputs,
    enc_states,
    cotangent,
    slot_order,
    seq_lengths,
    enc_lengths,
    self_query,
    self_key,
    self_value,
    self_out,
    cross_query,
    cross_key,
    cross_value,
    cross_out,
    feed_in,
    feed_out,
    norm_gains,
    norm_shifts,
):
    size, groups = lax.axis_size("ctx"), lax.axis_size("wsh")
    mine, row = lax.axis_index("ctx"), lax.axis_index("wsh")
    slots = inputs.shape[1]
    total = slots * size
    enc_slots = enc_states.shape[1]
    width = inputs.shape[2]
    rows = self_query.shape[0]
    cols = width // size
    piece = rows // size
    ff_cols = feed_in.shape[1] // size
    ff_rows = feed_out.shape[0] // size
    heads = cols // HEAD
    middle = total // 2
    part = size // 2
    block_bf, block_f = ((slots, width), BF), ((slots, width), F32)
    terms_f = ((2, width), F32)

    given = call_packing(give_pieces_kernel, [((2 * piece, width), BF)], self_out, cross_out)[0]
    given = swap(given, "wsh", 1)
    height = 3 * rows + piece * (width // cols)
    self_block = call_packing(
        functools.partial(pack_kernel, size=size, which=0),
        [((height + 16, cols), BF)],
        self_query,
        self_key,
        self_value,
        self_out,
        given,
        jnp.transpose(norm_gains),
        jnp.transpose(norm_shifts),
    )[0]
    self_blocks = send_z(self_block)
    token_blocks = start_ctx(inputs[0])
    self_blocks = pass_y(self_blocks)
    token_blocks = finish_ctx(token_blocks)
    cross_block = call_packing(
        functools.partial(pack_kernel, size=size, which=1),
        [((height, cols), BF)],
        after(cross_query, self_block),
        cross_key,
        cross_value,
        cross_out,
        given,
    )[0]
    packed = cross_block
    cross_block = gather_wsh(cross_block).reshape(groups, height, cols)
    feed = call_packing(
        functools.partial(pack_feed_kernel, groups=groups, size=size),
        [((2 * rows, ff_cols), BF)],
        after(feed_in, self_block),
        feed_out,
    )[0]
    feed = gather_wsh(after(feed, packed, self_blocks[2])).reshape(groups, 2 * rows, ff_cols)

    relative = jnp.arange(size, dtype=jnp.int32) ^ mine
    order = jnp.take(slot_order[0].reshape(size, slots), relative, axis=0).reshape(1, total)
    own_order = lax.dynamic_slice_in_dim(slot_order[0], mine * slots, slots).reshape(slots, 1)
    place = (relative[:, None] * slots + jnp.arange(slots, dtype=jnp.int32)).reshape(total)
    lower = jnp.arange(seq_lengths.shape[1])
    lower = lower[None, :] <= lower[:, None]
    ends = jnp.sum(jnp.where(lower, seq_lengths[0][None, :], 0), 1)
    enc_ends = jnp.sum(jnp.where(lower, enc_lengths[0][None, :], 0), 1)
    passed = ends[None, :] <= place[:, None]
    starts = jnp.max(jnp.where(passed, ends[None, :], 0), 1)
    enc_from = jnp.max(jnp.where(passed, enc_ends[None, :], 0), 1)
    enc_to = jnp.min(jnp.where(passed, enc_slots * size, enc_ends[None, :]), 1)
    self_range = Ranges(starts, place + 1, 256, 256, mine * (slots // 256))
    cross_range = Ranges(enc_from, enc_to, 256, 128, mine * (enc_slots // 128))
    half = total // 512

    def unsort(blocks):
        return call(functools.partial(unsort_kernel, size=size), [block_f], (), own_order, *blocks)[0]

    hat_all, tokens = call(
        functools.partial(sort_kernel, size=size), [((total, width), F32), block_f], (), order, *token_blocks
    )

    square, tall = ((width, cols), BF), ((total, cols), BF)
    wq, wk, wv, wo, norms, normed_one, queries, keys, values = call(
        functools.partial(project_kernel, groups=groups, rows=rows, piece=piece),
        [square] * 3 + [((cols, width), BF), ((8, width), F32), ((total, width), BF)] + [tall] * 3,
        (),
        hat_all,
        *self_blocks,
    )
    lanes = heads * 256
    half_outs = [((middle, cols), BF), ((half, 1, lanes), F32)] + [block_bf] * part
    scratch = [pltpu.VMEM((1, lanes), F32), pltpu.VMEM((1, lanes), F32), pltpu.VMEM((cols, 256), F32)]

    def self_forward(side, queries):
        body = functools.partial(
            attend_forward_kernel,
            own_queries=False,
            parts=part,
            offset=side * half,
            count=self_range.count,
            chunk=self_range.chunk,
        )
        return call(
            body, half_outs, (self_range.meta,), queries, keys, values, self_range.rows, wo, scratch=scratch
        )

    encoder = spread_ctx(after(enc_states[0], normed_one))
    mixed_high, lse_high, *far = self_forward(1, queries)
    sent, arrived = far_hop(far)
    mixed_low, lse_low, *near = self_forward(0, after(queries, sent))

    def normalize(base, near, arrived, which):
        return call(
            functools.partial(norm_kernel, which=which),
            [block_f, block_bf],
            (),
            norms,
            base,
            near[0],
            swap(near[1], "ctx", 1),
            arrived,
        )

    after_self, normed = normalize(tokens, near, arrived, 1)
    outside = spread_ctx(after(cotangent[0], arrived))
    outside = call(functools.partial(pick_kernel, size=size), [block_f], (), order, *outside)[0]

    normed_two = start_ctx(normed)
    cq, ck, cv, co, enc_keys, enc_values = call(
        functools.partial(cross_prepare_kernel, size=size, rows=rows, piece=piece),
        [square] * 3 + [((cols, width), BF)] + [((enc_slots * size, cols), BF)] * 2,
        (),
        cross_block,
        *encoder,
    )

    def cross_forward(side):
        body = functools.partial(
            attend_forward_kernel,
            own_queries=True,
            parts=part,
            offset=side * half,
            count=cross_range.count,
            chunk=cross_range.chunk,
        )
        return call(
            body,
            [((middle, cols), BF)] + half_outs,
            (cross_range.meta,),
            *normed_two[side * part : (side + 1) * part],
            cq,
            enc_keys,
            enc_values,
            cross_range.rows,
            co,
            scratch=scratch,
        )

    cross_low = cross_forward(0)
    normed_two = finish_ctx(normed_two, cross_low[3])
    cross_high = cross_forward(1)
    sent, arrived = far_hop(cross_high[3:])
    after_cross, normed = normalize(after_self, cross_low[3:], arrived, 2)

    normed_three = start_ctx(normed)
    def feed_forward(side):
        return call(
            functools.partial(feed_forward_kernel, parts=part),
            [((middle, ff_cols), BF)] * 2 + [block_bf] * part,
            (),
            *normed_three[side * part : (side + 1) * part],
            feed,
        )

    hidden_low, slope_low, *near = feed_forward(0)
    normed_three = finish_ctx(normed_three, near[0])
    hidden_high, slope_high, *far = feed_forward(1)
    sent, arrived = far_hop(far)
    result, grad_ffn, grad, terms_three = call(
        norm_turn_kernel,
        [block_bf, block_f, block_bf, terms_f],
        (),
        norms,
        after_cross,
        outside,
        near[0],
        swap(near[1], "ctx", 1),
        arrived,
    )

    def denormalize(value, grad, near, arrived, which):
        return call(
            functools.partial(norm_back_kernel, which=which),
            [block_f, block_bf, terms_f],
            (),
            norms,
            value,
            grad,
            near[0],
            swap(near[1], "ctx", 1),
            arrived,
        )

    grad_in = start_ctx(grad)

    def feed_backward(side, slope):
        return call(
            functools.partial(feed_backward_kernel, parts=part),
            [((middle, ff_cols), BF)] + [block_bf] * part,
            (),
            *grad_in[side * part : (side + 1) * part],
            feed,
            slope,
        )

    change_low, *near = feed_backward(0, slope_low)
    grad_in = finish_ctx(grad_in, near[0])
    change_high, *far = feed_backward(1, slope_high)
    sent, arrived = far_hop(far)
    feed_grads = call_streaming(
        functools.partial(feed_grad_kernel, size=size, rows=rows),
        ((groups, 2 * rows, width), BF),
        groups // 2,
        *normed_three,
        change_low,
        after(change_high, sent),
        hidden_low,
        hidden_high,
        *grad_in,
    )
    grad_cross, grad, terms_two = denormalize(after_cross, grad_ffn, near, after(arrived, feed_grads), 2)
    feed_grads = scatter_wsh(after(feed_grads, arrived).reshape(groups * 2 * rows, width))

    def weight_grads(terms, operands, out_grad, odd):
        height = 3 * rows + piece * (width // cols)
        count = groups if odd is None else groups // 2
        body = functools.partial(weight_grad_kernel, terms=terms, odd=odd, rows=rows, piece=piece, count=count)
        outs = [((count * height, cols), F32 if odd == 0 else BF)]
        if odd is None:
            return call_streaming(body, outs[0], count, *operands, out_grad)
        return call(body, outs, (), *operands, out_grad)[0]

    def backward(span, side, own_queries, sources, queries, mixed, lse, keys, values, wo, wq, before):
        body = functools.partial(
            attend_backward_kernel,
            own_queries=own_queries,
            parts=part,
            offset=side * half,
            count=span.count,
            chunk=span.chunk,
            fresh=before is None,
        )
        operands = [*sources, queries, mixed, lse, span.rows, keys, values, wo]
        if own_queries:
            operands.append(wq)
        aliases = {}
        if before is not None:
            aliases = {1 + len(operands) + i: 1 + i for i in range(3)}
            operands += before
        outs = [((middle, cols), BF), (keys.shape, F32), (keys.shape, F32), ((cols, width), F32)]
        if own_queries:
            outs += [block_bf] * part
        return call(
            body,
            outs,
            (span.meta,),
            *operands,
            scratch=[pltpu.VMEM((middle, cols), BF), pltpu.VMEM((cols, 256), F32)],
            aliases=aliases,
        )

    grad_in = start_ctx(grad)
    low = backward(
        cross_range, 0, True, grad_in[:part], *cross_low[:3], enc_keys, enc_values, co, cq, None
    )
    grad_in = finish_ctx(grad_in, low[4])
    high = backward(
        cross_range, 1, True, grad_in[part:], *cross_high[:3], enc_keys, enc_values, co, cq, list(low[1:4])
    )
    sent, arrived = far_hop(high[4:])
    dk, dv, dwo = high[1:4]
    operands = [*normed_two, low[0], high[0], *encoder, dk, dv]
    terms = []
    for index in range(size):
        side = index // part
        terms.append((0, index, 0, size + side, (index % part) * slots, slots))
    for index in range(size):
        for which in (1, 2):
            terms.append((which, size + 2 + index, 0, 2 * size + 1 + which, index * enc_slots, enc_slots))
    dk = after(dk, sent)
    operands[-2] = dk
    cross_share_local = weight_grads(tuple(terms), operands, dwo, None)
    enc_parts = call(encoder_grad_kernel, [((enc_slots, width), BF)] * size, (), dk, dv, ck, cv)
    cross_share = scatter_wsh(after(cross_share_local, arrived))
    arrived = after(arrived, cross_share_local, *enc_parts)
    grad_self, grad, terms_one = denormalize(after_self, grad_cross, low[4:], arrived, 1)

    grad_in = start_ctx(grad)
    low = backward(
        self_range, 0, False, grad_in[:part], queries, mixed_low, lse_low, keys, values, wo, None, None
    )
    grad_in = finish_ctx(grad_in, low[0])
    result = start_ctx(after(result, grad_in[2]))
    enc_sent, enc_far = far_hop([after(enc_parts[2], grad_in[2]), enc_parts[3]])
    enc_near = swap(enc_parts[1], "ctx", 1)
    enc_grad = enc_parts[0].astype(F32) + enc_near.astype(F32) + enc_far.astype(F32)
    high = backward(
        self_range, 1, False, grad_in[part:], queries, mixed_high, lse_high, keys, values, wo, None, list(low[1:4])
    )
    dk, dv, dwo = high[1:4]

    def back_project(side, dq):
        body = functools.partial(back_project_kernel, first=side * middle)
        return call(body, [block_bf] * part, (), dq, dk, dv, wq, wk, wv)

    far = back_project(1, high[0])
    operands = [normed_one, low[0], high[0], after(dk, result[2]), dv]
    terms = ((0, 0, 0, 1, 0, middle), (0, 0, middle, 2, 0, middle), (1, 0, 0, 3, 0, total), (2, 0, 0, 4, 0, total))
    odd = weight_grads(terms, operands, dwo, 1)
    sent, arrived = far_hop(far)
    self_odd = swap(odd, "wsh", 1)
    near = back_project(0, after(low[0], sent, odd))
    self_even = weight_grads(terms, operands, after(dwo, *near), 0)

    feed_blocks = start_ctx(after(feed_grads, sent))
    unused, grad, terms_zero = denormalize(tokens, grad_self, near, after(arrived, self_even), 0)
    input_grad = start_ctx(grad)

    def finish(result, extra=0):
        fourth = result[3 * rows : height]
        pair = jnp.concatenate([fourth, swap(fourth, "wsh", 1)], 0)
        pair = jnp.where(row % 2 == mine // 2, pair, swap(pair, "ctx", 2))
        three = result[: 3 * rows]
        outs = [((rows, width), F32)] * 4
        if extra:
            three = jnp.concatenate([three, result[height:]], 0)
            outs.append(((extra, rows), F32))
        return call(
            functools.partial(place_square_kernel, count=size, rows=rows, piece=piece),
            outs,
            (),
            *spread_ctx(three),
            pair,
            swap(pair, "ctx", 1),
        )

    terms = jnp.concatenate([terms_zero, terms_one, terms_two, terms_three], 0)
    tall = (height + 16, cols)
    share, *sent = call(
        functools.partial(sum_kernel, rows=rows, height=height),
        [(tall, F32)] + [(tall, BF)] * (groups // 2 - 1),
        (),
        after(self_even, feed_blocks[2], input_grad[2]),
        after(self_odd, grad),
        terms,
        swap(terms, "wsh", 1),
    )
    parts = [swap(value, "wsh", 2 * index + 2) for index, value in enumerate(sent)]
    feed_in_grad, feed_out_grad = call(
        functools.partial(place_feed_kernel, count=size, groups=groups, rows=rows, cols=ff_rows),
        [((rows, groups * size * ff_rows), F32), ((size * ff_rows, width), F32)],
        (),
        *finish_ctx(feed_blocks, sent[0]),
    )
    result = unsort(finish_ctx(result, sent[0]))
    input_grad = unsort(finish_ctx(input_grad, sent[0]))
    parts = after(tuple(parts), result, input_grad, feed_in_grad)
    for part in parts:
        share = share + part.astype(F32)
    share = share.astype(BF)
    *self_grads, terms = finish(share, 16)
    terms = jnp.transpose(terms[:8])
    cross_grads = finish(after(cross_share, share))
    return (
        result[None],
        input_grad[None],
        enc_grad[None],
        *self_grads,
        *cross_grads,
        feed_in_grad,
        feed_out_grad,
        terms[:, 0::2],
        terms[:, 1::2],
    )


def solution(mesh):
    token, weight = P("wsh", "ctx", None), P("wsh", None)
    in_specs = (token,) * 3 + (weight,) * 15
    out_specs = (token,) * 3 + (weight,) * 12
    body = fast_body if mesh.shape["ctx"] == 4 else plain_body
    return jax.shard_map(body, mesh=mesh, in_specs=in_specs, out_specs=out_specs, check_vma=False)
```

profile of v0, /device:TPU:0, one launch (start us, length us, event | category | flops | bytes accessed | tf_op | source)
XLA Modules:
  0.0 478.6 jit_solution(353369881917713900)
XLA Ops:
  8.3 3.0 collective-permute-start.3
  11.3 3.5 collective-permute-done.3.refs_4_
  17.3 2.5 shard_map.296
  21.8 2.4 shard_map.302
  24.2 3.4 collective-permute-done.5.refs_2_
  31.5 3.6 collective-permute-start.9
  35.4 4.6 collective-permute-done.1.refs_2_
  41.2 6.3 %collective-permute-done.9.refs_6_ = bf16[528,256]{1,0:T(8,128)(2,1)S(1)} collective-permute-done((bf16[528,256]{1,0:T(8,128)(2,1)S(1)}, bf16[528,256]{1,0:T(8,128)(2,1)S(1)}, u32[]{:S(2)}, u32[]{:S(2)}) %collective-permute-start.9) | collective-permute-done | bytes 270368 | tf_op jit(solution)/shard_map/ppermute | solution.py:29
  49.1 16.5 %collective-permute-done.7.refs_4_ = bf16[528,256]{1,0:T(8,128)(2,1)} collective-permute-done((bf16[528,256]{1,0:T(8,128)(2,1)S(1)}, bf16[528,256]{1,0:T(8,128)(2,1)}, u32[]{:S(2)}, u32[]{:S(2)}) %collective-permute-start.7) | collective-permute-done | bytes 270368 | tf_op jit(solution)/shard_map/ppermute | solution.py:29
  67.8 4.1 shard_map.289
  72.9 7.8 %collective-permute-done.10.refs_7_ = bf16[528,256]{1,0:T(8,128)(2,1)S(1)} collective-permute-done((bf16[528,256]{1,0:T(8,128)(2,1)S(1)}, bf16[528,256]{1,0:T(8,128)(2,1)S(1)}, u32[]{:S(2)}, u32[]{:S(2)}) %collective-permute-start.10) | collective-permute-done | bytes 270368 | tf_op jit(solution)/shard_map/ppermute | solution.py:29
  80.7 5.8 %collective-permute-done.8.refs_5_ = bf16[528,256]{1,0:T(8,128)(2,1)S(1)} collective-permute-done((bf16[528,256]{1,0:T(8,128)(2,1)}, bf16[528,256]{1,0:T(8,128)(2,1)S(1)}, u32[]{:S(2)}, u32[]{:S(2)}) %collective-permute-start.8) | collective-permute-done | bytes 270368 | tf_op jit(solution)/shard_map/ppermute | solution.py:29
  87.5 3.5 shard_map.292
  91.0 4.9 %shard_map.293 = (bf16[512,256]{1,0:T(8,128)(2,1)S(1)}, f32[2,1,1024]{2,1,0:T(1,128)S(1)}, bf16[256,1024]{1,0:T(8,128)(2,1)S(1)}, bf16[256,1024]{1,0:T(8,128)(2,1)S(1)}) custom-call(s32[9]{0:T(128)S(1)} %pad_add_fusion.2.meta, bf16[1024,256]{1,0:T(8,128)(2,1)S(1)} %get-tuple-element.165.refs_0_.refs_2_, ...), custom_call_target="tpu_custom_call" | custom-call | flops 1048576 | bytes 65536 | tf_op jit(solution)/shard_map/pallas_call | solution.py:496
  96.6 1.9 collective-permute-done.11
  99.5 4.2 shard_map.294
  107.6 12.9 %collective-permute-done.13.refs_2_ = bf16[256,1024]{1,0:T(8,128)(2,1)} collective-permute-done((bf16[256,1024]{1,0:T(8,128)(2,1)}, bf16[256,1024]{1,0:T(8,128)(2,1)}, u32[]{:S(2)}, u32[]{:S(2)}) %collective-permute-start.13) | collective-permute-done | bytes 524320 | tf_op jit(solution)/shard_map/ppermute | solution.py:29
  122.8 2.5 shard_map.295
  138.8 5.6 %shard_map.298 = (bf16[512,256]{1,0:T(8,128)(2,1)S(1)}, bf16[512,256]{1,0:T(8,128)(2,1)S(1)}, f32[2,1,1024]{2,1,0:T(1,128)S(1)}, bf16[256,1024]{1,0:T(8,128)(2,1)S(1)}, bf16[256,1024]{1,0:T(8,128)(2,1)S(1)}) custom-call(s32[9]{0:T(128)S(1)} %pad_add_fusion.3.meta, bf16[256,1024]{1,0:T(8,128)(2,1)} %get-tuple-element.169.refs_0_, ...), custom_call_target="tpu_custom_call" | custom-call | flops 1048576 | bytes 65536 | tf_op jit(solution)/shard_map/pallas_call | solution.py:496
  148.0 6.0 %shard_map.299 = (bf16[512,256]{1,0:T(8,128)(2,1)S(1)}, bf16[512,256]{1,0:T(8,128)(2,1)S(1)}, f32[2,1,1024]{2,1,0:T(1,128)S(1)}, bf16[256,1024]{1,0:T(8,128)(2,1)S(1)}, bf16[256,1024]{1,0:T(8,128)(2,1)S(1)}) custom-call(s32[9]{0:T(128)S(1)} %pad_add_fusion.3.meta, bf16[256,1024]{1,0:T(8,128)(2,1)} %collective-permute-done.19.refs_0_.refs_2_, ...), custom_call_target="tpu_custom_call" | custom-call | flops 1048576 | bytes 65536 | tf_op jit(solution)/shard_map/pallas_call | solution.py:496
  157.5 13.5 %collective-permute-done.22.refs_2_ = bf16[256,1024]{1,0:T(8,128)(2,1)S(1)} collective-permute-done((bf16[256,1024]{1,0:T(8,128)(2,1)S(1)}, bf16[256,1024]{1,0:T(8,128)(2,1)S(1)}, u32[]{:S(2)}, u32[]{:S(2)}) %collective-permute-start.22) | collective-permute-done | bytes 524320 | tf_op jit(solution)/shard_map/ppermute | solution.py:29
  176.2 2.2 copy-done
  179.5 4.5 shard_map.303
  183.9 4.0 collective-permute-done.28.refs_0_.refs_2_
  190.1 4.3 shard_map.304
  195.0 7.3 %collective-permute-done.24.refs_2_ = bf16[256,1024]{1,0:T(8,128)(2,1)S(1)} collective-permute-done((bf16[256,1024]{1,0:T(8,128)(2,1)S(1)}, bf16[256,1024]{1,0:T(8,128)(2,1)S(1)}, u32[]{:S(2)}, u32[]{:S(2)}) %collective-permute-start.24) | collective-permute-done | bytes 524320 | tf_op jit(solution)/shard_map/ppermute | solution.py:29
  205.0 12.0 %collective-permute-done.31.refs_2_ = bf16[256,1024]{1,0:T(8,128)(2,1)S(1)} collective-permute-done((bf16[256,1024]{1,0:T(8,128)(2,1)S(1)}, bf16[256,1024]{1,0:T(8,128)(2,1)S(1)}, u32[]{:S(2)}, u32[]{:S(2)}) %collective-permute-start.31) | collective-permute-done | bytes 524320 | tf_op jit(solution)/shard_map/ppermute | solution.py:29
  219.9 2.4 shard_map.306
  223.9 8.5 %collective-permute-done.34.refs_0_.refs_10_ = bf16[256,1024]{1,0:T(8,128)(2,1)S(1)} collective-permute-done((bf16[256,1024]{1,0:T(8,128)(2,1)S(1)}, bf16[256,1024]{1,0:T(8,128)(2,1)S(1)}, u32[]{:S(2)}, u32[]{:S(2)}) %collective-permute-start.34) | collective-permute-done | bytes 524320 | tf_op jit(solution)/shard_map/ppermute | solution.py:29
  232.4 1.9 collective-permute-done.35.refs_1_.refs_11_
  234.3 14.2 %shard_map.307 = (bf16[512,1024]{1,0:T(8,128)(2,1)S(1)}, bf16[256,1024]{1,0:T(8,128)(2,1)S(1)}, bf16[256,1024]{1,0:T(8,128)(2,1)S(1)}) custom-call(bf16[256,1024]{1,0:T(8,128)(2,1)S(1)} %collective-permute-done.34.refs_0_.refs_10_, bf16[256,1024]{1,0:T(8,128)(2,1)S(1)} %collective-permute-done.35.refs_1_.refs_11_, bf16[8,256,1024]{2,1,0:T(8,128)(2,1)S(1)} %bitcast.34, ...), custom_call_target="tpu_custom_call" | custom-call | flops 1048576 | bytes 65536 | tf_op jit(solution)/shard_map/pallas_call | solution.py:496
  251.3 6.8 %shard_map.308 = bf16[8,256,1024]{2,1,0:T(8,128)(2,1)S(1)} custom-call(bf16[256,1024]{1,0:T(8,128)(2,1)} %get-tuple-element.184.refs_0_, bf16[256,1024]{1,0:T(8,128)(2,1)S(1)} %copy-done.37, bf16[256,1024]{1,0:T(8,128)(2,1)} %collective-permute-done.28.refs_0_.refs_2_, bf16[256,1024]{1,0:T(8,128)(2,1)S(1)} %collective-permute-done.29.refs_1_.refs_3_, ...), custom_call_target="tpu_custom_call" | custom-call | flops 1048576 | bytes 65536 | tf_op jit(solution)/shard_map/pallas_call | solution.py:496
  258.1 2.0 copy-done.2
  260.0 4.6 collective-permute-done.37.refs_2_
  265.6 2.1 collective-permute-done.33.refs_1_
  276.2 6.5 %shard_map.310 = (bf16[512,256]{1,0:T(8,128)(2,1)S(1)}, f32[512,256]{1,0:T(8,128)S(1)}, f32[512,256]{1,0:T(8,128)S(1)}, f32[256,1024]{1,0:T(8,128)S(1)}, bf16[25...) custom-call(s32[9]{0:T(128)S(1)} %pad_add_fusion.3.meta, bf16[256,1024]{1,0:T(8,128)(2,1)S(1)} %get-tuple-element.209.refs_0_, ...), custom_call_target="tpu_custom_call" | custom-call | flops 1048576 | bytes 65536 | tf_op jit(solution)/shard_map/pallas_call | solution.py:496
  283.5 5.1 %collective-permute-done.40.refs_0_ = bf16[256,1024]{1,0:T(8,128)(2,1)S(1)} collective-permute-done((bf16[256,1024]{1,0:T(8,128)(2,1)S(1)}, bf16[256,1024]{1,0:T(8,128)(2,1)S(1)}, u32[]{:S(2)}, u32[]{:S(2)}) %collective-permute-start.40) | collective-permute-done | bytes 524320 | tf_op jit(solution)/shard_map/ppermute | solution.py:29
  288.6 1.9 collective-permute-done.41.refs_1_
  290.5 6.4 %shard_map.311 = (bf16[512,256]{1,0:T(8,128)(2,1)S(1)}, f32[512,256]{1,0:T(8,128)S(1)}, f32[512,256]{1,0:T(8,128)S(1)}, f32[256,1024]{1,0:T(8,128)S(1)}, bf16[25...) custom-call(s32[9]{0:T(128)S(1)} %pad_add_fusion.3.meta, ...), custom_call_target="tpu_custom_call", output_to_operand_aliasing={{1}: (11, {}), {2}: (12, {}), {3}: (13, {})} | custom-call | flops 1048576 | bytes 65536 | tf_op jit(solution)/shard_map/pallas_call | solution.py:496
  300.1 5.1 %shard_map.312 = bf16[4096,256]{1,0:T(8,128)(2,1)S(1)} custom-call(bf16[256,1024]{1,0:T(8,128)(2,1)} %get-tuple-element.169.refs_0_, bf16[256,1024]{1,0:T(8,128)(2,1)} %collective-permute-done.14.refs_1_, bf16[256,1024]{1,0:T(8,128)(2,1)} %collective-permute-done.19.refs_0_.refs_2_, bf16[256,1024]{1,0:T(8,128)(2,1)S(1)} %copy-done.40, ...), custom_call_target="tpu_custom_call" | custom-call | flops 1048576 | bytes 65536 | tf_op jit(solution)/shard_map/pallas_call | solution.py:496
  306.6 7.6 %collective-permute-done.43.refs_2_ = bf16[256,1024]{1,0:T(8,128)(2,1)} collective-permute-done((bf16[256,1024]{1,0:T(8,128)(2,1)}, bf16[256,1024]{1,0:T(8,128)(2,1)}, u32[]{:S(2)}, u32[]{:S(2)}) %collective-permute-start.43) | collective-permute-done | bytes 524320 | tf_op jit(solution)/shard_map/ppermute | solution.py:29
  318.5 2.2 shard_map.313
  323.3 2.1 shard_map.314
  327.4 4.7 shard_map.315
  332.2 7.7 %collective-permute-done.44.refs_0_ = bf16[256,1024]{1,0:T(8,128)(2,1)S(1)} collective-permute-done((bf16[256,1024]{1,0:T(8,128)(2,1)S(1)}, bf16[256,1024]{1,0:T(8,128)(2,1)S(1)}, u32[]{:S(2)}, u32[]{:S(2)}) %collective-permute-start.44) | collective-permute-done | bytes 524320 | tf_op jit(solution)/shard_map/ppermute | solution.py:29
  341.8 6.4 %shard_map.316 = (bf16[512,256]{1,0:T(8,128)(2,1)S(1)}, f32[1024,256]{1,0:T(8,128)S(1)}, f32[1024,256]{1,0:T(8,128)S(1)}, f32[256,1024]{1,0:T(8,128)S(1)}) custom-call(s32[9]{0:T(128)S(1)} %pad_add_fusion.2.meta, bf16[256,1024]{1,0:T(8,128)(2,1)S(1)} %collective-permute-done.44.refs_0_, ...), custom_call_target="tpu_custom_call", output_to_operand_aliasing={{1}: (10, {}), {2}: (11, {}), {3}: (12, {})} | custom-call | flops 1048576 | bytes 65536 | tf_op jit(solution)/shard_map/pallas_call | solution.py:496
  349.5 4.7 collective-permute-done.47.refs_2_
  354.2 2.7 shard_map.318
  359.1 2.0 shard_map.320.even
  362.4 8.4 %collective-permute-done.52.refs_2_ = bf16[256,1024]{1,0:T(8,128)(2,1)S(1)} collective-permute-done((bf16[256,1024]{1,0:T(8,128)(2,1)S(1)}, bf16[256,1024]{1,0:T(8,128)(2,1)S(1)}, u32[]{:S(2)}, u32[]{:S(2)}) %collective-permute-start.52) | collective-permute-done | bytes 524320 | tf_op jit(solution)/shard_map/ppermute | solution.py:29
  370.8 2.1 shard_map.321
  375.0 15.8 %collective-permute-done.54.odd = bf16[2048,256]{1,0:T(8,128)(2,1)S(1)} collective-permute-done((bf16[2048,256]{1,0:T(8,128)(2,1)}, bf16[2048,256]{1,0:T(8,128)(2,1)S(1)}, u32[]{:S(2)}, u32[]{:S(2)}) %collective-permute-start.54) | collective-permute-done | bytes 1048608 | tf_op jit(solution)/shard_map/ppermute | solution.py:29
  390.8 6.3 %collective-permute-done.50.refs_2_ = bf16[256,1024]{1,0:T(8,128)(2,1)S(1)} collective-permute-done((bf16[256,1024]{1,0:T(8,128)(2,1)}, bf16[256,1024]{1,0:T(8,128)(2,1)S(1)}, u32[]{:S(2)}, u32[]{:S(2)}) %collective-permute-start.50) | collective-permute-done | bytes 524320 | tf_op jit(solution)/shard_map/ppermute | solution.py:29
  404.9 4.4 collective-permute-start.64
  413.6 2.4 shard_map.325
  416.1 2.9 shard_map.324
  419.5 2.9 shard_map.323
  422.5 9.3 %collective-permute-done.63 = bf16[528,256]{1,0:T(8,128)(2,1)} collective-permute-done((bf16[528,256]{1,0:T(8,128)(2,1)}, bf16[528,256]{1,0:T(8,128)(2,1)}, u32[]{:S(2)}, u32[]{:S(2)}) %collective-permute-start.63) | collective-permute-done | bytes 270368 | tf_op jit(solution)/shard_map/ppermute | solution.py:29
  433.0 4.8 %reduce-scatter.5.cloned.1.call-done = bf16[512,256]{1,0:T(8,128)(2,1)} async-done(((bf16[4096,256]{1,0:T(8,128)(2,1)}), bf16[512,256]{1,0:T(8,128)(2,1)}) %reduce-scatter.5.cloned.1.call-update) | async-done | bytes 262160 | tf_op jit(solution)/shard_map/reduce_scatter | solution.py:259
  441.7 1.9 collective-permute-start.74
  444.3 3.6 collective-permute-done.70
  447.9 6.7 %collective-permute-done.77 = bf16[256,256]{1,0:T(8,128)(2,1)S(1)} collective-permute-done((bf16[256,256]{1,0:T(8,128)(2,1)S(1)}, bf16[256,256]{1,0:T(8,128)(2,1)S(1)}, u32[]{:S(2)}, u32[]{:S(2)}) %collective-permute-start.77) | collective-permute-done | bytes 131104 | tf_op jit(solution)/shard_map/ppermute | solution.py:29
  455.0 5.2 %collective-permute-done.71 = bf16[256,256]{1,0:T(8,128)(2,1)S(1)} collective-permute-done((bf16[256,256]{1,0:T(8,128)(2,1)S(1)}, bf16[256,256]{1,0:T(8,128)(2,1)S(1)}, u32[]{:S(2)}, u32[]{:S(2)}) %collective-permute-start.71) | collective-permute-done | bytes 131104 | tf_op jit(solution)/shard_map/ppermute | solution.py:29
  461.6 4.5 collective-permute-done.68.refs_2_
  (427 shorter events, 121.6 us)
Async XLA Ops:
  7.2 123.7 %all-gather.3.cloned.1.call-start = ((), (), s32[]{:S(2)}) async-start(), calls=%async_computation.2 | async-start | bytes 2359296 | tf_op jit(solution)/shard_map/all_gather | solution.py:255
  8.3 6.5 %collective-permute-start.3 = (bf16[64,1024]{1,0:T(8,128)(2,1)S(1)}, bf16[64,1024]{1,0:T(8,128)(2,1)S(1)}, u32[]{:S(2)}, u32[]{:S(2)}) collective-permute-start(bf16[64,1024]{1,0:T(8,128)(2,1)S(1)} %shard_map.290), channel_id=1, source_target_pairs={{0,1},{1,0},{2,3},{3,2},{4,5},{5,4},{6,7},{7,6},{8,9},{9,8},{10,11... | collective-permute-start | bytes 393224 | tf_op jit(solution)/shard_map/ppermute | solution.py:29
  19.9 156.4 %all-gather.5.cloned.1.call-start = ((), (), s32[]{:S(2)}) async-start(), calls=%async_computation.3 | async-start | bytes 4718592 | tf_op jit(solution)/shard_map/all_gather | solution.py:255
  19.9 7.7 %collective-permute-start.5 = (bf16[528,256]{1,0:T(8,128)(2,1)S(1)}, bf16[528,256]{1,0:T(8,128)(2,1)S(1)}, u32[]{:S(2)}, u32[]{:S(2)}) collective-permute-start(bf16[528,256]{1,0:T(8,128)(2,1)S(1)} %shard_map.291.refs_0_), channel_id=1, source_target_pairs={{0,2},{1,3},{2,0},{3,1},{4,6},{5,7},{6,4},{7,5},{8,10},{9,11},{10,... | collective-permute-start | bytes 811016 | tf_op jit(solution)/shard_map/ppermute | solution.py:29
  27.7 345.5 %reduce-scatter.3.cloned.1.call-start = ((), (), s32[]{:S(2)}) async-start(), calls=%async_computation.4 | async-start | bytes 4718592 | tf_op jit(solution)/shard_map/reduce_scatter | solution.py:259
  27.7 12.3 %collective-permute-start.1 = (bf16[256,1024]{1,0:T(8,128)(2,1)S(1)}, bf16[256,1024]{1,0:T(8,128)(2,1)S(1)}, u32[]{:S(2)}, u32[]{:S(2)}) collective-permute-start(bf16[256,1024]{1,0:T(8,128)(2,1)S(1)} %bitcast.41), channel_id=1, source_target_pairs={{0,16},{8,24},{16,0},{24,8},{1,17},{9,25},{17,1},{25,9},{2,18},{10... | collective-permute-start | bytes 1572872 | tf_op jit(solution)/shard_map/ppermute | solution.py:29
  29.2 37.9 %collective-permute-start = (bf16[256,1024]{1,0:T(8,128)(2,1)S(1)}, bf16[256,1024]{1,0:T(8,128)(2,1)S(1)}, u32[]{:S(2)}, u32[]{:S(2)}) collective-permute-start(bf16[256,1024]{1,0:T(8,128)(2,1)S(1)} %bitcast.42), channel_id=1, source_target_pairs={{0,8},{8,0},{16,24},{24,16},{1,9},{9,1},{17,25},{25,17},{2,10},{10... | collective-permute-start | bytes 1572872 | tf_op jit(solution)/shard_map/ppermute | solution.py:29
  31.5 15.9 %collective-permute-start.9 = (bf16[528,256]{1,0:T(8,128)(2,1)S(1)}, bf16[528,256]{1,0:T(8,128)(2,1)S(1)}, u32[]{:S(2)}, u32[]{:S(2)}) collective-permute-start(bf16[528,256]{1,0:T(8,128)(2,1)S(1)} %shard_map.291.refs_0_), channel_id=1, source_target_pairs={{0,6},{1,7},{2,4},{3,5},{4,2},{5,3},{6,0},{7,1},{8,14},{9,15},{10,... | collective-permute-start | bytes 811016 | tf_op jit(solution)/shard_map/ppermute | solution.py:29
  35.1 30.5 %collective-permute-start.7 = (bf16[528,256]{1,0:T(8,128)(2,1)S(1)}, bf16[528,256]{1,0:T(8,128)(2,1)}, u32[]{:S(2)}, u32[]{:S(2)}) collective-permute-start(bf16[528,256]{1,0:T(8,128)(2,1)S(1)} %shard_map.291.refs_0_), channel_id=1, source_target_pairs={{0,4},{1,5},{2,6},{3,7},{4,0},{5,1},{6,2},{7,3},{8,12},{9,13},{10,... | collective-permute-start | bytes 811016 | tf_op jit(solution)/shard_map/ppermute | solution.py:29
  40.0 27.8 %collective-permute-start.2 = (bf16[256,1024]{1,0:T(8,128)(2,1)S(1)}, bf16[256,1024]{1,0:T(8,128)(2,1)S(1)}, u32[]{:S(2)}, u32[]{:S(2)}) collective-permute-start(bf16[256,1024]{1,0:T(8,128)(2,1)S(1)} %collective-permute-done.1.refs_2_), channel_id=1, source_target_pairs={{0,8},{8,0},{16,24},{24,16},{1,9},{9,1},{17,25},{25,17},{2,10},{10... | collective-permute-start | bytes 1572872 | tf_op jit(solution)/shard_map/ppermute | solution.py:29
  40.0 32.9 %collective-permute-start.4 = (bf16[528,256]{1,0:T(8,128)(2,1)S(1)}, bf16[528,256]{1,0:T(8,128)(2,1)S(1)}, u32[]{:S(2)}, u32[]{:S(2)}) collective-permute-start(bf16[528,256]{1,0:T(8,128)(2,1)S(1)} %shard_map.291.refs_0_), channel_id=1, source_target_pairs={{0,1},{1,0},{2,3},{3,2},{4,5},{5,4},{6,7},{7,6},{8,9},{9,8},{10,11... | collective-permute-start | bytes 811016 | tf_op jit(solution)/shard_map/ppermute | solution.py:29
  47.5 25.4 %collective-permute-start.6 = (bf16[528,256]{1,0:T(8,128)(2,1)S(1)}, bf16[528,256]{1,0:T(8,128)(2,1)S(1)}, u32[]{:S(2)}, u32[]{:S(2)}) collective-permute-start(bf16[528,256]{1,0:T(8,128)(2,1)S(1)} %collective-permute-done.5.refs_2_), channel_id=1, source_target_pairs={{0,1},{1,0},{2,3},{3,2},{4,5},{5,4},{6,7},{7,6},{8,9},{9,8},{10,11... | collective-permute-start | bytes 811016 | tf_op jit(solution)/shard_map/ppermute | solution.py:29
  65.6 15.1 %collective-permute-start.10 = (bf16[528,256]{1,0:T(8,128)(2,1)S(1)}, bf16[528,256]{1,0:T(8,128)(2,1)S(1)}, u32[]{:S(2)}, u32[]{:S(2)}) collective-permute-start(bf16[528,256]{1,0:T(8,128)(2,1)S(1)} %collective-permute-done.9.refs_6_), channel_id=1, source_target_pairs={{0,1},{1,0},{2,3},{3,2},{4,5},{5,4},{6,7},{7,6},{8,9},{9,8},{10,11... | collective-permute-start | bytes 811016 | tf_op jit(solution)/shard_map/ppermute | solution.py:29
  67.1 19.4 %collective-permute-start.8 = (bf16[528,256]{1,0:T(8,128)(2,1)}, bf16[528,256]{1,0:T(8,128)(2,1)S(1)}, u32[]{:S(2)}, u32[]{:S(2)}) collective-permute-start(bf16[528,256]{1,0:T(8,128)(2,1)} %collective-permute-done.7.refs_4_), channel_id=1, source_target_pairs={{0,1},{1,0},{2,3},{3,2},{4,5},{5,4},{6,7},{7,6},{8,9},{9,8},{10,11... | collective-permute-start | bytes 811016 | tf_op jit(solution)/shard_map/ppermute | solution.py:29
  105.4 15.1 %collective-permute-start.13 = (bf16[256,1024]{1,0:T(8,128)(2,1)}, bf16[256,1024]{1,0:T(8,128)(2,1)}, u32[]{:S(2)}, u32[]{:S(2)}) collective-permute-start(bf16[256,1024]{1,0:T(8,128)(2,1)} %add_convert_fusion.5), channel_id=1, source_target_pairs={{0,16},{8,24},{16,0},{24,8},{1,17},{9,25},{17,1},{25,9},{2,18},{10... | collective-permute-start | bytes 1572872 | tf_op jit(solution)/shard_map/ppermute | solution.py:29
  106.9 21.2 %collective-permute-start.16 = (bf16[128,1024]{1,0:T(8,128)(2,1)S(1)}, bf16[128,1024]{1,0:T(8,128)(2,1)}, u32[]{:S(2)}, u32[]{:S(2)}) collective-permute-start(bf16[128,1024]{1,0:T(8,128)(2,1)S(1)} %bitcast.37), channel_id=1, source_target_pairs={{0,16},{8,24},{16,0},{24,8},{1,17},{9,25},{17,1},{25,9},{2,18},{10... | collective-permute-start | bytes 786440 | tf_op jit(solution)/shard_map/ppermute | solution.py:29
  126.2 12.6 %collective-permute-start.14 = (bf16[256,1024]{1,0:T(8,128)(2,1)}, bf16[256,1024]{1,0:T(8,128)(2,1)}, u32[]{:S(2)}, u32[]{:S(2)}) collective-permute-start(bf16[256,1024]{1,0:T(8,128)(2,1)} %get-tuple-element.169.refs_0_), channel_id=1, source_target_pairs={{0,8},{8,0},{16,24},{24,16},{1,9},{9,1},{17,25},{25,17},{2,10},{10... | collective-permute-start | bytes 1572872 | tf_op jit(solution)/shard_map/ppermute | solution.py:29
  126.2 19.6 %collective-permute-start.19 = (bf16[256,1024]{1,0:T(8,128)(2,1)}, bf16[256,1024]{1,0:T(8,128)(2,1)}, u32[]{:S(2)}, u32[]{:S(2)}) collective-permute-start(bf16[256,1024]{1,0:T(8,128)(2,1)} %get-tuple-element.169.refs_0_), channel_id=1, source_target_pairs={{0,16},{8,24},{16,0},{24,8},{1,17},{9,25},{17,1},{25,9},{2,18},{10... | collective-permute-start | bytes 1572872 | tf_op jit(solution)/shard_map/ppermute | solution.py:29
  156.9 14.2 %collective-permute-start.22 = (bf16[256,1024]{1,0:T(8,128)(2,1)S(1)}, bf16[256,1024]{1,0:T(8,128)(2,1)S(1)}, u32[]{:S(2)}, u32[]{:S(2)}) collective-permute-start(bf16[256,1024]{1,0:T(8,128)(2,1)S(1)} %add_convert_fusion.4), channel_id=1, source_target_pairs={{0,16},{8,24},{16,0},{24,8},{1,17},{9,25},{17,1},{25,9},{2,18},{10... | collective-permute-start | bytes 1572872 | tf_op jit(solution)/shard_map/ppermute | solution.py:29
  173.3 14.7 %collective-permute-start.28 = (bf16[256,1024]{1,0:T(8,128)(2,1)}, bf16[256,1024]{1,0:T(8,128)(2,1)}, u32[]{:S(2)}, u32[]{:S(2)}) collective-permute-start(bf16[256,1024]{1,0:T(8,128)(2,1)} %get-tuple-element.184.refs_0_), channel_id=1, source_target_pairs={{0,16},{8,24},{16,0},{24,8},{1,17},{9,25},{17,1},{25,9},{2,18},{10... | collective-permute-start | bytes 1572872 | tf_op jit(solution)/shard_map/ppermute | solution.py:29
  188.0 14.3 %collective-permute-start.24 = (bf16[256,1024]{1,0:T(8,128)(2,1)S(1)}, bf16[256,1024]{1,0:T(8,128)(2,1)S(1)}, u32[]{:S(2)}, u32[]{:S(2)}) collective-permute-start(bf16[256,1024]{1,0:T(8,128)(2,1)S(1)} %bitcast.44), channel_id=1, source_target_pairs={{0,16},{8,24},{16,0},{24,8},{1,17},{9,25},{17,1},{25,9},{2,18},{10... | collective-permute-start | bytes 1572872 | tf_op jit(solution)/shard_map/ppermute | solution.py:29
  194.4 8.4 %collective-permute-start.30 = (bf16[256,1024]{1,0:T(8,128)(2,1)S(1)}, bf16[256,1024]{1,0:T(8,128)(2,1)S(1)}, u32[]{:S(2)}, u32[]{:S(2)}) collective-permute-start(bf16[256,1024]{1,0:T(8,128)(2,1)S(1)} %get-tuple-element.191), channel_id=1, source_target_pairs={{0,8},{8,0},{16,24},{24,16},{1,9},{9,1},{17,25},{25,17},{2,10},{10... | collective-permute-start | bytes 1572872 | tf_op jit(solution)/shard_map/ppermute | solution.py:29
  194.6 9.1 %collective-permute-start.23 = (bf16[256,1024]{1,0:T(8,128)(2,1)S(1)}, bf16[256,1024]{1,0:T(8,128)(2,1)S(1)}, u32[]{:S(2)}, u32[]{:S(2)}) collective-permute-start(bf16[256,1024]{1,0:T(8,128)(2,1)S(1)} %bitcast.45), channel_id=1, source_target_pairs={{0,8},{8,0},{16,24},{24,16},{1,9},{9,1},{17,25},{25,17},{2,10},{10... | collective-permute-start | bytes 1572872 | tf_op jit(solution)/shard_map/ppermute | solution.py:29
  202.3 2.7 collective-permute-start.27
  203.0 13.9 %collective-permute-start.31 = (bf16[256,1024]{1,0:T(8,128)(2,1)S(1)}, bf16[256,1024]{1,0:T(8,128)(2,1)S(1)}, u32[]{:S(2)}, u32[]{:S(2)}) collective-permute-start(bf16[256,1024]{1,0:T(8,128)(2,1)S(1)} %add_convert_fusion.3), channel_id=1, source_target_pairs={{0,16},{8,24},{16,0},{24,8},{1,17},{9,25},{17,1},{25,9},{2,18},{10... | collective-permute-start | bytes 1572872 | tf_op jit(solution)/shard_map/ppermute | solution.py:29
  218.0 14.3 %collective-permute-start.34 = (bf16[256,1024]{1,0:T(8,128)(2,1)S(1)}, bf16[256,1024]{1,0:T(8,128)(2,1)S(1)}, u32[]{:S(2)}, u32[]{:S(2)}) collective-permute-start(bf16[256,1024]{1,0:T(8,128)(2,1)S(1)} %get-tuple-element.194.refs_0_.refs_8_), channel_id=1, source_target_pairs={{0,16},{8,24},{16,0},{24,8},{1,17},{9,25},{17,1},{25,9},{2,18},{10... | collective-permute-start | bytes 1572872 | tf_op jit(solution)/shard_map/ppermute | solution.py:29
  250.6 14.0 %collective-permute-start.37 = (bf16[256,1024]{1,0:T(8,128)(2,1)S(1)}, bf16[256,1024]{1,0:T(8,128)(2,1)S(1)}, u32[]{:S(2)}, u32[]{:S(2)}) collective-permute-start(bf16[256,1024]{1,0:T(8,128)(2,1)S(1)} %add_convert_fusion.2), channel_id=1, source_target_pairs={{0,16},{8,24},{16,0},{24,8},{1,17},{9,25},{17,1},{25,9},{2,18},{10... | collective-permute-start | bytes 1572872 | tf_op jit(solution)/shard_map/ppermute | solution.py:29
  265.5 172.4 %reduce-scatter.5.cloned.1.call-start = ((), (), s32[]{:S(2)}) async-start(), calls=%async_computation.5 | async-start | bytes 2359296 | tf_op jit(solution)/shard_map/reduce_scatter | solution.py:259
  274.5 14.1 %collective-permute-start.40 = (bf16[256,1024]{1,0:T(8,128)(2,1)S(1)}, bf16[256,1024]{1,0:T(8,128)(2,1)S(1)}, u32[]{:S(2)}, u32[]{:S(2)}) collective-permute-start(bf16[256,1024]{1,0:T(8,128)(2,1)S(1)} %get-tuple-element.209.refs_0_), channel_id=1, source_target_pairs={{0,16},{8,24},{16,0},{24,8},{1,17},{9,25},{17,1},{25,9},{2,18},{10... | collective-permute-start | bytes 1572872 | tf_op jit(solution)/shard_map/ppermute | solution.py:29
  300.0 14.3 %collective-permute-start.43 = (bf16[256,1024]{1,0:T(8,128)(2,1)}, bf16[256,1024]{1,0:T(8,128)(2,1)}, u32[]{:S(2)}, u32[]{:S(2)}) collective-permute-start(bf16[256,1024]{1,0:T(8,128)(2,1)} %add_convert_fusion.1), channel_id=1, source_target_pairs={{0,16},{8,24},{16,0},{24,8},{1,17},{9,25},{17,1},{25,9},{2,18},{10... | collective-permute-start | bytes 1572872 | tf_op jit(solution)/shard_map/ppermute | solution.py:29
  300.0 22.2 %collective-permute-start.39 = (bf16[256,1024]{1,0:T(8,128)(2,1)}, bf16[256,1024]{1,0:T(8,128)(2,1)}, u32[]{:S(2)}, u32[]{:S(2)}) collective-permute-start(bf16[256,1024]{1,0:T(8,128)(2,1)} %get-tuple-element.214), channel_id=1, source_target_pairs={{0,8},{8,0},{16,24},{24,16},{1,9},{9,1},{17,25},{25,17},{2,10},{10... | collective-permute-start | bytes 1572872 | tf_op jit(solution)/shard_map/ppermute | solution.py:29
  325.5 14.3 %collective-permute-start.44 = (bf16[256,1024]{1,0:T(8,128)(2,1)S(1)}, bf16[256,1024]{1,0:T(8,128)(2,1)S(1)}, u32[]{:S(2)}, u32[]{:S(2)}) collective-permute-start(bf16[256,1024]{1,0:T(8,128)(2,1)S(1)} %get-tuple-element.237.refs_0_), channel_id=1, source_target_pairs={{0,16},{8,24},{16,0},{24,8},{1,17},{9,25},{17,1},{25,9},{2,18},{10... | collective-permute-start | bytes 1572872 | tf_op jit(solution)/shard_map/ppermute | solution.py:29
  339.9 14.3 %collective-permute-start.47 = (bf16[256,1024]{1,0:T(8,128)(2,1)S(1)}, bf16[256,1024]{1,0:T(8,128)(2,1)S(1)}, u32[]{:S(2)}, u32[]{:S(2)}) collective-permute-start(bf16[256,1024]{1,0:T(8,128)(2,1)S(1)} %copy-done.59), channel_id=1, source_target_pairs={{0,16},{8,24},{16,0},{24,8},{1,17},{9,25},{17,1},{25,9},{2,18},{10... | collective-permute-start | bytes 1572872 | tf_op jit(solution)/shard_map/ppermute | solution.py:29
  349.3 7.7 %collective-permute-start.49 = (bf16[256,1024]{1,0:T(8,128)(2,1)S(1)}, bf16[256,1024]{1,0:T(8,128)(2,1)S(1)}, u32[]{:S(2)}, u32[]{:S(2)}) collective-permute-start(bf16[256,1024]{1,0:T(8,128)(2,1)S(1)} %get-tuple-element.257), channel_id=1, source_target_pairs={{0,8},{8,0},{16,24},{24,16},{1,9},{9,1},{17,25},{25,17},{2,10},{10... | collective-permute-start | bytes 1572872 | tf_op jit(solution)/shard_map/ppermute | solution.py:29
  357.2 13.6 %collective-permute-start.52 = (bf16[256,1024]{1,0:T(8,128)(2,1)S(1)}, bf16[256,1024]{1,0:T(8,128)(2,1)S(1)}, u32[]{:S(2)}, u32[]{:S(2)}) collective-permute-start(bf16[256,1024]{1,0:T(8,128)(2,1)S(1)} %add_convert_fusion), channel_id=1, source_target_pairs={{0,16},{8,24},{16,0},{24,8},{1,17},{9,25},{17,1},{25,9},{2,18},{10... | collective-permute-start | bytes 1572872 | tf_op jit(solution)/shard_map/ppermute | solution.py:29
  358.5 12.3 %collective-permute-start.51 = (bf16[256,1024]{1,0:T(8,128)(2,1)S(1)}, bf16[256,1024]{1,0:T(8,128)(2,1)S(1)}, u32[]{:S(2)}, u32[]{:S(2)}) collective-permute-start(bf16[256,1024]{1,0:T(8,128)(2,1)S(1)} %get-tuple-element.260), channel_id=1, source_target_pairs={{0,8},{8,0},{16,24},{24,16},{1,9},{9,1},{17,25},{25,17},{2,10},{10... | collective-permute-start | bytes 1572872 | tf_op jit(solution)/shard_map/ppermute | solution.py:29
  358.6 32.2 %collective-permute-start.54 = (bf16[2048,256]{1,0:T(8,128)(2,1)}, bf16[2048,256]{1,0:T(8,128)(2,1)S(1)}, u32[]{:S(2)}, u32[]{:S(2)}) collective-permute-start(bf16[2048,256]{1,0:T(8,128)(2,1)} %shard_map.318), channel_id=1, source_target_pairs={{0,1},{1,0},{2,3},{3,2},{4,5},{5,4},{6,7},{7,6},{8,9},{9,8},{10,11... | collective-permute-start | bytes 3145736 | tf_op jit(solution)/shard_map/ppermute | solution.py:29
  372.9 17.9 %collective-permute-start.53 = (bf16[256,1024]{1,0:T(8,128)(2,1)}, bf16[256,1024]{1,0:T(8,128)(2,1)S(1)}, u32[]{:S(2)}, u32[]{:S(2)}) collective-permute-start(bf16[256,1024]{1,0:T(8,128)(2,1)} %get-tuple-element.266.refs_0_), channel_id=1, source_target_pairs={{0,16},{8,24},{16,0},{24,8},{1,17},{9,25},{17,1},{25,9},{2,18},{10... | collective-permute-start | bytes 1572872 | tf_op jit(solution)/shard_map/ppermute | solution.py:29
  373.1 23.9 %collective-permute-start.50 = (bf16[256,1024]{1,0:T(8,128)(2,1)}, bf16[256,1024]{1,0:T(8,128)(2,1)S(1)}, u32[]{:S(2)}, u32[]{:S(2)}) collective-permute-start(bf16[256,1024]{1,0:T(8,128)(2,1)} %reduce-scatter.3.cloned.1.call-done.refs_0_), channel_id=1, source_target_pairs={{0,16},{8,24},{16,0},{24,8},{1,17},{9,25},{17,1},{25,9},{2,18},{10... | collective-permute-start | bytes 1572872 | tf_op jit(solution)/shard_map/ppermute | solution.py:29
  374.9 26.4 %collective-permute-start.57 = (bf16[256,1024]{1,0:T(8,128)(2,1)}, bf16[256,1024]{1,0:T(8,128)(2,1)S(1)}, u32[]{:S(2)}, u32[]{:S(2)}) collective-permute-start(bf16[256,1024]{1,0:T(8,128)(2,1)} %get-tuple-element.266.refs_0_), channel_id=1, source_target_pairs={{0,8},{8,0},{16,24},{24,16},{1,9},{9,1},{17,25},{25,17},{2,10},{10... | collective-permute-start | bytes 1572872 | tf_op jit(solution)/shard_map/ppermute | solution.py:29
  374.9 22.2 %collective-permute-start.55 = (f32[8,1024]{1,0:T(8,128)S(1)}, f32[8,1024]{1,0:T(8,128)S(1)}, u32[]{:S(2)}, u32[]{:S(2)}) collective-permute-start(f32[8,1024]{1,0:T(8,128)S(1)} %pad_maximum_fusion.3.terms), channel_id=1, source_target_pairs={{0,1},{1,0},{2,3},{3,2},{4,5},{5,4},{6,7},{7,6},{8,9},{9,8},{10,11... | collective-permute-start | bytes 98312 | tf_op jit(solution)/shard_map/ppermute | solution.py:29
  390.8 11.7 %collective-permute-start.65 = (bf16[256,1024]{1,0:T(8,128)(2,1)}, bf16[256,1024]{1,0:T(8,128)(2,1)S(1)}, u32[]{:S(2)}, u32[]{:S(2)}) collective-permute-start(bf16[256,1024]{1,0:T(8,128)(2,1)} %reduce-scatter.3.cloned.1.call-done.refs_0_), channel_id=1, source_target_pairs={{0,8},{8,0},{16,24},{24,16},{1,9},{9,1},{17,25},{25,17},{2,10},{10... | collective-permute-start | bytes 1572872 | tf_op jit(solution)/shard_map/ppermute | solution.py:29
  400.7 2.6 collective-permute-start.66
  400.7 3.4 collective-permute-start.58
  401.2 17.8 %collective-permute-start.46 = (bf16[256,1024]{1,0:T(8,128)(2,1)}, bf16[256,1024]{1,0:T(8,128)(2,1)}, u32[]{:S(2)}, u32[]{:S(2)}) collective-permute-start(bf16[256,1024]{1,0:T(8,128)(2,1)} %copy-done.58), channel_id=1, source_target_pairs={{0,8},{8,0},{16,24},{24,16},{1,9},{9,1},{17,25},{25,17},{2,10},{10... | collective-permute-start | bytes 1572872 | tf_op jit(solution)/shard_map/ppermute | solution.py:29
  402.0 17.0 %collective-permute-start.56 = (bf16[256,1024]{1,0:T(8,128)(2,1)}, bf16[256,1024]{1,0:T(8,128)(2,1)}, u32[]{:S(2)}, u32[]{:S(2)}) collective-permute-start(bf16[256,1024]{1,0:T(8,128)(2,1)} %copy-done.61), channel_id=1, source_target_pairs={{0,8},{8,0},{16,24},{24,16},{1,9},{9,1},{17,25},{25,17},{2,10},{10... | collective-permute-start | bytes 1572872 | tf_op jit(solution)/shard_map/ppermute | solution.py:29
  403.3 19.2 %collective-permute-start.62 = (bf16[528,256]{1,0:T(8,128)(2,1)}, bf16[528,256]{1,0:T(8,128)(2,1)}, u32[]{:S(2)}, u32[]{:S(2)}) collective-permute-start(bf16[528,256]{1,0:T(8,128)(2,1)} %get-tuple-element.273), channel_id=1, source_target_pairs={{0,2},{1,3},{2,0},{3,1},{4,6},{5,7},{6,4},{7,5},{8,10},{9,11},{10,... | collective-permute-start | bytes 811016 | tf_op jit(solution)/shard_map/ppermute | solution.py:29
  404.1 27.7 %collective-permute-start.63 = (bf16[528,256]{1,0:T(8,128)(2,1)}, bf16[528,256]{1,0:T(8,128)(2,1)}, u32[]{:S(2)}, u32[]{:S(2)}) collective-permute-start(bf16[528,256]{1,0:T(8,128)(2,1)} %get-tuple-element.278), channel_id=1, source_target_pairs={{0,4},{1,5},{2,6},{3,7},{4,0},{5,1},{6,2},{7,3},{8,12},{9,13},{10,... | collective-permute-start | bytes 811016 | tf_op jit(solution)/shard_map/ppermute | solution.py:29
  404.9 26.9 %collective-permute-start.64 = (bf16[528,256]{1,0:T(8,128)(2,1)S(1)}, bf16[528,256]{1,0:T(8,128)(2,1)}, u32[]{:S(2)}, u32[]{:S(2)}) collective-permute-start(bf16[528,256]{1,0:T(8,128)(2,1)S(1)} %get-tuple-element.279), channel_id=1, source_target_pairs={{0,6},{1,7},{2,4},{3,5},{4,2},{5,3},{6,0},{7,1},{8,14},{9,15},{10,... | collective-permute-start | bytes 811016 | tf_op jit(solution)/shard_map/ppermute | solution.py:29
  418.9 21.5 %collective-permute-start.60 = (bf16[128,1024]{1,0:T(8,128)(2,1)}, bf16[128,1024]{1,0:T(8,128)(2,1)S(1)}, u32[]{:S(2)}, u32[]{:S(2)}) collective-permute-start(bf16[128,1024]{1,0:T(8,128)(2,1)} %get-tuple-element.235), channel_id=1, source_target_pairs={{0,8},{8,0},{16,24},{24,16},{1,9},{9,1},{17,25},{25,17},{2,10},{10... | collective-permute-start | bytes 786440 | tf_op jit(solution)/shard_map/ppermute | solution.py:29
  419.0 41.4 %collective-permute-start.59 = (bf16[128,1024]{1,0:T(8,128)(2,1)}, bf16[128,1024]{1,0:T(8,128)(2,1)S(1)}, u32[]{:S(2)}, u32[]{:S(2)}) collective-permute-start(bf16[128,1024]{1,0:T(8,128)(2,1)} %get-tuple-element.233), channel_id=1, source_target_pairs={{0,8},{8,0},{16,24},{24,16},{1,9},{9,1},{17,25},{25,17},{2,10},{10... | collective-permute-start | bytes 786440 | tf_op jit(solution)/shard_map/ppermute | solution.py:29
  438.7 5.3 %collective-permute-start.76 = (bf16[128,256]{1,0:T(8,128)(2,1)S(1)}, bf16[128,256]{1,0:T(8,128)(2,1)S(1)}, u32[]{:S(2)}, u32[]{:S(2)}) collective-permute-start(bf16[128,256]{1,0:T(8,128)(2,1)S(1)} %slice.28), channel_id=1, source_target_pairs={{0,1},{1,0},{2,3},{3,2},{4,5},{5,4},{6,7},{7,6},{8,9},{9,8},{10,11... | collective-permute-start | bytes 196616 | tf_op jit(solution)/shard_map/ppermute | solution.py:29
  440.5 20.0 %collective-permute-start.61 = (bf16[128,1024]{1,0:T(8,128)(2,1)S(1)}, bf16[128,1024]{1,0:T(8,128)(2,1)S(1)}, u32[]{:S(2)}, u32[]{:S(2)}) collective-permute-start(bf16[128,1024]{1,0:T(8,128)(2,1)S(1)} %add_convert_fusion.7), channel_id=1, source_target_pairs={{0,16},{8,24},{16,0},{24,8},{1,17},{9,25},{17,1},{25,9},{2,18},{10... | collective-permute-start | bytes 786440 | tf_op jit(solution)/shard_map/ppermute | solution.py:29
  441.7 19.3 %collective-permute-start.74 = (bf16[384,256]{1,0:T(8,128)(2,1)S(1)}, bf16[384,256]{1,0:T(8,128)(2,1)S(1)}, u32[]{:S(2)}, u32[]{:S(2)}) collective-permute-start(bf16[384,256]{1,0:T(8,128)(2,1)S(1)} %slice.27.refs_0_), channel_id=1, source_target_pairs={{0,16},{8,24},{16,0},{24,8},{1,17},{9,25},{17,1},{25,9},{2,18},{10... | collective-permute-start | bytes 589832 | tf_op jit(solution)/shard_map/ppermute | solution.py:29
  443.7 4.3 collective-permute-start.70
  444.0 10.7 %collective-permute-start.77 = (bf16[256,256]{1,0:T(8,128)(2,1)S(1)}, bf16[256,256]{1,0:T(8,128)(2,1)S(1)}, u32[]{:S(2)}, u32[]{:S(2)}) collective-permute-start(bf16[256,256]{1,0:T(8,128)(2,1)S(1)} %pad_maximum_fusion.2), channel_id=1, source_target_pairs={{0,16},{8,24},{16,0},{24,8},{1,17},{9,25},{17,1},{25,9},{2,18},{10... | collective-permute-start | bytes 393224 | tf_op jit(solution)/shard_map/ppermute | solution.py:29
  447.9 13.2 %collective-permute-start.73 = (bf16[384,256]{1,0:T(8,128)(2,1)S(1)}, bf16[384,256]{1,0:T(8,128)(2,1)S(1)}, u32[]{:S(2)}, u32[]{:S(2)}) collective-permute-start(bf16[384,256]{1,0:T(8,128)(2,1)S(1)} %slice.27.refs_0_), channel_id=1, source_target_pairs={{0,8},{8,0},{16,24},{24,16},{1,9},{9,1},{17,25},{25,17},{2,10},{10... | collective-permute-start | bytes 589832 | tf_op jit(solution)/shard_map/ppermute | solution.py:29
  454.7 5.6 %collective-permute-start.71 = (bf16[256,256]{1,0:T(8,128)(2,1)S(1)}, bf16[256,256]{1,0:T(8,128)(2,1)S(1)}, u32[]{:S(2)}, u32[]{:S(2)}) collective-permute-start(bf16[256,256]{1,0:T(8,128)(2,1)S(1)} %pad_maximum_fusion.1), channel_id=1, source_target_pairs={{0,16},{8,24},{16,0},{24,8},{1,17},{9,25},{17,1},{25,9},{2,18},{10... | collective-permute-start | bytes 393224 | tf_op jit(solution)/shard_map/ppermute | solution.py:29
  460.3 5.8 %collective-permute-start.68 = (bf16[400,256]{1,0:T(8,128)(2,1)S(1)}, bf16[400,256]{1,0:T(8,128)(2,1)S(1)}, u32[]{:S(2)}, u32[]{:S(2)}) collective-permute-start(bf16[400,256]{1,0:T(8,128)(2,1)S(1)} %pad_maximum_fusion.refs_0_), channel_id=1, source_target_pairs={{0,16},{8,24},{16,0},{24,8},{1,17},{9,25},{17,1},{25,9},{2,18},{10... | collective-permute-start | bytes 614408 | tf_op jit(solution)/shard_map/ppermute | solution.py:29
  460.5 8.4 %collective-permute-start.67 = (bf16[400,256]{1,0:T(8,128)(2,1)S(1)}, bf16[400,256]{1,0:T(8,128)(2,1)S(1)}, u32[]{:S(2)}, u32[]{:S(2)}) collective-permute-start(bf16[400,256]{1,0:T(8,128)(2,1)S(1)} %pad_maximum_fusion.refs_0_), channel_id=1, source_target_pairs={{0,8},{8,0},{16,24},{24,16},{1,9},{9,1},{17,25},{25,17},{2,10},{10... | collective-permute-start | bytes 614408 | tf_op jit(solution)/shard_map/ppermute | solution.py:29
  460.5 6.4 %collective-permute-start.78 = (bf16[256,256]{1,0:T(8,128)(2,1)S(1)}, bf16[256,256]{1,0:T(8,128)(2,1)S(1)}, u32[]{:S(2)}, u32[]{:S(2)}) collective-permute-start(bf16[256,256]{1,0:T(8,128)(2,1)S(1)} %broadcast_select_fusion.refs_4_), channel_id=1, source_target_pairs={{0,8},{8,0},{16,24},{24,16},{1,9},{9,1},{17,25},{25,17},{2,10},{10... | collective-permute-start | bytes 393224 | tf_op jit(solution)/shard_map/ppermute | solution.py:29
  461.0 7.8 %collective-permute-start.72 = (bf16[256,256]{1,0:T(8,128)(2,1)S(1)}, bf16[256,256]{1,0:T(8,128)(2,1)S(1)}, u32[]{:S(2)}, u32[]{:S(2)}) collective-permute-start(bf16[256,256]{1,0:T(8,128)(2,1)S(1)} %broadcast_select_fusion.1.refs_4_), channel_id=1, source_target_pairs={{0,8},{8,0},{16,24},{24,16},{1,9},{9,1},{17,25},{25,17},{2,10},{10... | collective-permute-start | bytes 393224 | tf_op jit(solution)/shard_map/ppermute | solution.py:29
  461.1 5.8 %collective-permute-start.75 = (bf16[384,256]{1,0:T(8,128)(2,1)S(1)}, bf16[384,256]{1,0:T(8,128)(2,1)S(1)}, u32[]{:S(2)}, u32[]{:S(2)}) collective-permute-start(bf16[384,256]{1,0:T(8,128)(2,1)S(1)} %collective-permute-done.74.refs_2_), channel_id=1, source_target_pairs={{0,8},{8,0},{16,24},{24,16},{1,9},{9,1},{17,25},{25,17},{2,10},{10... | collective-permute-start | bytes 589832 | tf_op jit(solution)/shard_map/ppermute | solution.py:29
  466.0 2.8 collective-permute-start.69
  (133 other events, 800.9 us)
Sparse Core Ops, SparseCore 0:
  20.0 75.2 all-gather.2
  98.0 72.4 all-gather.4
  265.6 85.9 reduce-scatter.2
  355.4 82.4 reduce-scatter.4
where the time goes:
time: 484 us; the launch traced here: 479 us
  waiting for transfers between devices  225 us (46%)
  Pallas kernels  132 us (27%)
  local copies, waits for them, and re-layouts  57.3 us (12%)
  starting transfers between devices  42.4 us (9%)
  between operations  15.2 us (3%)
  other arithmetic  6.92 us (1%)
    ppermute x79, waiting for transfers between devices, swap(): return lax.ppermute(value, axis, [(i, i ^ bit) for i in range(size)])  220 us
    pallas_call x39, Pallas kernels, call(): pl.pallas_call(kernel, in_specs=specs, out_specs=[pl.BlockSpec(memory_spa...  132 us
    unnamed x231, local copies, waits for them, and re-layouts  53.6 us
    ppermute x79, starting transfers between devices, swap(): return lax.ppermute(value, axis, [(i, i ^ bit) for i in range(size)])  42.2 us
  transfers between devices with their start and end apart: 83, of which 43 were waited for; matrix products, arithmetic and copies ran while one was open for 2% of the time, Pallas kernels for 23%

commit v1 on v0

--- a/solution.py
+++ b/solution.py
@@ -645,14 +645,20 @@
 
 
 def unsort_kernel(order_ref, *refs, size):
-    sources, out_ref = refs[:size], refs[size]
-    slots = sources[0].shape[0]
+    count = len(refs) - 1 if len(refs) % size == 1 else len(refs) - 2
+    sources, out_ref = refs[:count], refs[count]
+    slots = out_ref.shape[0]
+    pieces = count // size
+    length = slots // pieces
     mine = lax.axis_index("ctx")
     total = jnp.zeros(out_ref.shape, F32)
-    for source in range(size):
-        place = (mine ^ source) * slots + lax.broadcasted_iota(jnp.int32, (slots, slots), 1)
-        total += dot(one_hot(order_ref[...] == place), sources[source][...])
+    for index, source in enumerate(sources):
+        first = (mine ^ (index // pieces)) * slots + (index % pieces) * length
+        place = first + lax.broadcasted_iota(jnp.int32, (slots, length), 1)
+        total += dot(one_hot(order_ref[...] == place), source[:length, :])
     out_ref[...] = total
+    if count + 1 < len(refs):
+        refs[count + 1][...] = sum(source[slots:, :].astype(F32) for source in sources)
 
 
 def wsh_rows(index, rows):
@@ -875,10 +881,22 @@
     terms_ref[1:2, :] = shift[None]
 
 
+def norm_first_kernel(norms, value_ref, grad_ref, near, other, far, one, two, three, sent_ref):
+    slots = value_ref.shape[0]
+    hat, rate = norm_parts(value_ref[...])
+    grad = near[...].astype(F32) + other[...].astype(F32) + far[...].astype(F32)
+    change, gain, shift = norm_back(hat, rate, norms[0:1, :], grad)
+    sent_ref[:slots, :] = (grad_ref[...] + change).astype(BF)
+    sums = [gain[None], shift[None], one[...], two[...], three[...], jnp.zeros((8, gain.shape[0]), F32)]
+    sent_ref[slots:, :] = jnp.concatenate(sums, 0).astype(BF)
+
+
 def norm_turn_kernel(norms, base, outside, *refs):
-    parts, (result_ref, out_ref, sent_ref, terms_ref) = refs[:-4], refs[-4:]
+    parts, (low_ref, high_ref, out_ref, sent_ref, terms_ref) = refs[:-5], refs[-5:]
     hat, rate = norm_parts(total_of(base, parts))
-    result_ref[...] = (hat * norms[3:4, :] + norms[7:8, :]).astype(BF)
+    result = (hat * norms[3:4, :] + norms[7:8, :]).astype(BF)
+    low_ref[...] = result[: low_ref.shape[0]]
+    high_ref[...] = result[low_ref.shape[0] :]
     change, gain, shift = norm_back(hat, rate, norms[3:4, :], outside[...])
     out_ref[...] = change
     sent_ref[...] = change.astype(BF)
@@ -946,17 +964,12 @@
 
 
 def weight_grad_kernel(*refs, terms, odd, rows, piece, count):
-    send = None
-    if odd is None:
-        *refs, send = refs
-    operands, extra, out_ref = refs[:-2], refs[-2], refs[-1]
-    height = out_ref.shape[0] // count
-    cols = out_ref.shape[1]
+    operands, extra, outs, held = refs[: -count - 2], refs[-count - 2], refs[-count - 1 : -1], refs[-1]
+    height, cols = outs[0].shape
     mine = lax.axis_index("wsh")
 
     def step(index, carry):
-        relative = index ^ mine if odd is None else 2 * index + odd
-        target = mine ^ relative
+        target = mine ^ (2 * index + odd)
         lanes = pl.ds(pl.multiple_of(target * rows, rows), rows)
         for part in range(3):
             value = None
@@ -967,31 +980,16 @@
                         operands[right][right_at : right_at + length, :].astype(BF),
                     )
                     value = one if value is None else value + one
-            at = pl.ds(pl.multiple_of(index * height + part * rows, rows), rows)
-            out_ref[at, :] = value.astype(out_ref.dtype)
-        taken = piece_rows(relative, piece)
+            held[index, part * rows : (part + 1) * rows, :] = value.astype(held.dtype)
+        taken = piece_rows(2 * index + odd, piece)
         for chunk in range(extra.shape[1] // cols):
-            at = pl.ds(pl.multiple_of(index * height + 3 * rows + chunk * piece, piece), piece)
-            out_ref[at, :] = extra[taken, chunk * cols : (chunk + 1) * cols].astype(out_ref.dtype)
-        if send is not None:
-            send(index)
+            at = 3 * rows + chunk * piece
+            held[index, at : at + piece, :] = extra[taken, chunk * cols : (chunk + 1) * cols].astype(held.dtype)
         return carry
 
     lax.fori_loop(0, count, step, 0)
-
-
-def sum_kernel(even, odd, terms, other_terms, *outs, rows, height):
-    total = terms[...] + other_terms[...]
     for index, out in enumerate(outs):
-        at = slice(index * height, (index + 1) * height)
-        out[:height, :] = (even[at, :] + odd[at, :].astype(F32)).astype(out.dtype)
-        lanes = (lax.axis_index("wsh") ^ (2 * index)) * rows
-        taken = jnp.zeros((8, rows), F32)
-        for block in range(total.shape[1] // rows):
-            taken = jnp.where(lanes == block * rows, total[:, block * rows : (block + 1) * rows], taken)
-        taken = jnp.concatenate([taken, jnp.zeros((8, rows), F32)], 0)
-        taken = jnp.concatenate([taken, jnp.zeros((16, out.shape[1] - rows), F32)], 1)
-        out[height:, :] = taken.astype(out.dtype)
+        out[...] = held[index]
 
 
 def back_project_kernel(dq_ref, dk_ref, dv_ref, wq, wk, wv, *outs, first):
@@ -1017,9 +1015,6 @@
     mine = lax.axis_index("ctx")
     threes, (near, other), outs = refs[:count], refs[count : count + 2], refs[count + 2 :]
     cols = threes[0].shape[1]
-    if len(outs) > 4:
-        last = [three[3 * rows :, :rows].astype(F32) for three in threes]
-        outs[4][...] = sum(last)
     span = HEAD * count
     blocks = [three[...].astype(F32) for three in threes]
     for group in range(count):
@@ -1199,7 +1194,10 @@
     half = total // 512
 
     def unsort(blocks):
-        return call(functools.partial(unsort_kernel, size=size), [block_f], (), own_order, *blocks)[0]
+        outs = [block_f]
+        if blocks[0].shape[0] > slots:
+            outs.append(((blocks[0].shape[0] - slots, width), F32))
+        return call(functools.partial(unsort_kernel, size=size), outs, (), own_order, *blocks)
 
     hat_all, tokens = call(
         functools.partial(sort_kernel, size=size), [((total, width), F32), block_f], (), order, *token_blocks
@@ -1302,9 +1300,9 @@
     normed_three = finish_ctx(normed_three, near[0])
     hidden_high, slope_high, *far = feed_forward(1)
     sent, arrived = far_hop(far)
-    result, grad_ffn, grad, terms_three = call(
+    result_low, result_high, grad_ffn, grad, terms_three = call(
         norm_turn_kernel,
-        [block_bf, block_f, block_bf, terms_f],
+        [((slots // 2, width), BF)] * 2 + [block_f, block_bf, terms_f],
         (),
         norms,
         after_cross,
@@ -1358,13 +1356,15 @@
     feed_grads = scatter_wsh(after(feed_grads, arrived).reshape(groups * 2 * rows, width))
 
     def weight_grads(terms, operands, out_grad, odd):
-        height = 3 * rows + piece * (width // cols)
-        count = groups if odd is None else groups // 2
+        count = groups // 2
+        kind = BF if odd else F32
         body = functools.partial(weight_grad_kernel, terms=terms, odd=odd, rows=rows, piece=piece, count=count)
-        outs = [((count * height, cols), F32 if odd == 0 else BF)]
-        if odd is None:
-            return call_streaming(body, outs[0], count, *operands, out_grad)
-        return call(body, outs, (), *operands, out_grad)[0]
+        outs = [((height, cols), kind)] * count
+        return call(body, outs, (), *operands, out_grad, scratch=[pltpu.VMEM((count, height, cols), kind)])
+
+    def pass_z(even, odd, index):
+        value = (even[index] + odd[index].astype(F32)).astype(BF)
+        return swap(value, "wsh", 2 * index)
 
     def backward(span, side, own_queries, sources, queries, mixed, lse, keys, values, wo, wq, before):
         body = functools.partial(
@@ -1400,10 +1400,11 @@
         cross_range, 0, True, grad_in[:part], *cross_low[:3], enc_keys, enc_values, co, cq, None
     )
     grad_in = finish_ctx(grad_in, low[4])
+    result_low = start_ctx(after(result_low, grad_in[2]))
     high = backward(
         cross_range, 1, True, grad_in[part:], *cross_high[:3], enc_keys, enc_values, co, cq, list(low[1:4])
     )
-    sent, arrived = far_hop(high[4:])
+    sent, arrived = far_hop([high[4], after(high[5], result_low[2])])
     dk, dv, dwo = high[1:4]
     operands = [*normed_two, low[0], high[0], *encoder, dk, dv]
     terms = []
@@ -1415,18 +1416,21 @@
             terms.append((which, size + 2 + index, 0, 2 * size + 1 + which, index * enc_slots, enc_slots))
     dk = after(dk, sent)
     operands[-2] = dk
-    cross_share_local = weight_grads(tuple(terms), operands, dwo, None)
+    odd = weight_grads(tuple(terms), operands, dwo, 1)
+    cross_even = weight_grads(tuple(terms), operands, dwo, 0)
     enc_parts = call(encoder_grad_kernel, [((enc_slots, width), BF)] * size, (), dk, dv, ck, cv)
-    cross_share = scatter_wsh(after(cross_share_local, arrived))
-    arrived = after(arrived, cross_share_local, *enc_parts)
+    cross_odd = [swap(block, "wsh", 1) for block in odd]
+    cross_far = pass_z(cross_even, cross_odd, 3)
+    arrived = after(arrived, cross_even[0], cross_odd[3], *enc_parts)
     grad_self, grad, terms_one = denormalize(after_self, grad_cross, low[4:], arrived, 1)
 
     grad_in = start_ctx(grad)
     low = backward(
         self_range, 0, False, grad_in[:part], queries, mixed_low, lse_low, keys, values, wo, None, None
     )
-    grad_in = finish_ctx(grad_in, low[0])
-    result = start_ctx(after(result, grad_in[2]))
+    grad_in = finish_ctx(grad_in, low[0], cross_odd[2])
+    cross_middle = pass_z(cross_even, cross_odd, 2)
+    result_high = start_ctx(after(result_high, grad_in[2]))
     enc_sent, enc_far = far_hop([after(enc_parts[2], grad_in[2]), enc_parts[3]])
     enc_near = swap(enc_parts[1], "ctx", 1)
     enc_grad = enc_parts[0].astype(F32) + enc_near.astype(F32) + enc_far.astype(F32)
@@ -1439,64 +1443,73 @@
         body = functools.partial(back_project_kernel, first=side * middle)
         return call(body, [block_bf] * part, (), dq, dk, dv, wq, wk, wv)
 
-    far = back_project(1, high[0])
-    operands = [normed_one, low[0], high[0], after(dk, result[2]), dv]
+    far = back_project(1, after(high[0], cross_odd[1], cross_far))
+    cross_near = pass_z(cross_even, cross_odd, 1)
+    operands = [normed_one, low[0], high[0], after(dk, result_high[2]), dv]
     terms = ((0, 0, 0, 1, 0, middle), (0, 0, middle, 2, 0, middle), (1, 0, 0, 3, 0, total), (2, 0, 0, 4, 0, total))
     odd = weight_grads(terms, operands, dwo, 1)
     sent, arrived = far_hop(far)
-    self_odd = swap(odd, "wsh", 1)
-    near = back_project(0, after(low[0], sent, odd))
+    self_odd = [swap(block, "wsh", 1) for block in odd]
+    near = back_project(0, after(low[0], sent, odd[0]))
     self_even = weight_grads(terms, operands, after(dwo, *near), 0)
+    self_far = pass_z(self_even, self_odd, 3)
 
     feed_blocks = start_ctx(after(feed_grads, sent))
-    unused, grad, terms_zero = denormalize(tokens, grad_self, near, after(arrived, self_even), 0)
+    grad = call(
+        norm_first_kernel,
+        [((slots + 16, width), BF)],
+        (),
+        norms,
+        tokens,
+        grad_self,
+        near[0],
+        swap(near[1], "ctx", 1),
+        after(arrived, self_even[0]),
+        terms_one,
+        terms_two,
+        terms_three,
+    )[0]
     input_grad = start_ctx(grad)
 
-    def finish(result, extra=0):
-        fourth = result[3 * rows : height]
+    def finish(even, odd, *parts):
+        share = even[0] + odd[0].astype(F32)
+        for value in parts:
+            share = share + value.astype(F32)
+        share = share.astype(BF)
+        three, fourth = share[: 3 * rows], share[3 * rows :]
         pair = jnp.concatenate([fourth, swap(fourth, "wsh", 1)], 0)
         pair = jnp.where(row % 2 == mine // 2, pair, swap(pair, "ctx", 2))
-        three = result[: 3 * rows]
-        outs = [((rows, width), F32)] * 4
-        if extra:
-            three = jnp.concatenate([three, result[height:]], 0)
-            outs.append(((extra, rows), F32))
         return call(
             functools.partial(place_square_kernel, count=size, rows=rows, piece=piece),
-            outs,
+            [((rows, width), F32)] * 4,
             (),
             *spread_ctx(three),
             pair,
             swap(pair, "ctx", 1),
         )
 
-    terms = jnp.concatenate([terms_zero, terms_one, terms_two, terms_three], 0)
-    tall = (height + 16, cols)
-    share, *sent = call(
-        functools.partial(sum_kernel, rows=rows, height=height),
-        [(tall, F32)] + [(tall, BF)] * (groups // 2 - 1),
-        (),
-        after(self_even, feed_blocks[2], input_grad[2]),
-        after(self_odd, grad),
-        terms,
-        swap(terms, "wsh", 1),
-    )
-    parts = [swap(value, "wsh", 2 * index + 2) for index, value in enumerate(sent)]
+    result_low = finish_ctx(result_low, self_odd[3], grad)
+    result_high = finish_ctx(result_high)
+    result = unsort([half for pair in zip(result_low, result_high) for half in pair])[0]
+    self_middle = pass_z(self_even, self_odd, 2)
+    self_near = pass_z(self_even, self_odd, 1)
     feed_in_grad, feed_out_grad = call(
         functools.partial(place_feed_kernel, count=size, groups=groups, rows=rows, cols=ff_rows),
         [((rows, groups * size * ff_rows), F32), ((size * ff_rows, width), F32)],
         (),
-        *finish_ctx(feed_blocks, sent[0]),
-    )
-    result = unsort(finish_ctx(result, sent[0]))
-    input_grad = unsort(finish_ctx(input_grad, sent[0]))
-    parts = after(tuple(parts), result, input_grad, feed_in_grad)
-    for part in parts:
-        share = share + part.astype(F32)
-    share = share.astype(BF)
-    *self_grads, terms = finish(share, 16)
-    terms = jnp.transpose(terms[:8])
-    cross_grads = finish(after(cross_share, share))
+        *finish_ctx(feed_blocks, self_odd[2], result, cross_near),
+    )
+    input_grad, terms = unsort(finish_ctx(input_grad, self_odd[1], self_far, feed_in_grad))
+    terms = terms[:8]
+    terms = terms + swap(terms, "wsh", 1)
+    pieces = [lax.dynamic_slice_in_dim(terms, (row ^ bit) * rows, rows, 1) for bit in range(0, groups, 2)]
+    terms = pieces[0]
+    for index in range(1, groups // 2):
+        terms = terms + swap(pieces[index], "wsh", 2 * index)
+    terms = jnp.transpose(terms)
+    cross_odd[0] = after(cross_odd[0], input_grad, self_middle, self_near)
+    cross_grads = finish(cross_even, cross_odd, cross_near, cross_middle, cross_far)
+    self_grads = finish(self_even, self_odd, self_near, self_middle, self_far)
     return (
         result[None],
         input_grad[None],

time: 484 us -> 461 us (0.952)
  starting transfers between devices: 42.4 us -> 97.9 us
  waiting for transfers between devices: 225 us -> 175 us
  Pallas kernels: 132 us -> 110 us
  local copies, waits for them, and re-layouts: 57.3 us -> 41.4 us
  other arithmetic: 6.92 us -> 12.6 us
    ppermute x79 -> x95, starting transfers between devices: 42.2 us -> 97.8 us  [swap(): return lax.ppermute(value, axis, [(i, i ^ bit) for i in range(size)])]
    ppermute x79 -> x95, waiting for transfers between devices: 220 us -> 173 us  [swap(): return lax.ppermute(value, axis, [(i, i ^ bit) for i in range(size)])]
    pallas_call x39, Pallas kernels: 132 us -> 110 us  [call(): pl.pallas_call(kernel, in_specs=specs, out_specs=[pl.BlockSpec(memory_spa...]
    unnamed x231 -> x195, local copies, waits for them, and re-layouts: 53.6 us -> 39.4 us
    convert_element_type x1 -> x8, other arithmetic: 1.24 us -> 8.5 us  [the longest x6 6.07 us: pass_z(): value = (even[index] + odd[index].astype(F32)).astype(BF)]
  transfers between devices with their start and end apart: 83 -> 98, of which waited for: 43 -> 45; matrix products, arithmetic and copies ran while one was open for 2% -> 3% of each run, Pallas kernels for 23% -> 22%
where the time goes in v1:
time: 461 us; the launch traced here: 453 us
  waiting for transfers between devices  175 us (38%)
  Pallas kernels  110 us (24%)
  starting transfers between devices  97.9 us (21%)
  local copies, waits for them, and re-layouts  41.4 us (9%)
  between operations  15.5 us (3%)
  other arithmetic  12.6 us (3%)
    ppermute x95, waiting for transfers between devices, swap(): return lax.ppermute(value, axis, [(i, i ^ bit) for i in range(size)])  173 us
    pallas_call x39, Pallas kernels, call(): pl.pallas_call(kernel, in_specs=specs, out_specs=[pl.BlockSpec(memory_spa...  110 us
    ppermute x95, starting transfers between devices, swap(): return lax.ppermute(value, axis, [(i, i ^ bit) for i in range(size)])  97.8 us
    unnamed x195, local copies, waits for them, and re-layouts  39.4 us
  transfers between devices with their start and end apart: 98, of which 45 were waited for; matrix products, arithmetic and copies ran while one was open for 3% of the time, Pallas kernels for 22%

profile of v1, /device:TPU:0, one launch (start us, length us, event | category | flops | bytes accessed | tf_op | source)
XLA Modules:
  0.0 452.5 jit_solution(11159922669898115954)
XLA Ops:
  8.3 3.0 collective-permute-start.3
  11.3 3.5 collective-permute-done.3.refs_4_
  17.3 2.5 shard_map.296
  19.8 1.9 collective-permute-start.5
  21.7 2.4 shard_map.302
  24.1 3.4 collective-permute-done.5.refs_2_
  31.3 3.6 collective-permute-start.9
  35.1 4.8 %collective-permute-done.1.refs_2_ = bf16[256,1024]{1,0:T(8,128)(2,1)S(1)} collective-permute-done((bf16[256,1024]{1,0:T(8,128)(2,1)S(1)}, bf16[256,1024]{1,0:T(8,128)(2,1)S(1)}, u32[]{:S(2)}, u32[]{:S(2)}) %collective-permute-start.1) | collective-permute-done | bytes 524320 | tf_op jit(solution)/shard_map/ppermute | solution.py:29
  41.3 6.3 %collective-permute-done.9.refs_6_ = bf16[528,256]{1,0:T(8,128)(2,1)S(1)} collective-permute-done((bf16[528,256]{1,0:T(8,128)(2,1)S(1)}, bf16[528,256]{1,0:T(8,128)(2,1)S(1)}, u32[]{:S(2)}, u32[]{:S(2)}) %collective-permute-start.9) | collective-permute-done | bytes 270368 | tf_op jit(solution)/shard_map/ppermute | solution.py:29
  49.2 16.1 %collective-permute-done.7.refs_4_ = bf16[528,256]{1,0:T(8,128)(2,1)S(1)} collective-permute-done((bf16[528,256]{1,0:T(8,128)(2,1)S(1)}, bf16[528,256]{1,0:T(8,128)(2,1)S(1)}, u32[]{:S(2)}, u32[]{:S(2)}) %collective-permute-start.7) | collective-permute-done | bytes 270368 | tf_op jit(solution)/shard_map/ppermute | solution.py:29
  67.4 4.1 shard_map.289
  71.6 8.8 %collective-permute-done.10.refs_7_ = bf16[528,256]{1,0:T(8,128)(2,1)S(1)} collective-permute-done((bf16[528,256]{1,0:T(8,128)(2,1)S(1)}, bf16[528,256]{1,0:T(8,128)(2,1)S(1)}, u32[]{:S(2)}, u32[]{:S(2)}) %collective-permute-start.10) | collective-permute-done | bytes 270368 | tf_op jit(solution)/shard_map/ppermute | solution.py:29
  80.4 6.1 %collective-permute-done.8.refs_5_ = bf16[528,256]{1,0:T(8,128)(2,1)S(1)} collective-permute-done((bf16[528,256]{1,0:T(8,128)(2,1)S(1)}, bf16[528,256]{1,0:T(8,128)(2,1)S(1)}, u32[]{:S(2)}, u32[]{:S(2)}) %collective-permute-start.8) | collective-permute-done | bytes 270368 | tf_op jit(solution)/shard_map/ppermute | solution.py:29
  87.4 2.5 shard_map.292
  90.0 4.9 %shard_map.293 = (bf16[512,256]{1,0:T(8,128)(2,1)S(1)}, f32[2,1,1024]{2,1,0:T(1,128)S(1)}, bf16[256,1024]{1,0:T(8,128)(2,1)S(1)}, bf16[256,1024]{1,0:T(8,128)(2,1)S(1)}) custom-call(s32[9]{0:T(128)S(1)} %pad_add_fusion.2.meta, bf16[1024,256]{1,0:T(8,128)(2,1)S(1)} %get-tuple-element.174.refs_0_.refs_2_, ...), custom_call_target="tpu_custom_call" | custom-call | flops 1048576 | bytes 65536 | tf_op jit(solution)/shard_map/pallas_call | solution.py:496
  95.6 1.9 collective-permute-done.11
  97.7 3.5 shard_map.294
  104.1 12.7 %collective-permute-done.13.refs_2_ = bf16[256,1024]{1,0:T(8,128)(2,1)S(1)} collective-permute-done((bf16[256,1024]{1,0:T(8,128)(2,1)S(1)}, bf16[256,1024]{1,0:T(8,128)(2,1)S(1)}, u32[]{:S(2)}, u32[]{:S(2)}) %collective-permute-start.13) | collective-permute-done | bytes 524320 | tf_op jit(solution)/shard_map/ppermute | solution.py:29
  131.9 3.6 shard_map.298
  139.2 6.0 %shard_map.299 = (bf16[512,256]{1,0:T(8,128)(2,1)S(1)}, bf16[512,256]{1,0:T(8,128)(2,1)S(1)}, f32[2,1,1024]{2,1,0:T(1,128)S(1)}, bf16[256,1024]{1,0:T(8,128)(2,1)S(1)}, bf16[256,1024]{1,0:T(8,128)(2,1)S(1)}) custom-call(s32[9]{0:T(128)S(1)} %pad_add_fusion.3.meta, bf16[256,1024]{1,0:T(8,128)(2,1)} %collective-permute-done.19.refs_0_.refs_2_, ...), custom_call_target="tpu_custom_call" | custom-call | flops 1048576 | bytes 65536 | tf_op jit(solution)/shard_map/pallas_call | solution.py:496
  150.4 12.7 %collective-permute-done.22.refs_2_ = bf16[256,1024]{1,0:T(8,128)(2,1)S(1)} collective-permute-done((bf16[256,1024]{1,0:T(8,128)(2,1)S(1)}, bf16[256,1024]{1,0:T(8,128)(2,1)S(1)}, u32[]{:S(2)}, u32[]{:S(2)}) %collective-permute-start.22) | collective-permute-done | bytes 524320 | tf_op jit(solution)/shard_map/ppermute | solution.py:29
  168.3 2.1 all-gather.5.cloned.1.call-done
  170.4 2.2 copy-done
  173.6 4.5 shard_map.303
  178.1 1.9 collective-permute-done.28.refs_0_.refs_2_
  182.2 4.3 shard_map.304
  187.1 7.3 %collective-permute-done.24.refs_2_ = bf16[256,1024]{1,0:T(8,128)(2,1)S(1)} collective-permute-done((bf16[256,1024]{1,0:T(8,128)(2,1)S(1)}, bf16[256,1024]{1,0:T(8,128)(2,1)S(1)}, u32[]{:S(2)}, u32[]{:S(2)}) %collective-permute-start.24) | collective-permute-done | bytes 524320 | tf_op jit(solution)/shard_map/ppermute | solution.py:29
  197.4 11.6 %collective-permute-done.31.refs_2_ = bf16[256,1024]{1,0:T(8,128)(2,1)S(1)} collective-permute-done((bf16[256,1024]{1,0:T(8,128)(2,1)S(1)}, bf16[256,1024]{1,0:T(8,128)(2,1)S(1)}, u32[]{:S(2)}, u32[]{:S(2)}) %collective-permute-start.31) | collective-permute-done | bytes 524320 | tf_op jit(solution)/shard_map/ppermute | solution.py:29
  212.3 2.4 shard_map.306
  215.5 9.2 %collective-permute-done.34.refs_0_.refs_10_ = bf16[256,1024]{1,0:T(8,128)(2,1)S(1)} collective-permute-done((bf16[256,1024]{1,0:T(8,128)(2,1)S(1)}, bf16[256,1024]{1,0:T(8,128)(2,1)S(1)}, u32[]{:S(2)}, u32[]{:S(2)}) %collective-permute-start.34) | collective-permute-done | bytes 524320 | tf_op jit(solution)/shard_map/ppermute | solution.py:29
  224.7 1.9 collective-permute-done.35.refs_1_.refs_11_
  226.6 2.6 shard_map.307
  232.9 6.8 %shard_map.308 = bf16[8,256,1024]{2,1,0:T(8,128)(2,1)S(1)} custom-call(bf16[256,1024]{1,0:T(8,128)(2,1)} %get-tuple-element.193.refs_0_, bf16[256,1024]{1,0:T(8,128)(2,1)S(1)} %copy-done.37, bf16[256,1024]{1,0:T(8,128)(2,1)} %collective-permute-done.28.refs_0_.refs_2_, bf16[256,1024]{1,0:T(8,128)(2,1)S(1)} %collective-permute-done.29.refs_1_.refs_3_, ...), custom_call_target="tpu_custom_call" | custom-call | flops 1048576 | bytes 65536 | tf_op jit(solution)/shard_map/pallas_call | solution.py:496
  239.7 2.0 copy-done.2
  241.7 3.7 collective-permute-done.37.refs_2_
  246.3 2.1 collective-permute-done.33.refs_1_
  255.9 3.7 shard_map.310
  259.6 8.7 %collective-permute-done.38.refs_0_ = bf16[256,1024]{1,0:T(8,128)(2,1)S(1)} collective-permute-done((bf16[256,1024]{1,0:T(8,128)(2,1)S(1)}, bf16[256,1024]{1,0:T(8,128)(2,1)S(1)}, u32[]{:S(2)}, u32[]{:S(2)}) %collective-permute-start.38) | collective-permute-done | bytes 524320 | tf_op jit(solution)/shard_map/ppermute | solution.py:29
  270.2 6.4 %shard_map.311 = (bf16[512,256]{1,0:T(8,128)(2,1)S(1)}, f32[512,256]{1,0:T(8,128)S(1)}, f32[512,256]{1,0:T(8,128)S(1)}, f32[256,1024]{1,0:T(8,128)S(1)}, bf16[25...) custom-call(s32[9]{0:T(128)S(1)} %pad_add_fusion.3.meta, ...), custom_call_target="tpu_custom_call", output_to_operand_aliasing={{1}: (11, {}), {2}: (12, {}), {3}: (13, {})} | custom-call | flops 1048576 | bytes 65536 | tf_op jit(solution)/shard_map/pallas_call | solution.py:496
  277.3 1.9 collective-permute-done.43
  281.0 3.3 shard_map.313
  288.7 3.5 shard_map.312
  292.2 2.8 collective-permute-done.45
  298.0 4.7 %shard_map.316 = (bf16[512,256]{1,0:T(8,128)(2,1)S(1)}, f32[1024,256]{1,0:T(8,128)S(1)}, f32[1024,256]{1,0:T(8,128)S(1)}, f32[256,1024]{1,0:T(8,128)S(1)}) custom-call(s32[9]{0:T(128)S(1)} %pad_add_fusion.2.meta, bf16[256,1024]{1,0:T(8,128)(2,1)S(1)} %get-tuple-element.251.refs_0_, bf16[256,1024]{1,0:T(8,128)(2,1)S(1)} %collective-permute-done.47.refs_1_, ...), custom_call_target="tpu_custom_call" | custom-call | flops 1048576 | bytes 65536 | tf_op jit(solution)/shard_map/pallas_call | solution.py:496
  302.7 4.4 collective-permute-done.48
  307.1 3.3 collective-permute-done.46.refs_0_
  310.5 8.8 %collective-permute-start.55 = (bf16[512,256]{1,0:T(8,128)(2,1)S(1)}, bf16[512,256]{1,0:T(8,128)(2,1)S(1)}, u32[]{:S(2)}, u32[]{:S(2)}) collective-permute-start(bf16[512,256]{1,0:T(8,128)(2,1)S(1)} %add_convert_fusion.14), channel_id=1, source_target_pairs={{0,6},{1,7},{2,4},{3,5},{4,2},{5,3},{6,0},{7,1},{8,14},{9,15},{10,... | collective-permute-start | bytes 786440 | tf_op jit(solution)/shard_map/ppermute | solution.py:29
  319.3 6.4 %shard_map.317 = (bf16[512,256]{1,0:T(8,128)(2,1)S(1)}, f32[1024,256]{1,0:T(8,128)S(1)}, f32[1024,256]{1,0:T(8,128)S(1)}, f32[256,1024]{1,0:T(8,128)S(1)}) custom-call(s32[9]{0:T(128)S(1)} %pad_add_fusion.2.meta, bf16[256,1024]{1,0:T(8,128)(2,1)S(1)} %collective-permute-done.46.refs_0_, ...), custom_call_target="tpu_custom_call", output_to_operand_aliasing={{1}: (10, {}), {2}: (11, {}), {3}: (12, {})} | custom-call | flops 1048576 | bytes 65536 | tf_op jit(solution)/shard_map/pallas_call | solution.py:496
  328.6 7.4 %collective-permute-done.52.refs_5_ = bf16[128,1024]{1,0:T(8,128)(2,1)} collective-permute-done((bf16[128,1024]{1,0:T(8,128)(2,1)S(1)}, bf16[128,1024]{1,0:T(8,128)(2,1)}, u32[]{:S(2)}, u32[]{:S(2)}) %collective-permute-start.52) | collective-permute-done | bytes 262176 | tf_op jit(solution)/shard_map/ppermute | solution.py:29
  336.0 2.6 shard_map.318
  342.9 14.8 %collective-permute-start.68 = (bf16[512,256]{1,0:T(8,128)(2,1)}, bf16[512,256]{1,0:T(8,128)(2,1)}, u32[]{:S(2)}, u32[]{:S(2)}) collective-permute-start(bf16[512,256]{1,0:T(8,128)(2,1)} %add_convert_fusion.12), channel_id=1, source_target_pairs={{0,2},{1,3},{2,0},{3,1},{4,6},{5,7},{6,4},{7,5},{8,10},{9,11},{10,... | collective-permute-start | bytes 786440 | tf_op jit(solution)/shard_map/ppermute | solution.py:29
  359.5 2.2 shard_map.321
  364.6 2.5 collective-permute-done.63
  372.3 4.3 collective-permute-start.64
  379.1 5.2 %collective-permute-start.75 = (bf16[512,256]{1,0:T(8,128)(2,1)}, bf16[512,256]{1,0:T(8,128)(2,1)}, u32[]{:S(2)}, u32[]{:S(2)}) collective-permute-start(bf16[512,256]{1,0:T(8,128)(2,1)} %add_convert_fusion.10), channel_id=1, source_target_pairs={{0,2},{1,3},{2,0},{3,1},{4,6},{5,7},{6,4},{7,5},{8,10},{9,11},{10,... | collective-permute-start | bytes 786440 | tf_op jit(solution)/shard_map/ppermute | solution.py:29
  385.0 2.8 collective-permute-start.62
  392.7 3.4 shard_map.323
  404.2 3.8 shard_map.324
  409.1 5.0 %collective-permute-done.81 = bf16[256,256]{1,0:T(8,128)(2,1)S(1)} collective-permute-done((bf16[256,256]{1,0:T(8,128)(2,1)S(1)}, bf16[256,256]{1,0:T(8,128)(2,1)S(1)}, u32[]{:S(2)}, u32[]{:S(2)}) %collective-permute-start.81) | collective-permute-done | bytes 131104 | tf_op jit(solution)/shard_map/ppermute | solution.py:29
  418.6 3.4 collective-permute-done.78.refs_2_
  423.2 2.6 collective-permute-done.73
  426.7 1.8 shard_map.326
  432.9 4.2 collective-permute-start.92
  437.1 2.9 collective-permute-start.94
  (426 shorter events, 131.2 us)
Async XLA Ops:
  7.2 116.9 %all-gather.3.cloned.1.call-start = ((), (), s32[]{:S(2)}) async-start(), calls=%async_computation.1 | async-start | bytes 2359296 | tf_op jit(solution)/shard_map/all_gather | solution.py:255
  19.8 150.6 %all-gather.5.cloned.1.call-start = ((), (), s32[]{:S(2)}) async-start(), calls=%async_computation.2 | async-start | bytes 4718592 | tf_op jit(solution)/shard_map/all_gather | solution.py:255
  19.8 7.7 %collective-permute-start.5 = (bf16[528,256]{1,0:T(8,128)(2,1)S(1)}, bf16[528,256]{1,0:T(8,128)(2,1)S(1)}, u32[]{:S(2)}, u32[]{:S(2)}) collective-permute-start(bf16[528,256]{1,0:T(8,128)(2,1)S(1)} %shard_map.291.refs_0_), channel_id=1, source_target_pairs={{0,2},{1,3},{2,0},{3,1},{4,6},{5,7},{6,4},{7,5},{8,10},{9,11},{10,... | collective-permute-start | bytes 811016 | tf_op jit(solution)/shard_map/ppermute | solution.py:29
  27.6 336.2 %reduce-scatter.2.cloned.1.call-start = ((), (), s32[]{:S(2)}) async-start(), calls=%async_computation.3 | async-start | bytes 4718592 | tf_op jit(solution)/shard_map/reduce_scatter | solution.py:259
  27.7 12.2 %collective-permute-start.1 = (bf16[256,1024]{1,0:T(8,128)(2,1)S(1)}, bf16[256,1024]{1,0:T(8,128)(2,1)S(1)}, u32[]{:S(2)}, u32[]{:S(2)}) collective-permute-start(bf16[256,1024]{1,0:T(8,128)(2,1)S(1)} %bitcast.42), channel_id=1, source_target_pairs={{0,16},{8,24},{16,0},{24,8},{1,17},{9,25},{17,1},{25,9},{2,18},{10... | collective-permute-start | bytes 1572872 | tf_op jit(solution)/shard_map/ppermute | solution.py:29
  29.1 37.7 %collective-permute-start = (bf16[256,1024]{1,0:T(8,128)(2,1)S(1)}, bf16[256,1024]{1,0:T(8,128)(2,1)S(1)}, u32[]{:S(2)}, u32[]{:S(2)}) collective-permute-start(bf16[256,1024]{1,0:T(8,128)(2,1)S(1)} %bitcast.43), channel_id=1, source_target_pairs={{0,8},{8,0},{16,24},{24,16},{1,9},{9,1},{17,25},{25,17},{2,10},{10... | collective-permute-start | bytes 1572872 | tf_op jit(solution)/shard_map/ppermute | solution.py:29
  31.3 16.4 %collective-permute-start.9 = (bf16[528,256]{1,0:T(8,128)(2,1)S(1)}, bf16[528,256]{1,0:T(8,128)(2,1)S(1)}, u32[]{:S(2)}, u32[]{:S(2)}) collective-permute-start(bf16[528,256]{1,0:T(8,128)(2,1)S(1)} %shard_map.291.refs_0_), channel_id=1, source_target_pairs={{0,6},{1,7},{2,4},{3,5},{4,2},{5,3},{6,0},{7,1},{8,14},{9,15},{10,... | collective-permute-start | bytes 811016 | tf_op jit(solution)/shard_map/ppermute | solution.py:29
  34.9 30.4 %collective-permute-start.7 = (bf16[528,256]{1,0:T(8,128)(2,1)S(1)}, bf16[528,256]{1,0:T(8,128)(2,1)S(1)}, u32[]{:S(2)}, u32[]{:S(2)}) collective-permute-start(bf16[528,256]{1,0:T(8,128)(2,1)S(1)} %shard_map.291.refs_0_), channel_id=1, source_target_pairs={{0,4},{1,5},{2,6},{3,7},{4,0},{5,1},{6,2},{7,3},{8,12},{9,13},{10,... | collective-permute-start | bytes 811016 | tf_op jit(solution)/shard_map/ppermute | solution.py:29
  39.9 27.5 %collective-permute-start.2 = (bf16[256,1024]{1,0:T(8,128)(2,1)S(1)}, bf16[256,1024]{1,0:T(8,128)(2,1)S(1)}, u32[]{:S(2)}, u32[]{:S(2)}) collective-permute-start(bf16[256,1024]{1,0:T(8,128)(2,1)S(1)} %collective-permute-done.1.refs_2_), channel_id=1, source_target_pairs={{0,8},{8,0},{16,24},{24,16},{1,9},{9,1},{17,25},{25,17},{2,10},{10... | collective-permute-start | bytes 1572872 | tf_op jit(solution)/shard_map/ppermute | solution.py:29
  40.2 31.4 %collective-permute-start.4 = (bf16[528,256]{1,0:T(8,128)(2,1)S(1)}, bf16[528,256]{1,0:T(8,128)(2,1)S(1)}, u32[]{:S(2)}, u32[]{:S(2)}) collective-permute-start(bf16[528,256]{1,0:T(8,128)(2,1)S(1)} %shard_map.291.refs_0_), channel_id=1, source_target_pairs={{0,1},{1,0},{2,3},{3,2},{4,5},{5,4},{6,7},{7,6},{8,9},{9,8},{10,11... | collective-permute-start | bytes 811016 | tf_op jit(solution)/shard_map/ppermute | solution.py:29
  47.6 23.9 %collective-permute-start.6 = (bf16[528,256]{1,0:T(8,128)(2,1)S(1)}, bf16[528,256]{1,0:T(8,128)(2,1)S(1)}, u32[]{:S(2)}, u32[]{:S(2)}) collective-permute-start(bf16[528,256]{1,0:T(8,128)(2,1)S(1)} %collective-permute-done.5.refs_2_), channel_id=1, source_target_pairs={{0,1},{1,0},{2,3},{3,2},{4,5},{5,4},{6,7},{7,6},{8,9},{9,8},{10,11... | collective-permute-start | bytes 811016 | tf_op jit(solution)/shard_map/ppermute | solution.py:29
  65.3 15.1 %collective-permute-start.10 = (bf16[528,256]{1,0:T(8,128)(2,1)S(1)}, bf16[528,256]{1,0:T(8,128)(2,1)S(1)}, u32[]{:S(2)}, u32[]{:S(2)}) collective-permute-start(bf16[528,256]{1,0:T(8,128)(2,1)S(1)} %collective-permute-done.9.refs_6_), channel_id=1, source_target_pairs={{0,1},{1,0},{2,3},{3,2},{4,5},{5,4},{6,7},{7,6},{8,9},{9,8},{10,11... | collective-permute-start | bytes 811016 | tf_op jit(solution)/shard_map/ppermute | solution.py:29
  66.8 19.7 %collective-permute-start.8 = (bf16[528,256]{1,0:T(8,128)(2,1)S(1)}, bf16[528,256]{1,0:T(8,128)(2,1)S(1)}, u32[]{:S(2)}, u32[]{:S(2)}) collective-permute-start(bf16[528,256]{1,0:T(8,128)(2,1)S(1)} %collective-permute-done.7.refs_4_), channel_id=1, source_target_pairs={{0,1},{1,0},{2,3},{3,2},{4,5},{5,4},{6,7},{7,6},{8,9},{9,8},{10,11... | collective-permute-start | bytes 811016 | tf_op jit(solution)/shard_map/ppermute | solution.py:29
  102.0 14.8 %collective-permute-start.13 = (bf16[256,1024]{1,0:T(8,128)(2,1)S(1)}, bf16[256,1024]{1,0:T(8,128)(2,1)S(1)}, u32[]{:S(2)}, u32[]{:S(2)}) collective-permute-start(bf16[256,1024]{1,0:T(8,128)(2,1)S(1)} %add_convert_fusion.5), channel_id=1, source_target_pairs={{0,16},{8,24},{16,0},{24,8},{1,17},{9,25},{17,1},{25,9},{2,18},{10... | collective-permute-start | bytes 1572872 | tf_op jit(solution)/shard_map/ppermute | solution.py:29
  103.5 18.3 %collective-permute-start.16 = (bf16[128,1024]{1,0:T(8,128)(2,1)S(1)}, bf16[128,1024]{1,0:T(8,128)(2,1)S(1)}, u32[]{:S(2)}, u32[]{:S(2)}) collective-permute-start(bf16[128,1024]{1,0:T(8,128)(2,1)S(1)} %bitcast.36), channel_id=1, source_target_pairs={{0,16},{8,24},{16,0},{24,8},{1,17},{9,25},{17,1},{25,9},{2,18},{10... | collective-permute-start | bytes 786440 | tf_op jit(solution)/shard_map/ppermute | solution.py:29
  119.1 12.9 %collective-permute-start.14 = (bf16[256,1024]{1,0:T(8,128)(2,1)}, bf16[256,1024]{1,0:T(8,128)(2,1)}, u32[]{:S(2)}, u32[]{:S(2)}) collective-permute-start(bf16[256,1024]{1,0:T(8,128)(2,1)} %get-tuple-element.178.refs_0_), channel_id=1, source_target_pairs={{0,8},{8,0},{16,24},{24,16},{1,9},{9,1},{17,25},{25,17},{2,10},{10... | collective-permute-start | bytes 1572872 | tf_op jit(solution)/shard_map/ppermute | solution.py:29
  119.1 17.9 %collective-permute-start.19 = (bf16[256,1024]{1,0:T(8,128)(2,1)}, bf16[256,1024]{1,0:T(8,128)(2,1)}, u32[]{:S(2)}, u32[]{:S(2)}) collective-permute-start(bf16[256,1024]{1,0:T(8,128)(2,1)} %get-tuple-element.178.refs_0_), channel_id=1, source_target_pairs={{0,16},{8,24},{16,0},{24,8},{1,17},{9,25},{17,1},{25,9},{2,18},{10... | collective-permute-start | bytes 1572872 | tf_op jit(solution)/shard_map/ppermute | solution.py:29
  148.8 14.3 %collective-permute-start.22 = (bf16[256,1024]{1,0:T(8,128)(2,1)S(1)}, bf16[256,1024]{1,0:T(8,128)(2,1)S(1)}, u32[]{:S(2)}, u32[]{:S(2)}) collective-permute-start(bf16[256,1024]{1,0:T(8,128)(2,1)S(1)} %add_convert_fusion.4), channel_id=1, source_target_pairs={{0,16},{8,24},{16,0},{24,8},{1,17},{9,25},{17,1},{25,9},{2,18},{10... | collective-permute-start | bytes 1572872 | tf_op jit(solution)/shard_map/ppermute | solution.py:29
  165.4 14.7 %collective-permute-start.28 = (bf16[256,1024]{1,0:T(8,128)(2,1)}, bf16[256,1024]{1,0:T(8,128)(2,1)}, u32[]{:S(2)}, u32[]{:S(2)}) collective-permute-start(bf16[256,1024]{1,0:T(8,128)(2,1)} %get-tuple-element.193.refs_0_), channel_id=1, source_target_pairs={{0,16},{8,24},{16,0},{24,8},{1,17},{9,25},{17,1},{25,9},{2,18},{10... | collective-permute-start | bytes 1572872 | tf_op jit(solution)/shard_map/ppermute | solution.py:29
  180.0 14.3 %collective-permute-start.24 = (bf16[256,1024]{1,0:T(8,128)(2,1)S(1)}, bf16[256,1024]{1,0:T(8,128)(2,1)S(1)}, u32[]{:S(2)}, u32[]{:S(2)}) collective-permute-start(bf16[256,1024]{1,0:T(8,128)(2,1)S(1)} %bitcast.45), channel_id=1, source_target_pairs={{0,16},{8,24},{16,0},{24,8},{1,17},{9,25},{17,1},{25,9},{2,18},{10... | collective-permute-start | bytes 1572872 | tf_op jit(solution)/shard_map/ppermute | solution.py:29
  186.5 8.4 %collective-permute-start.30 = (bf16[256,1024]{1,0:T(8,128)(2,1)S(1)}, bf16[256,1024]{1,0:T(8,128)(2,1)S(1)}, u32[]{:S(2)}, u32[]{:S(2)}) collective-permute-start(bf16[256,1024]{1,0:T(8,128)(2,1)S(1)} %get-tuple-element.200), channel_id=1, source_target_pairs={{0,8},{8,0},{16,24},{24,16},{1,9},{9,1},{17,25},{25,17},{2,10},{10... | collective-permute-start | bytes 1572872 | tf_op jit(solution)/shard_map/ppermute | solution.py:29
  186.7 10.0 %collective-permute-start.23 = (bf16[256,1024]{1,0:T(8,128)(2,1)S(1)}, bf16[256,1024]{1,0:T(8,128)(2,1)S(1)}, u32[]{:S(2)}, u32[]{:S(2)}) collective-permute-start(bf16[256,1024]{1,0:T(8,128)(2,1)S(1)} %bitcast.46), channel_id=1, source_target_pairs={{0,8},{8,0},{16,24},{24,16},{1,9},{9,1},{17,25},{25,17},{2,10},{10... | collective-permute-start | bytes 1572872 | tf_op jit(solution)/shard_map/ppermute | solution.py:29
  195.1 13.9 %collective-permute-start.31 = (bf16[256,1024]{1,0:T(8,128)(2,1)S(1)}, bf16[256,1024]{1,0:T(8,128)(2,1)S(1)}, u32[]{:S(2)}, u32[]{:S(2)}) collective-permute-start(bf16[256,1024]{1,0:T(8,128)(2,1)S(1)} %add_convert_fusion.3), channel_id=1, source_target_pairs={{0,16},{8,24},{16,0},{24,8},{1,17},{9,25},{17,1},{25,9},{2,18},{10... | collective-permute-start | bytes 1572872 | tf_op jit(solution)/shard_map/ppermute | solution.py:29
  210.4 14.3 %collective-permute-start.34 = (bf16[256,1024]{1,0:T(8,128)(2,1)S(1)}, bf16[256,1024]{1,0:T(8,128)(2,1)S(1)}, u32[]{:S(2)}, u32[]{:S(2)}) collective-permute-start(bf16[256,1024]{1,0:T(8,128)(2,1)S(1)} %get-tuple-element.203.refs_0_.refs_8_), channel_id=1, source_target_pairs={{0,16},{8,24},{16,0},{24,8},{1,17},{9,25},{17,1},{25,9},{2,18},{10... | collective-permute-start | bytes 1572872 | tf_op jit(solution)/shard_map/ppermute | solution.py:29
  231.4 14.0 %collective-permute-start.37 = (bf16[256,1024]{1,0:T(8,128)(2,1)S(1)}, bf16[256,1024]{1,0:T(8,128)(2,1)S(1)}, u32[]{:S(2)}, u32[]{:S(2)}) collective-permute-start(bf16[256,1024]{1,0:T(8,128)(2,1)S(1)} %add_convert_fusion.2), channel_id=1, source_target_pairs={{0,16},{8,24},{16,0},{24,8},{1,17},{9,25},{17,1},{25,9},{2,18},{10... | collective-permute-start | bytes 1572872 | tf_op jit(solution)/shard_map/ppermute | solution.py:29
  254.1 14.2 %collective-permute-start.38 = (bf16[256,1024]{1,0:T(8,128)(2,1)S(1)}, bf16[256,1024]{1,0:T(8,128)(2,1)S(1)}, u32[]{:S(2)}, u32[]{:S(2)}) collective-permute-start(bf16[256,1024]{1,0:T(8,128)(2,1)S(1)} %get-tuple-element.217.refs_0_), channel_id=1, source_target_pairs={{0,16},{8,24},{16,0},{24,8},{1,17},{9,25},{17,1},{25,9},{2,18},{10... | collective-permute-start | bytes 1572872 | tf_op jit(solution)/shard_map/ppermute | solution.py:29
  268.3 9.0 %collective-permute-start.42 = (bf16[128,1024]{1,0:T(8,128)(2,1)}, bf16[128,1024]{1,0:T(8,128)(2,1)}, u32[]{:S(2)}, u32[]{:S(2)}) collective-permute-start(bf16[128,1024]{1,0:T(8,128)(2,1)} %get-tuple-element.223.refs_0_), channel_id=1, source_target_pairs={{0,16},{8,24},{16,0},{24,8},{1,17},{9,25},{17,1},{25,9},{2,18},{10... | collective-permute-start | bytes 786440 | tf_op jit(solution)/shard_map/ppermute | solution.py:29
  279.4 15.6 %collective-permute-start.44 = (bf16[256,1024]{1,0:T(8,128)(2,1)S(1)}, bf16[256,1024]{1,0:T(8,128)(2,1)S(1)}, u32[]{:S(2)}, u32[]{:S(2)}) collective-permute-start(bf16[256,1024]{1,0:T(8,128)(2,1)S(1)} %add_convert_fusion.1), channel_id=1, source_target_pairs={{0,16},{8,24},{16,0},{24,8},{1,17},{9,25},{17,1},{25,9},{2,18},{10... | collective-permute-start | bytes 1572872 | tf_op jit(solution)/shard_map/ppermute | solution.py:29
  281.0 14.0 %collective-permute-start.40 = (bf16[256,1024]{1,0:T(8,128)(2,1)S(1)}, bf16[256,1024]{1,0:T(8,128)(2,1)S(1)}, u32[]{:S(2)}, u32[]{:S(2)}) collective-permute-start(bf16[256,1024]{1,0:T(8,128)(2,1)S(1)} %get-tuple-element.226), channel_id=1, source_target_pairs={{0,8},{8,0},{16,24},{24,16},{1,9},{9,1},{17,25},{25,17},{2,10},{10... | collective-permute-start | bytes 1572872 | tf_op jit(solution)/shard_map/ppermute | solution.py:29
  284.3 10.7 %collective-permute-start.45 = (bf16[512,256]{1,0:T(8,128)(2,1)S(1)}, bf16[512,256]{1,0:T(8,128)(2,1)S(1)}, u32[]{:S(2)}, u32[]{:S(2)}) collective-permute-start(bf16[512,256]{1,0:T(8,128)(2,1)S(1)} %get-tuple-element.243), channel_id=1, source_target_pairs={{0,1},{1,0},{2,3},{3,2},{4,5},{5,4},{6,7},{7,6},{8,9},{9,8},{10,11... | collective-permute-start | bytes 786440 | tf_op jit(solution)/shard_map/ppermute | solution.py:29
  296.0 14.3 %collective-permute-start.46 = (bf16[256,1024]{1,0:T(8,128)(2,1)S(1)}, bf16[256,1024]{1,0:T(8,128)(2,1)S(1)}, u32[]{:S(2)}, u32[]{:S(2)}) collective-permute-start(bf16[256,1024]{1,0:T(8,128)(2,1)S(1)} %get-tuple-element.251.refs_0_), channel_id=1, source_target_pairs={{0,16},{8,24},{16,0},{24,8},{1,17},{9,25},{17,1},{25,9},{2,18},{10... | collective-permute-start | bytes 1572872 | tf_op jit(solution)/shard_map/ppermute | solution.py:29
  296.1 10.9 %collective-permute-start.48 = (bf16[512,256]{1,0:T(8,128)(2,1)S(1)}, bf16[512,256]{1,0:T(8,128)(2,1)S(1)}, u32[]{:S(2)}, u32[]{:S(2)}) collective-permute-start(bf16[512,256]{1,0:T(8,128)(2,1)S(1)} %get-tuple-element.255), channel_id=1, source_target_pairs={{0,1},{1,0},{2,3},{3,2},{4,5},{5,4},{6,7},{7,6},{8,9},{9,8},{10,11... | collective-permute-start | bytes 786440 | tf_op jit(solution)/shard_map/ppermute | solution.py:29
  310.4 8.9 %collective-permute-start.51 = (bf16[256,1024]{1,0:T(8,128)(2,1)S(1)}, bf16[256,1024]{1,0:T(8,128)(2,1)S(1)}, u32[]{:S(2)}, u32[]{:S(2)}) collective-permute-start(bf16[256,1024]{1,0:T(8,128)(2,1)S(1)} %collective-permute-done.46.refs_0_), channel_id=1, source_target_pairs={{0,8},{8,0},{16,24},{24,16},{1,9},{9,1},{17,25},{25,17},{2,10},{10... | collective-permute-start | bytes 1572872 | tf_op jit(solution)/shard_map/ppermute | solution.py:29
  310.4 15.4 %collective-permute-start.54 = (bf16[512,256]{1,0:T(8,128)(2,1)S(1)}, bf16[512,256]{1,0:T(8,128)(2,1)S(1)}, u32[]{:S(2)}, u32[]{:S(2)}) collective-permute-start(bf16[512,256]{1,0:T(8,128)(2,1)S(1)} %get-tuple-element.270), channel_id=1, source_target_pairs={{0,1},{1,0},{2,3},{3,2},{4,5},{5,4},{6,7},{7,6},{8,9},{9,8},{10,11... | collective-permute-start | bytes 786440 | tf_op jit(solution)/shard_map/ppermute | solution.py:29
  310.5 15.6 %collective-permute-start.55 = (bf16[512,256]{1,0:T(8,128)(2,1)S(1)}, bf16[512,256]{1,0:T(8,128)(2,1)S(1)}, u32[]{:S(2)}, u32[]{:S(2)}) collective-permute-start(bf16[512,256]{1,0:T(8,128)(2,1)S(1)} %add_convert_fusion.14), channel_id=1, source_target_pairs={{0,6},{1,7},{2,4},{3,5},{4,2},{5,3},{6,0},{7,1},{8,14},{9,15},{10,... | collective-permute-start | bytes 786440 | tf_op jit(solution)/shard_map/ppermute | solution.py:29
  327.1 11.6 %collective-permute-start.56 = (bf16[256,1024]{1,0:T(8,128)(2,1)S(1)}, bf16[256,1024]{1,0:T(8,128)(2,1)S(1)}, u32[]{:S(2)}, u32[]{:S(2)}) collective-permute-start(bf16[256,1024]{1,0:T(8,128)(2,1)S(1)} %get-tuple-element.277), channel_id=1, source_target_pairs={{0,8},{8,0},{16,24},{24,16},{1,9},{9,1},{17,25},{25,17},{2,10},{10... | collective-permute-start | bytes 1572872 | tf_op jit(solution)/shard_map/ppermute | solution.py:29
  327.2 8.8 %collective-permute-start.52 = (bf16[128,1024]{1,0:T(8,128)(2,1)S(1)}, bf16[128,1024]{1,0:T(8,128)(2,1)}, u32[]{:S(2)}, u32[]{:S(2)}) collective-permute-start(bf16[128,1024]{1,0:T(8,128)(2,1)S(1)} %copy-done.61), channel_id=1, source_target_pairs={{0,16},{8,24},{16,0},{24,8},{1,17},{9,25},{17,1},{25,9},{2,18},{10... | collective-permute-start | bytes 786440 | tf_op jit(solution)/shard_map/ppermute | solution.py:29
  338.9 22.8 %collective-permute-start.58 = (bf16[256,1024]{1,0:T(8,128)(2,1)S(1)}, bf16[256,1024]{1,0:T(8,128)(2,1)S(1)}, u32[]{:S(2)}, u32[]{:S(2)}) collective-permute-start(bf16[256,1024]{1,0:T(8,128)(2,1)S(1)} %add_convert_fusion), channel_id=1, source_target_pairs={{0,16},{8,24},{16,0},{24,8},{1,17},{9,25},{17,1},{25,9},{2,18},{10... | collective-permute-start | bytes 1572872 | tf_op jit(solution)/shard_map/ppermute | solution.py:29
  341.4 20.4 %collective-permute-start.57 = (bf16[256,1024]{1,0:T(8,128)(2,1)S(1)}, bf16[256,1024]{1,0:T(8,128)(2,1)S(1)}, u32[]{:S(2)}, u32[]{:S(2)}) collective-permute-start(bf16[256,1024]{1,0:T(8,128)(2,1)S(1)} %get-tuple-element.281), channel_id=1, source_target_pairs={{0,8},{8,0},{16,24},{24,16},{1,9},{9,1},{17,25},{25,17},{2,10},{10... | collective-permute-start | bytes 1572872 | tf_op jit(solution)/shard_map/ppermute | solution.py:29
  341.4 16.3 %collective-permute-start.53 = (bf16[512,256]{1,0:T(8,128)(2,1)S(1)}, bf16[512,256]{1,0:T(8,128)(2,1)S(1)}, u32[]{:S(2)}, u32[]{:S(2)}) collective-permute-start(bf16[512,256]{1,0:T(8,128)(2,1)S(1)} %get-tuple-element.268), channel_id=1, source_target_pairs={{0,1},{1,0},{2,3},{3,2},{4,5},{5,4},{6,7},{7,6},{8,9},{9,8},{10,11... | collective-permute-start | bytes 786440 | tf_op jit(solution)/shard_map/ppermute | solution.py:29
  341.9 21.9 %collective-permute-start.49 = (bf16[128,1024]{1,0:T(8,128)(2,1)}, bf16[128,1024]{1,0:T(8,128)(2,1)S(1)}, u32[]{:S(2)}, u32[]{:S(2)}) collective-permute-start(bf16[128,1024]{1,0:T(8,128)(2,1)} %get-tuple-element.223.refs_0_), channel_id=1, source_target_pairs={{0,8},{8,0},{16,24},{24,16},{1,9},{9,1},{17,25},{25,17},{2,10},{10... | collective-permute-start | bytes 786440 | tf_op jit(solution)/shard_map/ppermute | solution.py:29
  342.9 21.8 %collective-permute-start.68 = (bf16[512,256]{1,0:T(8,128)(2,1)}, bf16[512,256]{1,0:T(8,128)(2,1)}, u32[]{:S(2)}, u32[]{:S(2)}) collective-permute-start(bf16[512,256]{1,0:T(8,128)(2,1)} %add_convert_fusion.12), channel_id=1, source_target_pairs={{0,2},{1,3},{2,0},{3,1},{4,6},{5,7},{6,4},{7,5},{8,10},{9,11},{10,... | collective-permute-start | bytes 786440 | tf_op jit(solution)/shard_map/ppermute | solution.py:29
  357.7 9.5 %collective-permute-start.63 = (bf16[512,256]{1,0:T(8,128)(2,1)}, bf16[512,256]{1,0:T(8,128)(2,1)}, u32[]{:S(2)}, u32[]{:S(2)}) collective-permute-start(bf16[512,256]{1,0:T(8,128)(2,1)} %get-tuple-element.289), channel_id=1, source_target_pairs={{0,1},{1,0},{2,3},{3,2},{4,5},{5,4},{6,7},{7,6},{8,9},{9,8},{10,11... | collective-permute-start | bytes 786440 | tf_op jit(solution)/shard_map/ppermute | solution.py:29
  361.7 8.1 %collective-permute-start.50 = (bf16[128,1024]{1,0:T(8,128)(2,1)S(1)}, bf16[128,1024]{1,0:T(8,128)(2,1)S(1)}, u32[]{:S(2)}, u32[]{:S(2)}) collective-permute-start(bf16[128,1024]{1,0:T(8,128)(2,1)S(1)} %copy-done.61), channel_id=1, source_target_pairs={{0,8},{8,0},{16,24},{24,16},{1,9},{9,1},{17,25},{25,17},{2,10},{10... | collective-permute-start | bytes 786440 | tf_op jit(solution)/shard_map/ppermute | solution.py:29
  361.8 10.5 %collective-permute-start.67 = (bf16[512,256]{1,0:T(8,128)(2,1)}, bf16[512,256]{1,0:T(8,128)(2,1)}, u32[]{:S(2)}, u32[]{:S(2)}) collective-permute-start(bf16[512,256]{1,0:T(8,128)(2,1)} %get-tuple-element.293), channel_id=1, source_target_pairs={{0,1},{1,0},{2,3},{3,2},{4,5},{5,4},{6,7},{7,6},{8,9},{9,8},{10,11... | collective-permute-start | bytes 786440 | tf_op jit(solution)/shard_map/ppermute | solution.py:29
  363.9 14.5 %collective-permute-start.60 = (bf16[128,1024]{1,0:T(8,128)(2,1)}, bf16[128,1024]{1,0:T(8,128)(2,1)S(1)}, u32[]{:S(2)}, u32[]{:S(2)}) collective-permute-start(bf16[128,1024]{1,0:T(8,128)(2,1)} %collective-permute-done.52.refs_5_), channel_id=1, source_target_pairs={{0,8},{8,0},{16,24},{24,16},{1,9},{9,1},{17,25},{25,17},{2,10},{10... | collective-permute-start | bytes 786440 | tf_op jit(solution)/shard_map/ppermute | solution.py:29
  364.6 19.7 %collective-permute-start.59 = (bf16[128,1024]{1,0:T(8,128)(2,1)}, bf16[128,1024]{1,0:T(8,128)(2,1)S(1)}, u32[]{:S(2)}, u32[]{:S(2)}) collective-permute-start(bf16[128,1024]{1,0:T(8,128)(2,1)} %collective-permute-done.42.refs_4_), channel_id=1, source_target_pairs={{0,8},{8,0},{16,24},{24,16},{1,9},{9,1},{17,25},{25,17},{2,10},{10... | collective-permute-start | bytes 786440 | tf_op jit(solution)/shard_map/ppermute | solution.py:29
  367.2 17.8 %collective-permute-start.66 = (bf16[256,1024]{1,0:T(8,128)(2,1)}, bf16[256,1024]{1,0:T(8,128)(2,1)}, u32[]{:S(2)}, u32[]{:S(2)}) collective-permute-start(bf16[256,1024]{1,0:T(8,128)(2,1)} %reduce-scatter.2.cloned.1.call-done.refs_0_), channel_id=1, source_target_pairs={{0,16},{8,24},{16,0},{24,8},{1,17},{9,25},{17,1},{25,9},{2,18},{10... | collective-permute-start | bytes 1572872 | tf_op jit(solution)/shard_map/ppermute | solution.py:29
  370.5 25.6 %collective-permute-start.74 = (bf16[512,256]{1,0:T(8,128)(2,1)}, bf16[512,256]{1,0:T(8,128)(2,1)}, u32[]{:S(2)}, u32[]{:S(2)}) collective-permute-start(bf16[512,256]{1,0:T(8,128)(2,1)} %copy-done.88), channel_id=1, source_target_pairs={{0,1},{1,0},{2,3},{3,2},{4,5},{5,4},{6,7},{7,6},{8,9},{9,8},{10,11... | collective-permute-start | bytes 786440 | tf_op jit(solution)/shard_map/ppermute | solution.py:29
  372.3 23.9 %collective-permute-start.64 = (bf16[512,256]{1,0:T(8,128)(2,1)}, bf16[512,256]{1,0:T(8,128)(2,1)}, u32[]{:S(2)}, u32[]{:S(2)}) collective-permute-start(bf16[512,256]{1,0:T(8,128)(2,1)} %add_convert_fusion.13), channel_id=1, source_target_pairs={{0,6},{1,7},{2,4},{3,5},{4,2},{5,3},{6,0},{7,1},{8,14},{9,15},{10,... | collective-permute-start | bytes 786440 | tf_op jit(solution)/shard_map/ppermute | solution.py:29
  379.1 17.6 %collective-permute-start.75 = (bf16[512,256]{1,0:T(8,128)(2,1)}, bf16[512,256]{1,0:T(8,128)(2,1)}, u32[]{:S(2)}, u32[]{:S(2)}) collective-permute-start(bf16[512,256]{1,0:T(8,128)(2,1)} %add_convert_fusion.10), channel_id=1, source_target_pairs={{0,2},{1,3},{2,0},{3,1},{4,6},{5,7},{6,4},{7,5},{8,10},{9,11},{10,... | collective-permute-start | bytes 786440 | tf_op jit(solution)/shard_map/ppermute | solution.py:29
  385.0 13.5 %collective-permute-start.76 = (bf16[512,256]{1,0:T(8,128)(2,1)}, bf16[512,256]{1,0:T(8,128)(2,1)}, u32[]{:S(2)}, u32[]{:S(2)}) collective-permute-start(bf16[512,256]{1,0:T(8,128)(2,1)} %add_convert_fusion.9), channel_id=1, source_target_pairs={{0,4},{1,5},{2,6},{3,7},{4,0},{5,1},{6,2},{7,3},{8,12},{9,13},{10,... | collective-permute-start | bytes 786440 | tf_op jit(solution)/shard_map/ppermute | solution.py:29
  385.0 23.0 %collective-permute-start.62 = (bf16[272,1024]{1,0:T(8,128)(2,1)S(1)}, bf16[272,1024]{1,0:T(8,128)(2,1)S(1)}, u32[]{:S(2)}, u32[]{:S(2)}) collective-permute-start(bf16[272,1024]{1,0:T(8,128)(2,1)S(1)} %shard_map.322.refs_0_), channel_id=1, source_target_pairs={{0,16},{8,24},{16,0},{24,8},{1,17},{9,25},{17,1},{25,9},{2,18},{10... | collective-permute-start | bytes 1671176 | tf_op jit(solution)/shard_map/ppermute | solution.py:29
  396.7 11.9 %collective-permute-start.72 = (bf16[128,1024]{1,0:T(8,128)(2,1)}, bf16[128,1024]{1,0:T(8,128)(2,1)S(1)}, u32[]{:S(2)}, u32[]{:S(2)}) collective-permute-start(bf16[128,1024]{1,0:T(8,128)(2,1)} %copy-done.87), channel_id=1, source_target_pairs={{0,8},{8,0},{16,24},{24,16},{1,9},{9,1},{17,25},{25,17},{2,10},{10... | collective-permute-start | bytes 786440 | tf_op jit(solution)/shard_map/ppermute | solution.py:29
  399.8 8.2 %collective-permute-start.80 = (bf16[128,256]{1,0:T(8,128)(2,1)S(1)}, bf16[128,256]{1,0:T(8,128)(2,1)S(1)}, u32[]{:S(2)}, u32[]{:S(2)}) collective-permute-start(bf16[128,256]{1,0:T(8,128)(2,1)S(1)} %slice.31), channel_id=1, source_target_pairs={{0,1},{1,0},{2,3},{3,2},{4,5},{5,4},{6,7},{7,6},{8,9},{9,8},{10,11... | collective-permute-start | bytes 196616 | tf_op jit(solution)/shard_map/ppermute | solution.py:29
  402.6 15.5 %collective-permute-start.83 = (bf16[512,256]{1,0:T(8,128)(2,1)}, bf16[512,256]{1,0:T(8,128)(2,1)S(1)}, u32[]{:S(2)}, u32[]{:S(2)}) collective-permute-start(bf16[512,256]{1,0:T(8,128)(2,1)} %copy-done.86), channel_id=1, source_target_pairs={{0,1},{1,0},{2,3},{3,2},{4,5},{5,4},{6,7},{7,6},{8,9},{9,8},{10,11... | collective-permute-start | bytes 786440 | tf_op jit(solution)/shard_map/ppermute | solution.py:29
  403.0 15.2 %collective-permute-start.84 = (bf16[512,256]{1,0:T(8,128)(2,1)S(1)}, bf16[512,256]{1,0:T(8,128)(2,1)S(1)}, u32[]{:S(2)}, u32[]{:S(2)}) collective-permute-start(bf16[512,256]{1,0:T(8,128)(2,1)S(1)} %add_convert_fusion.7), channel_id=1, source_target_pairs={{0,4},{1,5},{2,6},{3,7},{4,0},{5,1},{6,2},{7,3},{8,12},{9,13},{10,... | collective-permute-start | bytes 786440 | tf_op jit(solution)/shard_map/ppermute | solution.py:29
  414.1 7.8 %collective-permute-start.78 = (bf16[384,256]{1,0:T(8,128)(2,1)S(1)}, bf16[384,256]{1,0:T(8,128)(2,1)S(1)}, u32[]{:S(2)}, u32[]{:S(2)}) collective-permute-start(bf16[384,256]{1,0:T(8,128)(2,1)S(1)} %slice.30.refs_0_), channel_id=1, source_target_pairs={{0,16},{8,24},{16,0},{24,8},{1,17},{9,25},{17,1},{25,9},{2,18},{10... | collective-permute-start | bytes 589832 | tf_op jit(solution)/shard_map/ppermute | solution.py:29
  414.5 8.6 %collective-permute-start.71 = (bf16[128,1024]{1,0:T(8,128)(2,1)S(1)}, bf16[128,1024]{1,0:T(8,128)(2,1)S(1)}, u32[]{:S(2)}, u32[]{:S(2)}) collective-permute-start(bf16[128,1024]{1,0:T(8,128)(2,1)S(1)} %copy-done.85), channel_id=1, source_target_pairs={{0,8},{8,0},{16,24},{24,16},{1,9},{9,1},{17,25},{25,17},{2,10},{10... | collective-permute-start | bytes 786440 | tf_op jit(solution)/shard_map/ppermute | solution.py:29
  414.6 11.2 %collective-permute-start.73 = (bf16[128,1024]{1,0:T(8,128)(2,1)S(1)}, bf16[128,1024]{1,0:T(8,128)(2,1)S(1)}, u32[]{:S(2)}, u32[]{:S(2)}) collective-permute-start(bf16[128,1024]{1,0:T(8,128)(2,1)S(1)} %add_convert_fusion.11), channel_id=1, source_target_pairs={{0,16},{8,24},{16,0},{24,8},{1,17},{9,25},{17,1},{25,9},{2,18},{10... | collective-permute-start | bytes 786440 | tf_op jit(solution)/shard_map/ppermute | solution.py:29
  418.1 8.6 %collective-permute-start.77 = (bf16[384,256]{1,0:T(8,128)(2,1)S(1)}, bf16[384,256]{1,0:T(8,128)(2,1)S(1)}, u32[]{:S(2)}, u32[]{:S(2)}) collective-permute-start(bf16[384,256]{1,0:T(8,128)(2,1)S(1)} %slice.30.refs_0_), channel_id=1, source_target_pairs={{0,8},{8,0},{16,24},{24,16},{1,9},{9,1},{17,25},{25,17},{2,10},{10... | collective-permute-start | bytes 589832 | tf_op jit(solution)/shard_map/ppermute | solution.py:29
  418.3 8.4 %collective-permute-start.82 = (bf16[256,256]{1,0:T(8,128)(2,1)S(1)}, bf16[256,256]{1,0:T(8,128)(2,1)S(1)}, u32[]{:S(2)}, u32[]{:S(2)}) collective-permute-start(bf16[256,256]{1,0:T(8,128)(2,1)S(1)} %broadcast_select_fusion.1.refs_4_), channel_id=1, source_target_pairs={{0,8},{8,0},{16,24},{24,16},{1,9},{9,1},{17,25},{25,17},{2,10},{10... | collective-permute-start | bytes 393224 | tf_op jit(solution)/shard_map/ppermute | solution.py:29
  428.6 11.5 %collective-permute-start.86 = (bf16[384,256]{1,0:T(8,128)(2,1)S(1)}, bf16[384,256]{1,0:T(8,128)(2,1)S(1)}, u32[]{:S(2)}, u32[]{:S(2)}) collective-permute-start(bf16[384,256]{1,0:T(8,128)(2,1)S(1)} %slice.32.refs_0_), channel_id=1, source_target_pairs={{0,16},{8,24},{16,0},{24,8},{1,17},{9,25},{17,1},{25,9},{2,18},{10... | collective-permute-start | bytes 589832 | tf_op jit(solution)/shard_map/ppermute | solution.py:29
  429.0 14.7 %collective-permute-start.85 = (bf16[384,256]{1,0:T(8,128)(2,1)S(1)}, bf16[384,256]{1,0:T(8,128)(2,1)S(1)}, u32[]{:S(2)}, u32[]{:S(2)}) collective-permute-start(bf16[384,256]{1,0:T(8,128)(2,1)S(1)} %slice.32.refs_0_), channel_id=1, source_target_pairs={{0,8},{8,0},{16,24},{24,16},{1,9},{9,1},{17,25},{25,17},{2,10},{10... | collective-permute-start | bytes 589832 | tf_op jit(solution)/shard_map/ppermute | solution.py:29
  (130 other events, 740.5 us)
Sparse Core Ops, SparseCore 0:
  19.9 75.2 all-gather.2
  97.9 72.4 all-gather.4
  246.3 102.4 reduce-scatter.1

commit v2 on v1

--- a/solution.py
+++ b/solution.py
@@ -636,12 +636,17 @@
     sources, out_ref = refs[:size], refs[size]
     slots = sources[0].shape[0]
     base = lax.axis_index("ctx") * slots
-    total = jnp.zeros(out_ref.shape, F32)
-    for source in range(size):
-        order = order_ref[:, source * slots : (source + 1) * slots]
-        place = base + lax.broadcasted_iota(jnp.int32, (slots, slots), 0)
-        total += dot(one_hot(order == place), sources[source][...])
-    out_ref[...] = total
+    def columns(tile, carry):
+        lanes = pl.ds(pl.multiple_of(tile * 256, 256), 256)
+        total = jnp.zeros((slots, 256), F32)
+        for source in range(size):
+            order = order_ref[:, source * slots : (source + 1) * slots]
+            place = base + lax.broadcasted_iota(jnp.int32, (slots, slots), 0)
+            total += dot(one_hot(order == place), sources[source][:, lanes])
+        out_ref[:, lanes] = total
+        return carry
+
+    lax.fori_loop(0, out_ref.shape[1] // 256, columns, 0)
 
 
 def unsort_kernel(order_ref, *refs, size):
@@ -651,12 +656,18 @@
     pieces = count // size
     length = slots // pieces
     mine = lax.axis_index("ctx")
-    total = jnp.zeros(out_ref.shape, F32)
-    for index, source in enumerate(sources):
-        first = (mine ^ (index // pieces)) * slots + (index % pieces) * length
-        place = first + lax.broadcasted_iota(jnp.int32, (slots, length), 1)
-        total += dot(one_hot(order_ref[...] == place), source[:length, :])
-    out_ref[...] = total
+
+    def columns(tile, carry):
+        lanes = pl.ds(pl.multiple_of(tile * 256, 256), 256)
+        total = jnp.zeros((slots, 256), F32)
+        for index, source in enumerate(sources):
+            first = (mine ^ (index // pieces)) * slots + (index % pieces) * length
+            place = first + lax.broadcasted_iota(jnp.int32, (slots, length), 1)
+            total += dot(one_hot(order_ref[...] == place), source[:length, lanes])
+        out_ref[:, lanes] = total
+        return carry
+
+    lax.fori_loop(0, out_ref.shape[1] // 256, columns, 0)
     if count + 1 < len(refs):
         refs[count + 1][...] = sum(source[slots:, :].astype(F32) for source in sources)
 
@@ -904,37 +915,67 @@
     terms_ref[1:2, :] = shift[None]
 
 
-def feed_halves(feed):
-    groups, rows, cols = feed.shape
-    rows = rows // 2
-    return feed[:, :rows, :].reshape(groups * rows, cols), feed[:, rows:, :].reshape(groups * rows, cols)
+def feed_tile(feed, part, tile):
+    groups, rows = feed.shape[0], feed.shape[1] // 2
+    block = feed[:, part * rows : (part + 1) * rows, pl.ds(pl.multiple_of(tile * 256, 256), 256)]
+    return block.reshape(groups * rows, 256)
 
 
 def feed_forward_kernel(*refs, parts):
     sources, (feed, hidden_ref, slope_ref), outs = refs[:parts], refs[parts : parts + 3], refs[parts + 3 :]
     rate = 0.7978845608028654
-    first, second = feed_halves(feed)
+    tiles = feed.shape[2] // 256
     for index, (source, out) in enumerate(zip(sources, outs)):
         slots = source.shape[0]
         at = slice(index * slots, (index + 1) * slots)
-        pre = dot(source[...], first)
-        square = pre * pre
-        bend = jnp.tanh(rate * pre * (1.0 + 0.044715 * square))
-        half = 0.5 * (1.0 + bend)
-        slope_ref[at, :] = (half + 0.5 * pre * (1.0 - bend * bend) * rate * (1.0 + 0.134145 * square)).astype(BF)
-        hidden_ref[at, :] = (pre * half).astype(BF)
-        out[...] = dot(hidden_ref[at, :], second).astype(BF)
+
+        def first(tile, carry):
+            lanes = pl.ds(pl.multiple_of(tile * 256, 256), 256)
+            pre = dot(source[...], feed_tile(feed, 0, tile))
+            square = pre * pre
+            bend = jnp.tanh(rate * pre * (1.0 + 0.044715 * square))
+            half = 0.5 * (1.0 + bend)
+            slope = half + 0.5 * pre * (1.0 - bend * bend) * rate * (1.0 + 0.134145 * square)
+            slope_ref[at, lanes] = slope.astype(BF)
+            hidden_ref[at, lanes] = (pre * half).astype(BF)
+            return carry
+
+        def second(tile, carry):
+            lanes = pl.ds(pl.multiple_of(tile * 256, 256), 256)
+            out[:, lanes] = dot(hidden_ref[at, :], feed_tile(feed, 1, tile)).astype(BF)
+            return carry
+
+        lax.fori_loop(0, tiles, first, 0)
+        lax.fori_loop(0, tiles, second, 0)
+
+
+def feed_rows(feed, part, tile):
+    rows = feed.shape[1] // 2
+    count = 256 // rows
+    block = feed[pl.ds(tile * count, count), part * rows : (part + 1) * rows, :]
+    return block.reshape(256, feed.shape[2])
 
 
 def feed_backward_kernel(*refs, parts):
     sources, (feed, slope_ref, change_ref), outs = refs[:parts], refs[parts : parts + 3], refs[parts + 3 :]
-    first, second = feed_halves(feed)
+    tiles = feed.shape[0] * feed.shape[1] // 512
     for index, (source, out) in enumerate(zip(sources, outs)):
         slots = source.shape[0]
         at = slice(index * slots, (index + 1) * slots)
-        change = dot_right(source[...], second) * slope_ref[at, :].astype(F32)
-        change_ref[at, :] = change.astype(BF)
-        out[...] = dot_right(change_ref[at, :], first).astype(BF)
+
+        def second(tile, carry):
+            lanes = pl.ds(pl.multiple_of(tile * 256, 256), 256)
+            change = dot_right(source[...], feed_rows(feed, 1, tile)) * slope_ref[at, lanes].astype(F32)
+            change_ref[at, lanes] = change.astype(BF)
+            return carry
+
+        def first(tile, carry):
+            lanes = pl.ds(pl.multiple_of(tile * 256, 256), 256)
+            out[:, lanes] = dot_right(change_ref[at, :], feed_rows(feed, 0, tile)).astype(BF)
+            return carry
+
+        lax.fori_loop(0, tiles, second, 0)
+        lax.fori_loop(0, tiles, first, 0)
 
 
 def feed_grad_kernel(*refs, size, rows):
@@ -1507,7 +1548,7 @@
     for index in range(1, groups // 2):
         terms = terms + swap(pieces[index], "wsh", 2 * index)
     terms = jnp.transpose(terms)
-    cross_odd[0] = after(cross_odd[0], input_grad, self_middle, self_near)
+    cross_odd[0] = after(cross_odd[0], input_grad, self_near)
     cross_grads = finish(cross_even, cross_odd, cross_near, cross_middle, cross_far)
     self_grads = finish(self_even, self_odd, self_near, self_middle, self_far)
     return (

time: 461 us -> 459 us (level)
  Pallas kernels: 110 us -> 123 us
  starting transfers between devices: 97.9 us -> 90.1 us
    pallas_call x39, Pallas kernels: 110 us -> 123 us  [call(): pl.pallas_call(kernel, in_specs=specs, out_specs=[pl.BlockSpec(memory_spa...]
    ppermute x95, starting transfers between devices: 97.8 us -> 90 us  [swap(): return lax.ppermute(value, axis, [(i, i ^ bit) for i in range(size)])]
    ppermute x95, waiting for transfers between devices: 173 us -> 168 us  [swap(): return lax.ppermute(value, axis, [(i, i ^ bit) for i in range(size)])]
  transfers between devices with their start and end apart: 98 -> 98, of which waited for: 45 -> 46; matrix products, arithmetic and copies ran while one was open for 3% -> 3% of each run, Pallas kernels for 22% -> 24%
where the time goes in v2:
time: 459 us; the launch traced here: 453 us
  waiting for transfers between devices  171 us (37%)
  Pallas kernels  123 us (27%)
  starting transfers between devices  90.1 us (20%)
  local copies, waits for them, and re-layouts  40.9 us (9%)
  between operations  15.2 us (3%)
  other arithmetic  12.6 us (3%)
    ppermute x95, waiting for transfers between devices, swap(): return lax.ppermute(value, axis, [(i, i ^ bit) for i in range(size)])  168 us
    pallas_call x39, Pallas kernels, call(): pl.pallas_call(kernel, in_specs=specs, out_specs=[pl.BlockSpec(memory_spa...  123 us
    ppermute x95, starting transfers between devices, swap(): return lax.ppermute(value, axis, [(i, i ^ bit) for i in range(size)])  90 us
    unnamed x195, local copies, waits for them, and re-layouts  38.9 us
  transfers between devices with their start and end apart: 98, of which 46 were waited for; matrix products, arithmetic and copies ran while one was open for 3% of the time, Pallas kernels for 24%

profile of v2, /device:TPU:0, one launch (start us, length us, event | category | flops | bytes accessed | tf_op | source)
XLA Modules:
  0.0 453.0 jit_solution(6315973081096930225)
XLA Ops:
  8.3 3.0 collective-permute-start.3
  11.3 3.5 collective-permute-done.3.refs_4_
  17.3 2.5 shard_map.296
  19.8 1.9 collective-permute-start.5
  21.7 2.4 shard_map.302
  24.1 3.4 collective-permute-done.5.refs_2_
  31.3 3.6 collective-permute-start.9
  35.1 4.8 %collective-permute-done.1.refs_2_ = bf16[256,1024]{1,0:T(8,128)(2,1)S(1)} collective-permute-done((bf16[256,1024]{1,0:T(8,128)(2,1)S(1)}, bf16[256,1024]{1,0:T(8,128)(2,1)S(1)}, u32[]{:S(2)}, u32[]{:S(2)}) %collective-permute-start.1) | collective-permute-done | bytes 524320 | tf_op jit(solution)/shard_map/ppermute | solution.py:29
  41.3 6.3 %collective-permute-done.9.refs_6_ = bf16[528,256]{1,0:T(8,128)(2,1)S(1)} collective-permute-done((bf16[528,256]{1,0:T(8,128)(2,1)S(1)}, bf16[528,256]{1,0:T(8,128)(2,1)S(1)}, u32[]{:S(2)}, u32[]{:S(2)}) %collective-permute-start.9) | collective-permute-done | bytes 270368 | tf_op jit(solution)/shard_map/ppermute | solution.py:29
  49.2 16.1 %collective-permute-done.7.refs_4_ = bf16[528,256]{1,0:T(8,128)(2,1)S(1)} collective-permute-done((bf16[528,256]{1,0:T(8,128)(2,1)S(1)}, bf16[528,256]{1,0:T(8,128)(2,1)S(1)}, u32[]{:S(2)}, u32[]{:S(2)}) %collective-permute-start.7) | collective-permute-done | bytes 270368 | tf_op jit(solution)/shard_map/ppermute | solution.py:29
  67.4 4.3 shard_map.289
  71.7 8.6 %collective-permute-done.10.refs_7_ = bf16[528,256]{1,0:T(8,128)(2,1)S(1)} collective-permute-done((bf16[528,256]{1,0:T(8,128)(2,1)S(1)}, bf16[528,256]{1,0:T(8,128)(2,1)S(1)}, u32[]{:S(2)}, u32[]{:S(2)}) %collective-permute-start.10) | collective-permute-done | bytes 270368 | tf_op jit(solution)/shard_map/ppermute | solution.py:29
  80.4 6.1 %collective-permute-done.8.refs_5_ = bf16[528,256]{1,0:T(8,128)(2,1)S(1)} collective-permute-done((bf16[528,256]{1,0:T(8,128)(2,1)S(1)}, bf16[528,256]{1,0:T(8,128)(2,1)S(1)}, u32[]{:S(2)}, u32[]{:S(2)}) %collective-permute-start.8) | collective-permute-done | bytes 270368 | tf_op jit(solution)/shard_map/ppermute | solution.py:29
  87.4 2.5 shard_map.292
  90.0 4.9 %shard_map.293 = (bf16[512,256]{1,0:T(8,128)(2,1)S(1)}, f32[2,1,1024]{2,1,0:T(1,128)S(1)}, bf16[256,1024]{1,0:T(8,128)(2,1)S(1)}, bf16[256,1024]{1,0:T(8,128)(2,1)S(1)}) custom-call(s32[9]{0:T(128)S(1)} %pad_add_fusion.2.meta, bf16[1024,256]{1,0:T(8,128)(2,1)S(1)} %get-tuple-element.174.refs_0_.refs_2_, ...), custom_call_target="tpu_custom_call" | custom-call | flops 1048576 | bytes 65536 | tf_op jit(solution)/shard_map/pallas_call | solution.py:496
  95.6 1.9 collective-permute-done.11
  97.7 3.5 shard_map.294
  104.1 12.7 %collective-permute-done.13.refs_2_ = bf16[256,1024]{1,0:T(8,128)(2,1)S(1)} collective-permute-done((bf16[256,1024]{1,0:T(8,128)(2,1)S(1)}, bf16[256,1024]{1,0:T(8,128)(2,1)S(1)}, u32[]{:S(2)}, u32[]{:S(2)}) %collective-permute-start.13) | collective-permute-done | bytes 524320 | tf_op jit(solution)/shard_map/ppermute | solution.py:29
  131.9 3.6 shard_map.298
  139.2 5.5 %shard_map.299 = (bf16[512,256]{1,0:T(8,128)(2,1)S(1)}, bf16[512,256]{1,0:T(8,128)(2,1)S(1)}, f32[2,1,1024]{2,1,0:T(1,128)S(1)}, bf16[256,1024]{1,0:T(8,128)(2,1)S(1)}, bf16[256,1024]{1,0:T(8,128)(2,1)S(1)}) custom-call(s32[9]{0:T(128)S(1)} %pad_add_fusion.3.meta, bf16[256,1024]{1,0:T(8,128)(2,1)} %collective-permute-done.19.refs_0_.refs_2_, ...), custom_call_target="tpu_custom_call" | custom-call | flops 1048576 | bytes 65536 | tf_op jit(solution)/shard_map/pallas_call | solution.py:496
  149.9 12.7 %collective-permute-done.22.refs_2_ = bf16[256,1024]{1,0:T(8,128)(2,1)S(1)} collective-permute-done((bf16[256,1024]{1,0:T(8,128)(2,1)S(1)}, bf16[256,1024]{1,0:T(8,128)(2,1)S(1)}, u32[]{:S(2)}, u32[]{:S(2)}) %collective-permute-start.22) | collective-permute-done | bytes 524320 | tf_op jit(solution)/shard_map/ppermute | solution.py:29
  167.8 2.6 all-gather.5.cloned.1.call-done
  170.4 2.2 copy-done
  173.6 7.1 %shard_map.303 = (bf16[512,1024]{1,0:T(8,128)(2,1)S(1)}, bf16[512,1024]{1,0:T(8,128)(2,1)S(1)}, bf16[256,1024]{1,0:T(8,128)(2,1)S(1)}, bf16[256,1024]{1,0:T(8,128)(2,1)S(1)}) custom-call(bf16[256,1024]{1,0:T(8,128)(2,1)} %get-tuple-element.193.refs_0_, bf16[256,1024]{1,0:T(8,128)(2,1)S(1)} %copy-done.36, bf16[8,256,1024]{2,1,0:T(8,128)(2,1)S(1)} %bitcast.31), custom_call_target="tpu_custom_call" | custom-call | flops 1048576 | bytes 65536 | tf_op jit(solution)/shard_map/pallas_call | solution.py:496
  183.0 7.2 %shard_map.304 = (bf16[512,1024]{1,0:T(8,128)(2,1)S(1)}, bf16[512,1024]{1,0:T(8,128)(2,1)S(1)}, bf16[256,1024]{1,0:T(8,128)(2,1)S(1)}, bf16[256,1024]{1,0:T(8,128)(2,1)S(1)}) custom-call(bf16[256,1024]{1,0:T(8,128)(2,1)} %collective-permute-done.28.refs_0_.refs_2_, bf16[256,1024]{1,0:T(8,128)(2,1)S(1)} %collective-permute-done.29.refs_1_.refs_3_, ...), custom_call_target="tpu_custom_call" | custom-call | flops 1048576 | bytes 65536 | tf_op jit(solution)/shard_map/pallas_call | solution.py:496
  190.8 4.5 collective-permute-done.24.refs_2_
  198.7 11.1 %collective-permute-done.31.refs_2_ = bf16[256,1024]{1,0:T(8,128)(2,1)S(1)} collective-permute-done((bf16[256,1024]{1,0:T(8,128)(2,1)S(1)}, bf16[256,1024]{1,0:T(8,128)(2,1)S(1)}, u32[]{:S(2)}, u32[]{:S(2)}) %collective-permute-start.31) | collective-permute-done | bytes 524320 | tf_op jit(solution)/shard_map/ppermute | solution.py:29
  213.1 5.4 %shard_map.306 = (bf16[512,1024]{1,0:T(8,128)(2,1)S(1)}, bf16[256,1024]{1,0:T(8,128)(2,1)S(1)}, bf16[256,1024]{1,0:T(8,128)(2,1)S(1)}) custom-call(bf16[256,1024]{1,0:T(8,128)(2,1)S(1)} %get-tuple-element.203.refs_0_.refs_8_, bf16[256,1024]{1,0:T(8,128)(2,1)S(1)} %collective-permute-done.32.refs_1_.refs_9_, bf16[8,256,1024]{2,1,0:T(8,128)(2,1)S(1)} %bitcast.33, ...), custom_call_target="tpu_custom_call" | custom-call | flops 1048576 | bytes 65536 | tf_op jit(solution)/shard_map/pallas_call | solution.py:496
  219.3 6.2 %collective-permute-done.34.refs_0_.refs_10_ = bf16[256,1024]{1,0:T(8,128)(2,1)S(1)} collective-permute-done((bf16[256,1024]{1,0:T(8,128)(2,1)S(1)}, bf16[256,1024]{1,0:T(8,128)(2,1)S(1)}, u32[]{:S(2)}, u32[]{:S(2)}) %collective-permute-start.34) | collective-permute-done | bytes 524320 | tf_op jit(solution)/shard_map/ppermute | solution.py:29
  225.5 1.9 collective-permute-done.35.refs_1_.refs_11_
  227.4 5.4 %shard_map.307 = (bf16[512,1024]{1,0:T(8,128)(2,1)S(1)}, bf16[256,1024]{1,0:T(8,128)(2,1)S(1)}, bf16[256,1024]{1,0:T(8,128)(2,1)S(1)}) custom-call(bf16[256,1024]{1,0:T(8,128)(2,1)S(1)} %collective-permute-done.34.refs_0_.refs_10_, bf16[256,1024]{1,0:T(8,128)(2,1)S(1)} %collective-permute-done.35.refs_1_.refs_11_, bf16[8,256,1024]{2,1,0:T(8,128)(2,1)S(1)} %bitcast.34, ...), custom_call_target="tpu_custom_call" | custom-call | flops 1048576 | bytes 65536 | tf_op jit(solution)/shard_map/pallas_call | solution.py:496
  236.6 6.8 %shard_map.308 = bf16[8,256,1024]{2,1,0:T(8,128)(2,1)S(1)} custom-call(bf16[256,1024]{1,0:T(8,128)(2,1)} %get-tuple-element.193.refs_0_, bf16[256,1024]{1,0:T(8,128)(2,1)S(1)} %copy-done.37, bf16[256,1024]{1,0:T(8,128)(2,1)} %collective-permute-done.28.refs_0_.refs_2_, bf16[256,1024]{1,0:T(8,128)(2,1)S(1)} %collective-permute-done.29.refs_1_.refs_3_, ...), custom_call_target="tpu_custom_call" | custom-call | flops 1048576 | bytes 65536 | tf_op jit(solution)/shard_map/pallas_call | solution.py:496
  243.3 2.0 copy-done.2
  245.3 3.7 collective-permute-done.37.refs_2_
  250.0 2.1 collective-permute-done.33.refs_1_
  259.5 3.7 shard_map.310
  263.3 8.7 %collective-permute-done.38.refs_0_ = bf16[256,1024]{1,0:T(8,128)(2,1)S(1)} collective-permute-done((bf16[256,1024]{1,0:T(8,128)(2,1)S(1)}, bf16[256,1024]{1,0:T(8,128)(2,1)S(1)}, u32[]{:S(2)}, u32[]{:S(2)}) %collective-permute-start.38) | collective-permute-done | bytes 524320 | tf_op jit(solution)/shard_map/ppermute | solution.py:29
  273.9 6.4 %shard_map.311 = (bf16[512,256]{1,0:T(8,128)(2,1)S(1)}, f32[512,256]{1,0:T(8,128)S(1)}, f32[512,256]{1,0:T(8,128)S(1)}, f32[256,1024]{1,0:T(8,128)S(1)}, bf16[25...) custom-call(s32[9]{0:T(128)S(1)} %pad_add_fusion.3.meta, ...), custom_call_target="tpu_custom_call", output_to_operand_aliasing={{1}: (11, {}), {2}: (12, {}), {3}: (13, {})} | custom-call | flops 1048576 | bytes 65536 | tf_op jit(solution)/shard_map/pallas_call | solution.py:496
  281.0 1.9 collective-permute-done.43
  284.7 3.3 shard_map.313
  292.3 3.7 shard_map.312
  296.1 5.3 %collective-permute-done.45 = bf16[512,256]{1,0:T(8,128)(2,1)S(1)} collective-permute-done((bf16[512,256]{1,0:T(8,128)(2,1)S(1)}, bf16[512,256]{1,0:T(8,128)(2,1)S(1)}, u32[]{:S(2)}, u32[]{:S(2)}) %collective-permute-start.45) | collective-permute-done | bytes 262176 | tf_op jit(solution)/shard_map/ppermute | solution.py:29
  304.3 4.7 %shard_map.316 = (bf16[512,256]{1,0:T(8,128)(2,1)S(1)}, f32[1024,256]{1,0:T(8,128)S(1)}, f32[1024,256]{1,0:T(8,128)S(1)}, f32[256,1024]{1,0:T(8,128)S(1)}) custom-call(s32[9]{0:T(128)S(1)} %pad_add_fusion.2.meta, bf16[256,1024]{1,0:T(8,128)(2,1)S(1)} %get-tuple-element.251.refs_0_, bf16[256,1024]{1,0:T(8,128)(2,1)S(1)} %collective-permute-done.47.refs_1_, ...), custom_call_target="tpu_custom_call" | custom-call | flops 1048576 | bytes 65536 | tf_op jit(solution)/shard_map/pallas_call | solution.py:496
  309.0 6.9 %collective-permute-done.48 = bf16[512,256]{1,0:T(8,128)(2,1)S(1)} collective-permute-done((bf16[512,256]{1,0:T(8,128)(2,1)S(1)}, bf16[512,256]{1,0:T(8,128)(2,1)S(1)}, u32[]{:S(2)}, u32[]{:S(2)}) %collective-permute-start.48) | collective-permute-done | bytes 262176 | tf_op jit(solution)/shard_map/ppermute | solution.py:29
  317.2 3.0 collective-permute-start.55
  320.3 6.4 %shard_map.317 = (bf16[512,256]{1,0:T(8,128)(2,1)S(1)}, f32[1024,256]{1,0:T(8,128)S(1)}, f32[1024,256]{1,0:T(8,128)S(1)}, f32[256,1024]{1,0:T(8,128)S(1)}) custom-call(s32[9]{0:T(128)S(1)} %pad_add_fusion.2.meta, bf16[256,1024]{1,0:T(8,128)(2,1)S(1)} %collective-permute-done.46.refs_0_, ...), custom_call_target="tpu_custom_call", output_to_operand_aliasing={{1}: (10, {}), {2}: (11, {}), {3}: (12, {})} | custom-call | flops 1048576 | bytes 65536 | tf_op jit(solution)/shard_map/pallas_call | solution.py:496
  330.3 7.2 %collective-permute-done.52.refs_5_ = bf16[128,1024]{1,0:T(8,128)(2,1)} collective-permute-done((bf16[128,1024]{1,0:T(8,128)(2,1)S(1)}, bf16[128,1024]{1,0:T(8,128)(2,1)}, u32[]{:S(2)}, u32[]{:S(2)}) %collective-permute-start.52) | collective-permute-done | bytes 262176 | tf_op jit(solution)/shard_map/ppermute | solution.py:29
  337.6 2.7 shard_map.318
  345.9 13.5 %collective-permute-start.68 = (bf16[512,256]{1,0:T(8,128)(2,1)}, bf16[512,256]{1,0:T(8,128)(2,1)}, u32[]{:S(2)}, u32[]{:S(2)}) collective-permute-start(bf16[512,256]{1,0:T(8,128)(2,1)} %add_convert_fusion.12), channel_id=1, source_target_pairs={{0,2},{1,3},{2,0},{3,1},{4,6},{5,7},{6,4},{7,5},{8,10},{9,11},{10,... | collective-permute-start | bytes 786440 | tf_op jit(solution)/shard_map/ppermute | solution.py:29
  359.8 2.0 shard_map.321
  366.5 2.4 collective-permute-done.63
  372.0 2.5 collective-permute-done.67
  374.5 3.8 collective-permute-start.64
  380.8 4.8 %collective-permute-start.75 = (bf16[512,256]{1,0:T(8,128)(2,1)}, bf16[512,256]{1,0:T(8,128)(2,1)}, u32[]{:S(2)}, u32[]{:S(2)}) collective-permute-start(bf16[512,256]{1,0:T(8,128)(2,1)} %add_convert_fusion.10), channel_id=1, source_target_pairs={{0,2},{1,3},{2,0},{3,1},{4,6},{5,7},{6,4},{7,5},{8,10},{9,11},{10,... | collective-permute-start | bytes 786440 | tf_op jit(solution)/shard_map/ppermute | solution.py:29
  392.1 4.3 shard_map.323
  397.0 3.3 collective-permute-done.76
  404.8 3.8 shard_map.324
  410.2 4.5 collective-permute-done.81
  416.9 2.5 shard_map.325
  419.9 2.6 collective-permute-done.78.refs_2_
  427.3 1.8 shard_map.326
  430.1 1.9 collective-permute-start.91
  434.1 3.5 collective-permute-start.92
  437.8 3.4 collective-permute-start.94
  (426 shorter events, 131.3 us)
Async XLA Ops:
  7.2 116.9 %all-gather.3.cloned.1.call-start = ((), (), s32[]{:S(2)}) async-start(), calls=%async_computation.1 | async-start | bytes 2359296 | tf_op jit(solution)/shard_map/all_gather | solution.py:255
  19.8 150.6 %all-gather.5.cloned.1.call-start = ((), (), s32[]{:S(2)}) async-start(), calls=%async_computation.2 | async-start | bytes 4718592 | tf_op jit(solution)/shard_map/all_gather | solution.py:255
  19.8 7.7 %collective-permute-start.5 = (bf16[528,256]{1,0:T(8,128)(2,1)S(1)}, bf16[528,256]{1,0:T(8,128)(2,1)S(1)}, u32[]{:S(2)}, u32[]{:S(2)}) collective-permute-start(bf16[528,256]{1,0:T(8,128)(2,1)S(1)} %shard_map.291.refs_0_), channel_id=1, source_target_pairs={{0,2},{1,3},{2,0},{3,1},{4,6},{5,7},{6,4},{7,5},{8,10},{9,11},{10,... | collective-permute-start | bytes 811016 | tf_op jit(solution)/shard_map/ppermute | solution.py:29
  27.6 337.7 %reduce-scatter.2.cloned.1.call-start = ((), (), s32[]{:S(2)}) async-start(), calls=%async_computation.3 | async-start | bytes 4718592 | tf_op jit(solution)/shard_map/reduce_scatter | solution.py:259
  27.7 12.2 %collective-permute-start.1 = (bf16[256,1024]{1,0:T(8,128)(2,1)S(1)}, bf16[256,1024]{1,0:T(8,128)(2,1)S(1)}, u32[]{:S(2)}, u32[]{:S(2)}) collective-permute-start(bf16[256,1024]{1,0:T(8,128)(2,1)S(1)} %bitcast.42), channel_id=1, source_target_pairs={{0,16},{8,24},{16,0},{24,8},{1,17},{9,25},{17,1},{25,9},{2,18},{10... | collective-permute-start | bytes 1572872 | tf_op jit(solution)/shard_map/ppermute | solution.py:29
  29.1 37.7 %collective-permute-start = (bf16[256,1024]{1,0:T(8,128)(2,1)S(1)}, bf16[256,1024]{1,0:T(8,128)(2,1)S(1)}, u32[]{:S(2)}, u32[]{:S(2)}) collective-permute-start(bf16[256,1024]{1,0:T(8,128)(2,1)S(1)} %bitcast.43), channel_id=1, source_target_pairs={{0,8},{8,0},{16,24},{24,16},{1,9},{9,1},{17,25},{25,17},{2,10},{10... | collective-permute-start | bytes 1572872 | tf_op jit(solution)/shard_map/ppermute | solution.py:29
  31.3 16.4 %collective-permute-start.9 = (bf16[528,256]{1,0:T(8,128)(2,1)S(1)}, bf16[528,256]{1,0:T(8,128)(2,1)S(1)}, u32[]{:S(2)}, u32[]{:S(2)}) collective-permute-start(bf16[528,256]{1,0:T(8,128)(2,1)S(1)} %shard_map.291.refs_0_), channel_id=1, source_target_pairs={{0,6},{1,7},{2,4},{3,5},{4,2},{5,3},{6,0},{7,1},{8,14},{9,15},{10,... | collective-permute-start | bytes 811016 | tf_op jit(solution)/shard_map/ppermute | solution.py:29
  34.9 30.4 %collective-permute-start.7 = (bf16[528,256]{1,0:T(8,128)(2,1)S(1)}, bf16[528,256]{1,0:T(8,128)(2,1)S(1)}, u32[]{:S(2)}, u32[]{:S(2)}) collective-permute-start(bf16[528,256]{1,0:T(8,128)(2,1)S(1)} %shard_map.291.refs_0_), channel_id=1, source_target_pairs={{0,4},{1,5},{2,6},{3,7},{4,0},{5,1},{6,2},{7,3},{8,12},{9,13},{10,... | collective-permute-start | bytes 811016 | tf_op jit(solution)/shard_map/ppermute | solution.py:29
  39.9 27.5 %collective-permute-start.2 = (bf16[256,1024]{1,0:T(8,128)(2,1)S(1)}, bf16[256,1024]{1,0:T(8,128)(2,1)S(1)}, u32[]{:S(2)}, u32[]{:S(2)}) collective-permute-start(bf16[256,1024]{1,0:T(8,128)(2,1)S(1)} %collective-permute-done.1.refs_2_), channel_id=1, source_target_pairs={{0,8},{8,0},{16,24},{24,16},{1,9},{9,1},{17,25},{25,17},{2,10},{10... | collective-permute-start | bytes 1572872 | tf_op jit(solution)/shard_map/ppermute | solution.py:29
  40.2 31.6 %collective-permute-start.4 = (bf16[528,256]{1,0:T(8,128)(2,1)S(1)}, bf16[528,256]{1,0:T(8,128)(2,1)S(1)}, u32[]{:S(2)}, u32[]{:S(2)}) collective-permute-start(bf16[528,256]{1,0:T(8,128)(2,1)S(1)} %shard_map.291.refs_0_), channel_id=1, source_target_pairs={{0,1},{1,0},{2,3},{3,2},{4,5},{5,4},{6,7},{7,6},{8,9},{9,8},{10,11... | collective-permute-start | bytes 811016 | tf_op jit(solution)/shard_map/ppermute | solution.py:29
  47.6 24.1 %collective-permute-start.6 = (bf16[528,256]{1,0:T(8,128)(2,1)S(1)}, bf16[528,256]{1,0:T(8,128)(2,1)S(1)}, u32[]{:S(2)}, u32[]{:S(2)}) collective-permute-start(bf16[528,256]{1,0:T(8,128)(2,1)S(1)} %collective-permute-done.5.refs_2_), channel_id=1, source_target_pairs={{0,1},{1,0},{2,3},{3,2},{4,5},{5,4},{6,7},{7,6},{8,9},{9,8},{10,11... | collective-permute-start | bytes 811016 | tf_op jit(solution)/shard_map/ppermute | solution.py:29
  65.3 15.1 %collective-permute-start.10 = (bf16[528,256]{1,0:T(8,128)(2,1)S(1)}, bf16[528,256]{1,0:T(8,128)(2,1)S(1)}, u32[]{:S(2)}, u32[]{:S(2)}) collective-permute-start(bf16[528,256]{1,0:T(8,128)(2,1)S(1)} %collective-permute-done.9.refs_6_), channel_id=1, source_target_pairs={{0,1},{1,0},{2,3},{3,2},{4,5},{5,4},{6,7},{7,6},{8,9},{9,8},{10,11... | collective-permute-start | bytes 811016 | tf_op jit(solution)/shard_map/ppermute | solution.py:29
  66.8 19.7 %collective-permute-start.8 = (bf16[528,256]{1,0:T(8,128)(2,1)S(1)}, bf16[528,256]{1,0:T(8,128)(2,1)S(1)}, u32[]{:S(2)}, u32[]{:S(2)}) collective-permute-start(bf16[528,256]{1,0:T(8,128)(2,1)S(1)} %collective-permute-done.7.refs_4_), channel_id=1, source_target_pairs={{0,1},{1,0},{2,3},{3,2},{4,5},{5,4},{6,7},{7,6},{8,9},{9,8},{10,11... | collective-permute-start | bytes 811016 | tf_op jit(solution)/shard_map/ppermute | solution.py:29
  102.0 14.8 %collective-permute-start.13 = (bf16[256,1024]{1,0:T(8,128)(2,1)S(1)}, bf16[256,1024]{1,0:T(8,128)(2,1)S(1)}, u32[]{:S(2)}, u32[]{:S(2)}) collective-permute-start(bf16[256,1024]{1,0:T(8,128)(2,1)S(1)} %add_convert_fusion.5), channel_id=1, source_target_pairs={{0,16},{8,24},{16,0},{24,8},{1,17},{9,25},{17,1},{25,9},{2,18},{10... | collective-permute-start | bytes 1572872 | tf_op jit(solution)/shard_map/ppermute | solution.py:29
  103.5 18.3 %collective-permute-start.16 = (bf16[128,1024]{1,0:T(8,128)(2,1)S(1)}, bf16[128,1024]{1,0:T(8,128)(2,1)S(1)}, u32[]{:S(2)}, u32[]{:S(2)}) collective-permute-start(bf16[128,1024]{1,0:T(8,128)(2,1)S(1)} %bitcast.36), channel_id=1, source_target_pairs={{0,16},{8,24},{16,0},{24,8},{1,17},{9,25},{17,1},{25,9},{2,18},{10... | collective-permute-start | bytes 786440 | tf_op jit(solution)/shard_map/ppermute | solution.py:29
  119.1 12.9 %collective-permute-start.14 = (bf16[256,1024]{1,0:T(8,128)(2,1)}, bf16[256,1024]{1,0:T(8,128)(2,1)}, u32[]{:S(2)}, u32[]{:S(2)}) collective-permute-start(bf16[256,1024]{1,0:T(8,128)(2,1)} %get-tuple-element.178.refs_0_), channel_id=1, source_target_pairs={{0,8},{8,0},{16,24},{24,16},{1,9},{9,1},{17,25},{25,17},{2,10},{10... | collective-permute-start | bytes 1572872 | tf_op jit(solution)/shard_map/ppermute | solution.py:29
  119.1 17.9 %collective-permute-start.19 = (bf16[256,1024]{1,0:T(8,128)(2,1)}, bf16[256,1024]{1,0:T(8,128)(2,1)}, u32[]{:S(2)}, u32[]{:S(2)}) collective-permute-start(bf16[256,1024]{1,0:T(8,128)(2,1)} %get-tuple-element.178.refs_0_), channel_id=1, source_target_pairs={{0,16},{8,24},{16,0},{24,8},{1,17},{9,25},{17,1},{25,9},{2,18},{10... | collective-permute-start | bytes 1572872 | tf_op jit(solution)/shard_map/ppermute | solution.py:29
  148.4 14.3 %collective-permute-start.22 = (bf16[256,1024]{1,0:T(8,128)(2,1)S(1)}, bf16[256,1024]{1,0:T(8,128)(2,1)S(1)}, u32[]{:S(2)}, u32[]{:S(2)}) collective-permute-start(bf16[256,1024]{1,0:T(8,128)(2,1)S(1)} %add_convert_fusion.4), channel_id=1, source_target_pairs={{0,16},{8,24},{16,0},{24,8},{1,17},{9,25},{17,1},{25,9},{2,18},{10... | collective-permute-start | bytes 1572872 | tf_op jit(solution)/shard_map/ppermute | solution.py:29
  164.9 15.9 %collective-permute-start.28 = (bf16[256,1024]{1,0:T(8,128)(2,1)}, bf16[256,1024]{1,0:T(8,128)(2,1)}, u32[]{:S(2)}, u32[]{:S(2)}) collective-permute-start(bf16[256,1024]{1,0:T(8,128)(2,1)} %get-tuple-element.193.refs_0_), channel_id=1, source_target_pairs={{0,16},{8,24},{16,0},{24,8},{1,17},{9,25},{17,1},{25,9},{2,18},{10... | collective-permute-start | bytes 1572872 | tf_op jit(solution)/shard_map/ppermute | solution.py:29
  180.9 14.3 %collective-permute-start.24 = (bf16[256,1024]{1,0:T(8,128)(2,1)S(1)}, bf16[256,1024]{1,0:T(8,128)(2,1)S(1)}, u32[]{:S(2)}, u32[]{:S(2)}) collective-permute-start(bf16[256,1024]{1,0:T(8,128)(2,1)S(1)} %bitcast.45), channel_id=1, source_target_pairs={{0,16},{8,24},{16,0},{24,8},{1,17},{9,25},{17,1},{25,9},{2,18},{10... | collective-permute-start | bytes 1572872 | tf_op jit(solution)/shard_map/ppermute | solution.py:29
  195.9 13.9 %collective-permute-start.31 = (bf16[256,1024]{1,0:T(8,128)(2,1)S(1)}, bf16[256,1024]{1,0:T(8,128)(2,1)S(1)}, u32[]{:S(2)}, u32[]{:S(2)}) collective-permute-start(bf16[256,1024]{1,0:T(8,128)(2,1)S(1)} %add_convert_fusion.3), channel_id=1, source_target_pairs={{0,16},{8,24},{16,0},{24,8},{1,17},{9,25},{17,1},{25,9},{2,18},{10... | collective-permute-start | bytes 1572872 | tf_op jit(solution)/shard_map/ppermute | solution.py:29
  211.2 14.3 %collective-permute-start.34 = (bf16[256,1024]{1,0:T(8,128)(2,1)S(1)}, bf16[256,1024]{1,0:T(8,128)(2,1)S(1)}, u32[]{:S(2)}, u32[]{:S(2)}) collective-permute-start(bf16[256,1024]{1,0:T(8,128)(2,1)S(1)} %get-tuple-element.203.refs_0_.refs_8_), channel_id=1, source_target_pairs={{0,16},{8,24},{16,0},{24,8},{1,17},{9,25},{17,1},{25,9},{2,18},{10... | collective-permute-start | bytes 1572872 | tf_op jit(solution)/shard_map/ppermute | solution.py:29
  235.0 14.0 %collective-permute-start.37 = (bf16[256,1024]{1,0:T(8,128)(2,1)S(1)}, bf16[256,1024]{1,0:T(8,128)(2,1)S(1)}, u32[]{:S(2)}, u32[]{:S(2)}) collective-permute-start(bf16[256,1024]{1,0:T(8,128)(2,1)S(1)} %add_convert_fusion.2), channel_id=1, source_target_pairs={{0,16},{8,24},{16,0},{24,8},{1,17},{9,25},{17,1},{25,9},{2,18},{10... | collective-permute-start | bytes 1572872 | tf_op jit(solution)/shard_map/ppermute | solution.py:29
  257.7 14.2 %collective-permute-start.38 = (bf16[256,1024]{1,0:T(8,128)(2,1)S(1)}, bf16[256,1024]{1,0:T(8,128)(2,1)S(1)}, u32[]{:S(2)}, u32[]{:S(2)}) collective-permute-start(bf16[256,1024]{1,0:T(8,128)(2,1)S(1)} %get-tuple-element.217.refs_0_), channel_id=1, source_target_pairs={{0,16},{8,24},{16,0},{24,8},{1,17},{9,25},{17,1},{25,9},{2,18},{10... | collective-permute-start | bytes 1572872 | tf_op jit(solution)/shard_map/ppermute | solution.py:29
  272.0 9.0 %collective-permute-start.42 = (bf16[128,1024]{1,0:T(8,128)(2,1)}, bf16[128,1024]{1,0:T(8,128)(2,1)}, u32[]{:S(2)}, u32[]{:S(2)}) collective-permute-start(bf16[128,1024]{1,0:T(8,128)(2,1)} %get-tuple-element.223.refs_0_), channel_id=1, source_target_pairs={{0,16},{8,24},{16,0},{24,8},{1,17},{9,25},{17,1},{25,9},{2,18},{10... | collective-permute-start | bytes 786440 | tf_op jit(solution)/shard_map/ppermute | solution.py:29
  283.1 18.2 %collective-permute-start.44 = (bf16[256,1024]{1,0:T(8,128)(2,1)S(1)}, bf16[256,1024]{1,0:T(8,128)(2,1)S(1)}, u32[]{:S(2)}, u32[]{:S(2)}) collective-permute-start(bf16[256,1024]{1,0:T(8,128)(2,1)S(1)} %add_convert_fusion.1), channel_id=1, source_target_pairs={{0,16},{8,24},{16,0},{24,8},{1,17},{9,25},{17,1},{25,9},{2,18},{10... | collective-permute-start | bytes 1572872 | tf_op jit(solution)/shard_map/ppermute | solution.py:29
  284.6 16.7 %collective-permute-start.40 = (bf16[256,1024]{1,0:T(8,128)(2,1)S(1)}, bf16[256,1024]{1,0:T(8,128)(2,1)S(1)}, u32[]{:S(2)}, u32[]{:S(2)}) collective-permute-start(bf16[256,1024]{1,0:T(8,128)(2,1)S(1)} %get-tuple-element.226), channel_id=1, source_target_pairs={{0,8},{8,0},{16,24},{24,16},{1,9},{9,1},{17,25},{25,17},{2,10},{10... | collective-permute-start | bytes 1572872 | tf_op jit(solution)/shard_map/ppermute | solution.py:29
  288.0 13.4 %collective-permute-start.45 = (bf16[512,256]{1,0:T(8,128)(2,1)S(1)}, bf16[512,256]{1,0:T(8,128)(2,1)S(1)}, u32[]{:S(2)}, u32[]{:S(2)}) collective-permute-start(bf16[512,256]{1,0:T(8,128)(2,1)S(1)} %get-tuple-element.243), channel_id=1, source_target_pairs={{0,1},{1,0},{2,3},{3,2},{4,5},{5,4},{6,7},{7,6},{8,9},{9,8},{10,11... | collective-permute-start | bytes 786440 | tf_op jit(solution)/shard_map/ppermute | solution.py:29
  302.4 14.3 %collective-permute-start.46 = (bf16[256,1024]{1,0:T(8,128)(2,1)S(1)}, bf16[256,1024]{1,0:T(8,128)(2,1)S(1)}, u32[]{:S(2)}, u32[]{:S(2)}) collective-permute-start(bf16[256,1024]{1,0:T(8,128)(2,1)S(1)} %get-tuple-element.251.refs_0_), channel_id=1, source_target_pairs={{0,16},{8,24},{16,0},{24,8},{1,17},{9,25},{17,1},{25,9},{2,18},{10... | collective-permute-start | bytes 1572872 | tf_op jit(solution)/shard_map/ppermute | solution.py:29
  302.4 13.5 %collective-permute-start.48 = (bf16[512,256]{1,0:T(8,128)(2,1)S(1)}, bf16[512,256]{1,0:T(8,128)(2,1)S(1)}, u32[]{:S(2)}, u32[]{:S(2)}) collective-permute-start(bf16[512,256]{1,0:T(8,128)(2,1)S(1)} %get-tuple-element.255), channel_id=1, source_target_pairs={{0,1},{1,0},{2,3},{3,2},{4,5},{5,4},{6,7},{7,6},{8,9},{9,8},{10,11... | collective-permute-start | bytes 786440 | tf_op jit(solution)/shard_map/ppermute | solution.py:29
  316.7 10.0 %collective-permute-start.54 = (bf16[512,256]{1,0:T(8,128)(2,1)S(1)}, bf16[512,256]{1,0:T(8,128)(2,1)S(1)}, u32[]{:S(2)}, u32[]{:S(2)}) collective-permute-start(bf16[512,256]{1,0:T(8,128)(2,1)S(1)} %get-tuple-element.270), channel_id=1, source_target_pairs={{0,1},{1,0},{2,3},{3,2},{4,5},{5,4},{6,7},{7,6},{8,9},{9,8},{10,11... | collective-permute-start | bytes 786440 | tf_op jit(solution)/shard_map/ppermute | solution.py:29
  317.2 10.4 %collective-permute-start.55 = (bf16[512,256]{1,0:T(8,128)(2,1)S(1)}, bf16[512,256]{1,0:T(8,128)(2,1)S(1)}, u32[]{:S(2)}, u32[]{:S(2)}) collective-permute-start(bf16[512,256]{1,0:T(8,128)(2,1)S(1)} %add_convert_fusion.14), channel_id=1, source_target_pairs={{0,6},{1,7},{2,4},{3,5},{4,2},{5,3},{6,0},{7,1},{8,14},{9,15},{10,... | collective-permute-start | bytes 786440 | tf_op jit(solution)/shard_map/ppermute | solution.py:29
  328.7 11.6 %collective-permute-start.56 = (bf16[256,1024]{1,0:T(8,128)(2,1)S(1)}, bf16[256,1024]{1,0:T(8,128)(2,1)S(1)}, u32[]{:S(2)}, u32[]{:S(2)}) collective-permute-start(bf16[256,1024]{1,0:T(8,128)(2,1)S(1)} %get-tuple-element.277), channel_id=1, source_target_pairs={{0,8},{8,0},{16,24},{24,16},{1,9},{9,1},{17,25},{25,17},{2,10},{10... | collective-permute-start | bytes 1572872 | tf_op jit(solution)/shard_map/ppermute | solution.py:29
  328.8 8.8 %collective-permute-start.52 = (bf16[128,1024]{1,0:T(8,128)(2,1)S(1)}, bf16[128,1024]{1,0:T(8,128)(2,1)}, u32[]{:S(2)}, u32[]{:S(2)}) collective-permute-start(bf16[128,1024]{1,0:T(8,128)(2,1)S(1)} %copy-done.61), channel_id=1, source_target_pairs={{0,16},{8,24},{16,0},{24,8},{1,17},{9,25},{17,1},{25,9},{2,18},{10... | collective-permute-start | bytes 786440 | tf_op jit(solution)/shard_map/ppermute | solution.py:29
  340.4 21.4 %collective-permute-start.58 = (bf16[256,1024]{1,0:T(8,128)(2,1)S(1)}, bf16[256,1024]{1,0:T(8,128)(2,1)S(1)}, u32[]{:S(2)}, u32[]{:S(2)}) collective-permute-start(bf16[256,1024]{1,0:T(8,128)(2,1)S(1)} %add_convert_fusion), channel_id=1, source_target_pairs={{0,16},{8,24},{16,0},{24,8},{1,17},{9,25},{17,1},{25,9},{2,18},{10... | collective-permute-start | bytes 1572872 | tf_op jit(solution)/shard_map/ppermute | solution.py:29
  343.0 18.9 %collective-permute-start.57 = (bf16[256,1024]{1,0:T(8,128)(2,1)S(1)}, bf16[256,1024]{1,0:T(8,128)(2,1)S(1)}, u32[]{:S(2)}, u32[]{:S(2)}) collective-permute-start(bf16[256,1024]{1,0:T(8,128)(2,1)S(1)} %get-tuple-element.281), channel_id=1, source_target_pairs={{0,8},{8,0},{16,24},{24,16},{1,9},{9,1},{17,25},{25,17},{2,10},{10... | collective-permute-start | bytes 1572872 | tf_op jit(solution)/shard_map/ppermute | solution.py:29
  343.1 16.3 %collective-permute-start.53 = (bf16[512,256]{1,0:T(8,128)(2,1)S(1)}, bf16[512,256]{1,0:T(8,128)(2,1)S(1)}, u32[]{:S(2)}, u32[]{:S(2)}) collective-permute-start(bf16[512,256]{1,0:T(8,128)(2,1)S(1)} %get-tuple-element.268), channel_id=1, source_target_pairs={{0,1},{1,0},{2,3},{3,2},{4,5},{5,4},{6,7},{7,6},{8,9},{9,8},{10,11... | collective-permute-start | bytes 786440 | tf_op jit(solution)/shard_map/ppermute | solution.py:29
  344.9 20.4 %collective-permute-start.49 = (bf16[128,1024]{1,0:T(8,128)(2,1)}, bf16[128,1024]{1,0:T(8,128)(2,1)S(1)}, u32[]{:S(2)}, u32[]{:S(2)}) collective-permute-start(bf16[128,1024]{1,0:T(8,128)(2,1)} %get-tuple-element.223.refs_0_), channel_id=1, source_target_pairs={{0,8},{8,0},{16,24},{24,16},{1,9},{9,1},{17,25},{25,17},{2,10},{10... | collective-permute-start | bytes 786440 | tf_op jit(solution)/shard_map/ppermute | solution.py:29
  345.9 20.7 %collective-permute-start.68 = (bf16[512,256]{1,0:T(8,128)(2,1)}, bf16[512,256]{1,0:T(8,128)(2,1)}, u32[]{:S(2)}, u32[]{:S(2)}) collective-permute-start(bf16[512,256]{1,0:T(8,128)(2,1)} %add_convert_fusion.12), channel_id=1, source_target_pairs={{0,2},{1,3},{2,0},{3,1},{4,6},{5,7},{6,4},{7,5},{8,10},{9,11},{10,... | collective-permute-start | bytes 786440 | tf_op jit(solution)/shard_map/ppermute | solution.py:29
  359.4 9.5 %collective-permute-start.63 = (bf16[512,256]{1,0:T(8,128)(2,1)}, bf16[512,256]{1,0:T(8,128)(2,1)}, u32[]{:S(2)}, u32[]{:S(2)}) collective-permute-start(bf16[512,256]{1,0:T(8,128)(2,1)} %get-tuple-element.289), channel_id=1, source_target_pairs={{0,1},{1,0},{2,3},{3,2},{4,5},{5,4},{6,7},{7,6},{8,9},{9,8},{10,11... | collective-permute-start | bytes 786440 | tf_op jit(solution)/shard_map/ppermute | solution.py:29
  361.8 9.0 %collective-permute-start.50 = (bf16[128,1024]{1,0:T(8,128)(2,1)S(1)}, bf16[128,1024]{1,0:T(8,128)(2,1)S(1)}, u32[]{:S(2)}, u32[]{:S(2)}) collective-permute-start(bf16[128,1024]{1,0:T(8,128)(2,1)S(1)} %copy-done.61), channel_id=1, source_target_pairs={{0,8},{8,0},{16,24},{24,16},{1,9},{9,1},{17,25},{25,17},{2,10},{10... | collective-permute-start | bytes 786440 | tf_op jit(solution)/shard_map/ppermute | solution.py:29
  361.9 12.6 %collective-permute-start.67 = (bf16[512,256]{1,0:T(8,128)(2,1)}, bf16[512,256]{1,0:T(8,128)(2,1)}, u32[]{:S(2)}, u32[]{:S(2)}) collective-permute-start(bf16[512,256]{1,0:T(8,128)(2,1)} %get-tuple-element.293), channel_id=1, source_target_pairs={{0,1},{1,0},{2,3},{3,2},{4,5},{5,4},{6,7},{7,6},{8,9},{9,8},{10,11... | collective-permute-start | bytes 786440 | tf_op jit(solution)/shard_map/ppermute | solution.py:29
  365.3 14.7 %collective-permute-start.60 = (bf16[128,1024]{1,0:T(8,128)(2,1)}, bf16[128,1024]{1,0:T(8,128)(2,1)S(1)}, u32[]{:S(2)}, u32[]{:S(2)}) collective-permute-start(bf16[128,1024]{1,0:T(8,128)(2,1)} %collective-permute-done.52.refs_5_), channel_id=1, source_target_pairs={{0,8},{8,0},{16,24},{24,16},{1,9},{9,1},{17,25},{25,17},{2,10},{10... | collective-permute-start | bytes 786440 | tf_op jit(solution)/shard_map/ppermute | solution.py:29
  366.5 19.0 %collective-permute-start.59 = (bf16[128,1024]{1,0:T(8,128)(2,1)}, bf16[128,1024]{1,0:T(8,128)(2,1)S(1)}, u32[]{:S(2)}, u32[]{:S(2)}) collective-permute-start(bf16[128,1024]{1,0:T(8,128)(2,1)} %collective-permute-done.42.refs_4_), channel_id=1, source_target_pairs={{0,8},{8,0},{16,24},{24,16},{1,9},{9,1},{17,25},{25,17},{2,10},{10... | collective-permute-start | bytes 786440 | tf_op jit(solution)/shard_map/ppermute | solution.py:29
  368.9 17.4 %collective-permute-start.66 = (bf16[256,1024]{1,0:T(8,128)(2,1)}, bf16[256,1024]{1,0:T(8,128)(2,1)}, u32[]{:S(2)}, u32[]{:S(2)}) collective-permute-start(bf16[256,1024]{1,0:T(8,128)(2,1)} %reduce-scatter.2.cloned.1.call-done.refs_0_), channel_id=1, source_target_pairs={{0,16},{8,24},{16,0},{24,8},{1,17},{9,25},{17,1},{25,9},{2,18},{10... | collective-permute-start | bytes 1572872 | tf_op jit(solution)/shard_map/ppermute | solution.py:29
  371.6 24.8 %collective-permute-start.74 = (bf16[512,256]{1,0:T(8,128)(2,1)}, bf16[512,256]{1,0:T(8,128)(2,1)}, u32[]{:S(2)}, u32[]{:S(2)}) collective-permute-start(bf16[512,256]{1,0:T(8,128)(2,1)} %copy-done.88), channel_id=1, source_target_pairs={{0,1},{1,0},{2,3},{3,2},{4,5},{5,4},{6,7},{7,6},{8,9},{9,8},{10,11... | collective-permute-start | bytes 786440 | tf_op jit(solution)/shard_map/ppermute | solution.py:29
  374.5 21.9 %collective-permute-start.64 = (bf16[512,256]{1,0:T(8,128)(2,1)}, bf16[512,256]{1,0:T(8,128)(2,1)}, u32[]{:S(2)}, u32[]{:S(2)}) collective-permute-start(bf16[512,256]{1,0:T(8,128)(2,1)} %add_convert_fusion.13), channel_id=1, source_target_pairs={{0,6},{1,7},{2,4},{3,5},{4,2},{5,3},{6,0},{7,1},{8,14},{9,15},{10,... | collective-permute-start | bytes 786440 | tf_op jit(solution)/shard_map/ppermute | solution.py:29
  380.8 16.1 %collective-permute-start.75 = (bf16[512,256]{1,0:T(8,128)(2,1)}, bf16[512,256]{1,0:T(8,128)(2,1)}, u32[]{:S(2)}, u32[]{:S(2)}) collective-permute-start(bf16[512,256]{1,0:T(8,128)(2,1)} %add_convert_fusion.10), channel_id=1, source_target_pairs={{0,2},{1,3},{2,0},{3,1},{4,6},{5,7},{6,4},{7,5},{8,10},{9,11},{10,... | collective-permute-start | bytes 786440 | tf_op jit(solution)/shard_map/ppermute | solution.py:29
  386.3 14.0 %collective-permute-start.76 = (bf16[512,256]{1,0:T(8,128)(2,1)}, bf16[512,256]{1,0:T(8,128)(2,1)}, u32[]{:S(2)}, u32[]{:S(2)}) collective-permute-start(bf16[512,256]{1,0:T(8,128)(2,1)} %add_convert_fusion.9), channel_id=1, source_target_pairs={{0,4},{1,5},{2,6},{3,7},{4,0},{5,1},{6,2},{7,3},{8,12},{9,13},{10,... | collective-permute-start | bytes 786440 | tf_op jit(solution)/shard_map/ppermute | solution.py:29
  386.3 22.3 %collective-permute-start.62 = (bf16[272,1024]{1,0:T(8,128)(2,1)S(1)}, bf16[272,1024]{1,0:T(8,128)(2,1)S(1)}, u32[]{:S(2)}, u32[]{:S(2)}) collective-permute-start(bf16[272,1024]{1,0:T(8,128)(2,1)S(1)} %shard_map.322.refs_0_), channel_id=1, source_target_pairs={{0,16},{8,24},{16,0},{24,8},{1,17},{9,25},{17,1},{25,9},{2,18},{10... | collective-permute-start | bytes 1671176 | tf_op jit(solution)/shard_map/ppermute | solution.py:29
  396.4 8.4 %collective-permute-start.69 = (bf16[256,1024]{1,0:T(8,128)(2,1)}, bf16[256,1024]{1,0:T(8,128)(2,1)}, u32[]{:S(2)}, u32[]{:S(2)}) collective-permute-start(bf16[256,1024]{1,0:T(8,128)(2,1)} %collective-permute-done.66.refs_2_), channel_id=1, source_target_pairs={{0,8},{8,0},{16,24},{24,16},{1,9},{9,1},{17,25},{25,17},{2,10},{10... | collective-permute-start | bytes 1572872 | tf_op jit(solution)/shard_map/ppermute | solution.py:29
  396.9 12.2 %collective-permute-start.72 = (bf16[128,1024]{1,0:T(8,128)(2,1)}, bf16[128,1024]{1,0:T(8,128)(2,1)S(1)}, u32[]{:S(2)}, u32[]{:S(2)}) collective-permute-start(bf16[128,1024]{1,0:T(8,128)(2,1)} %copy-done.87), channel_id=1, source_target_pairs={{0,8},{8,0},{16,24},{24,16},{1,9},{9,1},{17,25},{25,17},{2,10},{10... | collective-permute-start | bytes 786440 | tf_op jit(solution)/shard_map/ppermute | solution.py:29
  403.0 16.4 %collective-permute-start.83 = (bf16[512,256]{1,0:T(8,128)(2,1)}, bf16[512,256]{1,0:T(8,128)(2,1)S(1)}, u32[]{:S(2)}, u32[]{:S(2)}) collective-permute-start(bf16[512,256]{1,0:T(8,128)(2,1)} %copy-done.86), channel_id=1, source_target_pairs={{0,1},{1,0},{2,3},{3,2},{4,5},{5,4},{6,7},{7,6},{8,9},{9,8},{10,11... | collective-permute-start | bytes 786440 | tf_op jit(solution)/shard_map/ppermute | solution.py:29
  404.8 14.7 %collective-permute-start.84 = (bf16[512,256]{1,0:T(8,128)(2,1)S(1)}, bf16[512,256]{1,0:T(8,128)(2,1)S(1)}, u32[]{:S(2)}, u32[]{:S(2)}) collective-permute-start(bf16[512,256]{1,0:T(8,128)(2,1)S(1)} %add_convert_fusion.7), channel_id=1, source_target_pairs={{0,4},{1,5},{2,6},{3,7},{4,0},{5,1},{6,2},{7,3},{8,12},{9,13},{10,... | collective-permute-start | bytes 786440 | tf_op jit(solution)/shard_map/ppermute | solution.py:29
  408.6 7.1 %collective-permute-start.70 = (bf16[272,1024]{1,0:T(8,128)(2,1)S(1)}, bf16[272,1024]{1,0:T(8,128)(2,1)S(1)}, u32[]{:S(2)}, u32[]{:S(2)}) collective-permute-start(bf16[272,1024]{1,0:T(8,128)(2,1)S(1)} %collective-permute-done.62.refs_2_), channel_id=1, source_target_pairs={{0,8},{8,0},{16,24},{24,16},{1,9},{9,1},{17,25},{25,17},{2,10},{10... | collective-permute-start | bytes 1671176 | tf_op jit(solution)/shard_map/ppermute | solution.py:29
  414.7 7.8 %collective-permute-start.78 = (bf16[384,256]{1,0:T(8,128)(2,1)S(1)}, bf16[384,256]{1,0:T(8,128)(2,1)S(1)}, u32[]{:S(2)}, u32[]{:S(2)}) collective-permute-start(bf16[384,256]{1,0:T(8,128)(2,1)S(1)} %slice.30.refs_0_), channel_id=1, source_target_pairs={{0,16},{8,24},{16,0},{24,8},{1,17},{9,25},{17,1},{25,9},{2,18},{10... | collective-permute-start | bytes 589832 | tf_op jit(solution)/shard_map/ppermute | solution.py:29
  415.7 8.0 %collective-permute-start.71 = (bf16[128,1024]{1,0:T(8,128)(2,1)S(1)}, bf16[128,1024]{1,0:T(8,128)(2,1)S(1)}, u32[]{:S(2)}, u32[]{:S(2)}) collective-permute-start(bf16[128,1024]{1,0:T(8,128)(2,1)S(1)} %copy-done.85), channel_id=1, source_target_pairs={{0,8},{8,0},{16,24},{24,16},{1,9},{9,1},{17,25},{25,17},{2,10},{10... | collective-permute-start | bytes 786440 | tf_op jit(solution)/shard_map/ppermute | solution.py:29
  415.8 10.6 %collective-permute-start.73 = (bf16[128,1024]{1,0:T(8,128)(2,1)S(1)}, bf16[128,1024]{1,0:T(8,128)(2,1)S(1)}, u32[]{:S(2)}, u32[]{:S(2)}) collective-permute-start(bf16[128,1024]{1,0:T(8,128)(2,1)S(1)} %add_convert_fusion.11), channel_id=1, source_target_pairs={{0,16},{8,24},{16,0},{24,8},{1,17},{9,25},{17,1},{25,9},{2,18},{10... | collective-permute-start | bytes 786440 | tf_op jit(solution)/shard_map/ppermute | solution.py:29
  419.4 7.9 %collective-permute-start.77 = (bf16[384,256]{1,0:T(8,128)(2,1)S(1)}, bf16[384,256]{1,0:T(8,128)(2,1)S(1)}, u32[]{:S(2)}, u32[]{:S(2)}) collective-permute-start(bf16[384,256]{1,0:T(8,128)(2,1)S(1)} %slice.30.refs_0_), channel_id=1, source_target_pairs={{0,8},{8,0},{16,24},{24,16},{1,9},{9,1},{17,25},{25,17},{2,10},{10... | collective-permute-start | bytes 589832 | tf_op jit(solution)/shard_map/ppermute | solution.py:29
  419.6 7.7 %collective-permute-start.82 = (bf16[256,256]{1,0:T(8,128)(2,1)S(1)}, bf16[256,256]{1,0:T(8,128)(2,1)S(1)}, u32[]{:S(2)}, u32[]{:S(2)}) collective-permute-start(bf16[256,256]{1,0:T(8,128)(2,1)S(1)} %broadcast_select_fusion.1.refs_4_), channel_id=1, source_target_pairs={{0,8},{8,0},{16,24},{24,16},{1,9},{9,1},{17,25},{25,17},{2,10},{10... | collective-permute-start | bytes 393224 | tf_op jit(solution)/shard_map/ppermute | solution.py:29
  423.7 8.4 %collective-permute-start.88 = (bf16[128,256]{1,0:T(8,128)(2,1)S(1)}, bf16[128,256]{1,0:T(8,128)(2,1)S(1)}, u32[]{:S(2)}, u32[]{:S(2)}) collective-permute-start(bf16[128,256]{1,0:T(8,128)(2,1)S(1)} %slice.33), channel_id=1, source_target_pairs={{0,1},{1,0},{2,3},{3,2},{4,5},{5,4},{6,7},{7,6},{8,9},{9,8},{10,11... | collective-permute-start | bytes 196616 | tf_op jit(solution)/shard_map/ppermute | solution.py:29
  429.1 12.2 %collective-permute-start.86 = (bf16[384,256]{1,0:T(8,128)(2,1)S(1)}, bf16[384,256]{1,0:T(8,128)(2,1)S(1)}, u32[]{:S(2)}, u32[]{:S(2)}) collective-permute-start(bf16[384,256]{1,0:T(8,128)(2,1)S(1)} %slice.32.refs_0_), channel_id=1, source_target_pairs={{0,16},{8,24},{16,0},{24,8},{1,17},{9,25},{17,1},{25,9},{2,18},{10... | collective-permute-start | bytes 589832 | tf_op jit(solution)/shard_map/ppermute | solution.py:29
  430.1 14.3 %collective-permute-start.85 = (bf16[384,256]{1,0:T(8,128)(2,1)S(1)}, bf16[384,256]{1,0:T(8,128)(2,1)S(1)}, u32[]{:S(2)}, u32[]{:S(2)}) collective-permute-start(bf16[384,256]{1,0:T(8,128)(2,1)S(1)} %slice.32.refs_0_), channel_id=1, source_target_pairs={{0,8},{8,0},{16,24},{24,16},{1,9},{9,1},{17,25},{25,17},{2,10},{10... | collective-permute-start | bytes 589832 | tf_op jit(solution)/shard_map/ppermute | solution.py:29
  434.1 7.1 %collective-permute-start.92 = (f32[8,128]{1,0:T(8,128)S(1)}, f32[8,128]{1,0:T(8,128)S(1)}, u32[]{:S(2)}, u32[]{:S(2)}) collective-permute-start(f32[8,128]{1,0:T(8,128)S(1)} %get-tuple-element.318), channel_id=1, source_target_pairs={{0,2},{1,3},{2,0},{3,1},{4,6},{5,7},{6,4},{7,5},{8,10},{9,11},{10,... | collective-permute-start | bytes 12296 | tf_op jit(solution)/shard_map/ppermute | solution.py:29
  (130 other events, 748.0 us)
Sparse Core Ops, SparseCore 0:
  19.9 75.2 all-gather.2
  97.9 72.4 all-gather.4
  250.0 100.3 reduce-scatter.1

commit v3 on v2

--- a/solution.py
+++ b/solution.py
@@ -523,25 +523,6 @@
     return call(fetching, outs, (), *operands, scratch=scratch, space=pltpu.HBM)
 
 
-def call_streaming(kernel, out, steps, *operands, vmem=20):
-    shape, kind = out
-    part = shape[0] // steps
-
-    def streaming(*refs):
-        *sources, out_ref, held, done = refs
-
-        def copy(index):
-            at = pl.ds(index * part, part)
-            return pltpu.make_async_copy(held.at[at], out_ref.at[at], done.at[index])
-
-        kernel(*sources, held, lambda index: copy(index).start())
-        for index in range(steps):
-            copy(index).wait()
-
-    scratch = [pltpu.VMEM(shape, kind), pltpu.SemaphoreType.DMA((steps,))]
-    return call(streaming, [out], (), *operands, scratch=scratch, vmem=vmem, out_space=pltpu.HBM)[0]
-
-
 def one_hot(hit):
     return jnp.where(hit, 1.0, 0.0).astype(BF)
 
@@ -980,7 +961,7 @@
 
 def feed_grad_kernel(*refs, size, rows):
     normed, (change_low, change_high, hidden_low, hidden_high) = refs[:size], refs[size : size + 4]
-    grads, (out_ref, send) = refs[size + 4 : 2 * size + 4], refs[-2:]
+    grads, out_ref = refs[size + 4 : 2 * size + 4], refs[-1]
     middle, slots = size // 2, normed[0].shape[0]
     wide = 2 * rows
 
@@ -998,7 +979,6 @@
             at = slice(part * rows, (part + 1) * rows)
             out_ref[2 * index + part, 0:rows, :] = first[at, :].astype(BF)
             out_ref[2 * index + part, rows : 2 * rows, :] = second[at, :].astype(BF)
-        send(index)
         return carry
 
     lax.fori_loop(0, out_ref.shape[0] // 2, step, 0)
@@ -1382,17 +1362,17 @@
     grad_in = finish_ctx(grad_in, near[0])
     change_high, *far = feed_backward(1, slope_high)
     sent, arrived = far_hop(far)
-    feed_grads = call_streaming(
+    feed_grads = call(
         functools.partial(feed_grad_kernel, size=size, rows=rows),
-        ((groups, 2 * rows, width), BF),
-        groups // 2,
+        [((groups, 2 * rows, width), BF)],
+        (),
         *normed_three,
         change_low,
         after(change_high, sent),
         hidden_low,
         hidden_high,
         *grad_in,
-    )
+    )[0]
     grad_cross, grad, terms_two = denormalize(after_cross, grad_ffn, near, after(arrived, feed_grads), 2)
     feed_grads = scatter_wsh(after(feed_grads, arrived).reshape(groups * 2 * rows, width))
 

time: 459 us -> 453 us (0.987)
  starting transfers between devices: 90.1 us -> 76.7 us
  waiting for transfers between devices: 171 us -> 176 us
    ppermute x95, starting transfers between devices: 90 us -> 76.5 us  [swap(): return lax.ppermute(value, axis, [(i, i ^ bit) for i in range(size)])]
  transfers between devices with their start and end apart: 98 -> 98, of which waited for: 46 -> 47; matrix products, arithmetic and copies ran while one was open for 3% -> 3% of each run, Pallas kernels for 24% -> 24%
where the time goes in v3:
time: 453 us; the launch traced here: 444 us
  waiting for transfers between devices  176 us (39%)
  Pallas kernels  122 us (27%)
  starting transfers between devices  76.7 us (17%)
  local copies, waits for them, and re-layouts  41.9 us (9%)
  between operations  15.2 us (3%)
  other arithmetic  12.6 us (3%)
    ppermute x95, waiting for transfers between devices, swap(): return lax.ppermute(value, axis, [(i, i ^ bit) for i in range(size)])  172 us
    pallas_call x39, Pallas kernels, call(): pl.pallas_call(kernel, in_specs=specs, out_specs=[pl.BlockSpec(memory_spa...  122 us
    ppermute x95, starting transfers between devices, swap(): return lax.ppermute(value, axis, [(i, i ^ bit) for i in range(size)])  76.5 us
    unnamed x195, local copies, waits for them, and re-layouts  39.9 us
  transfers between devices with their start and end apart: 98, of which 47 were waited for; matrix products, arithmetic and copies ran while one was open for 3% of the time, Pallas kernels for 24%

profile of v3, /device:TPU:0, one launch (start us, length us, event | category | flops | bytes accessed | tf_op | source)
XLA Modules:
  0.0 443.7 jit_solution(9024606298615945252)
XLA Ops:
  8.3 3.0 collective-permute-start.3
  11.3 3.5 collective-permute-done.3.refs_4_
  17.3 2.5 shard_map.296
  19.8 1.9 collective-permute-start.5
  21.7 2.4 shard_map.302
  24.1 3.4 collective-permute-done.5.refs_2_
  31.3 3.6 collective-permute-start.9
  35.1 4.8 %collective-permute-done.1.refs_2_ = bf16[256,1024]{1,0:T(8,128)(2,1)S(1)} collective-permute-done((bf16[256,1024]{1,0:T(8,128)(2,1)S(1)}, bf16[256,1024]{1,0:T(8,128)(2,1)S(1)}, u32[]{:S(2)}, u32[]{:S(2)}) %collective-permute-start.1) | collective-permute-done | bytes 524320 | tf_op jit(solution)/shard_map/ppermute | solution.py:29
  41.3 6.3 %collective-permute-done.9.refs_6_ = bf16[528,256]{1,0:T(8,128)(2,1)S(1)} collective-permute-done((bf16[528,256]{1,0:T(8,128)(2,1)S(1)}, bf16[528,256]{1,0:T(8,128)(2,1)S(1)}, u32[]{:S(2)}, u32[]{:S(2)}) %collective-permute-start.9) | collective-permute-done | bytes 270368 | tf_op jit(solution)/shard_map/ppermute | solution.py:29
  49.2 16.1 %collective-permute-done.7.refs_4_ = bf16[528,256]{1,0:T(8,128)(2,1)S(1)} collective-permute-done((bf16[528,256]{1,0:T(8,128)(2,1)S(1)}, bf16[528,256]{1,0:T(8,128)(2,1)S(1)}, u32[]{:S(2)}, u32[]{:S(2)}) %collective-permute-start.7) | collective-permute-done | bytes 270368 | tf_op jit(solution)/shard_map/ppermute | solution.py:29
  67.4 4.3 shard_map.289
  71.7 8.6 %collective-permute-done.10.refs_7_ = bf16[528,256]{1,0:T(8,128)(2,1)S(1)} collective-permute-done((bf16[528,256]{1,0:T(8,128)(2,1)S(1)}, bf16[528,256]{1,0:T(8,128)(2,1)S(1)}, u32[]{:S(2)}, u32[]{:S(2)}) %collective-permute-start.10) | collective-permute-done | bytes 270368 | tf_op jit(solution)/shard_map/ppermute | solution.py:29
  80.4 6.1 %collective-permute-done.8.refs_5_ = bf16[528,256]{1,0:T(8,128)(2,1)S(1)} collective-permute-done((bf16[528,256]{1,0:T(8,128)(2,1)S(1)}, bf16[528,256]{1,0:T(8,128)(2,1)S(1)}, u32[]{:S(2)}, u32[]{:S(2)}) %collective-permute-start.8) | collective-permute-done | bytes 270368 | tf_op jit(solution)/shard_map/ppermute | solution.py:29
  87.4 2.5 shard_map.292
  90.0 4.9 %shard_map.293 = (bf16[512,256]{1,0:T(8,128)(2,1)S(1)}, f32[2,1,1024]{2,1,0:T(1,128)S(1)}, bf16[256,1024]{1,0:T(8,128)(2,1)S(1)}, bf16[256,1024]{1,0:T(8,128)(2,1)S(1)}) custom-call(s32[9]{0:T(128)S(1)} %pad_add_fusion.2.meta, bf16[1024,256]{1,0:T(8,128)(2,1)S(1)} %get-tuple-element.174.refs_0_.refs_2_, ...), custom_call_target="tpu_custom_call" | custom-call | flops 1048576 | bytes 65536 | tf_op jit(solution)/shard_map/pallas_call | solution.py:496
  95.6 1.9 collective-permute-done.11
  97.7 3.5 shard_map.294
  104.1 12.7 %collective-permute-done.13.refs_2_ = bf16[256,1024]{1,0:T(8,128)(2,1)S(1)} collective-permute-done((bf16[256,1024]{1,0:T(8,128)(2,1)S(1)}, bf16[256,1024]{1,0:T(8,128)(2,1)S(1)}, u32[]{:S(2)}, u32[]{:S(2)}) %collective-permute-start.13) | collective-permute-done | bytes 524320 | tf_op jit(solution)/shard_map/ppermute | solution.py:29
  131.9 4.1 shard_map.298
  139.8 4.4 shard_map.299
  149.4 12.7 %collective-permute-done.22.refs_2_ = bf16[256,1024]{1,0:T(8,128)(2,1)S(1)} collective-permute-done((bf16[256,1024]{1,0:T(8,128)(2,1)S(1)}, bf16[256,1024]{1,0:T(8,128)(2,1)S(1)}, u32[]{:S(2)}, u32[]{:S(2)}) %collective-permute-start.22) | collective-permute-done | bytes 524320 | tf_op jit(solution)/shard_map/ppermute | solution.py:29
  167.3 3.1 all-gather.5.cloned.1.call-done
  170.4 2.2 copy-done
  173.6 7.1 %shard_map.303 = (bf16[512,1024]{1,0:T(8,128)(2,1)S(1)}, bf16[512,1024]{1,0:T(8,128)(2,1)S(1)}, bf16[256,1024]{1,0:T(8,128)(2,1)S(1)}, bf16[256,1024]{1,0:T(8,128)(2,1)S(1)}) custom-call(bf16[256,1024]{1,0:T(8,128)(2,1)} %get-tuple-element.193.refs_0_, bf16[256,1024]{1,0:T(8,128)(2,1)S(1)} %copy-done.36, bf16[8,256,1024]{2,1,0:T(8,128)(2,1)S(1)} %bitcast.31), custom_call_target="tpu_custom_call" | custom-call | flops 1048576 | bytes 65536 | tf_op jit(solution)/shard_map/pallas_call | solution.py:496
  183.0 7.2 %shard_map.304 = (bf16[512,1024]{1,0:T(8,128)(2,1)S(1)}, bf16[512,1024]{1,0:T(8,128)(2,1)S(1)}, bf16[256,1024]{1,0:T(8,128)(2,1)S(1)}, bf16[256,1024]{1,0:T(8,128)(2,1)S(1)}) custom-call(bf16[256,1024]{1,0:T(8,128)(2,1)} %collective-permute-done.28.refs_0_.refs_2_, bf16[256,1024]{1,0:T(8,128)(2,1)S(1)} %collective-permute-done.29.refs_1_.refs_3_, ...), custom_call_target="tpu_custom_call" | custom-call | flops 1048576 | bytes 65536 | tf_op jit(solution)/shard_map/pallas_call | solution.py:496
  190.8 4.5 %collective-permute-done.24.refs_2_ = bf16[256,1024]{1,0:T(8,128)(2,1)S(1)} collective-permute-done((bf16[256,1024]{1,0:T(8,128)(2,1)S(1)}, bf16[256,1024]{1,0:T(8,128)(2,1)S(1)}, u32[]{:S(2)}, u32[]{:S(2)}) %collective-permute-start.24) | collective-permute-done | bytes 524320 | tf_op jit(solution)/shard_map/ppermute | solution.py:29
  198.7 11.1 %collective-permute-done.31.refs_2_ = bf16[256,1024]{1,0:T(8,128)(2,1)S(1)} collective-permute-done((bf16[256,1024]{1,0:T(8,128)(2,1)S(1)}, bf16[256,1024]{1,0:T(8,128)(2,1)S(1)}, u32[]{:S(2)}, u32[]{:S(2)}) %collective-permute-start.31) | collective-permute-done | bytes 524320 | tf_op jit(solution)/shard_map/ppermute | solution.py:29
  214.1 5.4 %shard_map.306 = (bf16[512,1024]{1,0:T(8,128)(2,1)S(1)}, bf16[256,1024]{1,0:T(8,128)(2,1)S(1)}, bf16[256,1024]{1,0:T(8,128)(2,1)S(1)}) custom-call(bf16[256,1024]{1,0:T(8,128)(2,1)S(1)} %get-tuple-element.203.refs_0_.refs_8_, bf16[256,1024]{1,0:T(8,128)(2,1)S(1)} %collective-permute-done.32.refs_1_.refs_9_, bf16[8,256,1024]{2,1,0:T(8,128)(2,1)S(1)} %bitcast.33, ...), custom_call_target="tpu_custom_call" | custom-call | flops 1048576 | bytes 65536 | tf_op jit(solution)/shard_map/pallas_call | solution.py:496
  220.3 6.2 %collective-permute-done.34.refs_0_.refs_10_ = bf16[256,1024]{1,0:T(8,128)(2,1)S(1)} collective-permute-done((bf16[256,1024]{1,0:T(8,128)(2,1)S(1)}, bf16[256,1024]{1,0:T(8,128)(2,1)S(1)}, u32[]{:S(2)}, u32[]{:S(2)}) %collective-permute-start.34) | collective-permute-done | bytes 524320 | tf_op jit(solution)/shard_map/ppermute | solution.py:29
  226.5 1.9 collective-permute-done.35.refs_1_.refs_11_
  228.5 5.4 %shard_map.307 = (bf16[512,1024]{1,0:T(8,128)(2,1)S(1)}, bf16[256,1024]{1,0:T(8,128)(2,1)S(1)}, bf16[256,1024]{1,0:T(8,128)(2,1)S(1)}) custom-call(bf16[256,1024]{1,0:T(8,128)(2,1)S(1)} %collective-permute-done.34.refs_0_.refs_10_, bf16[256,1024]{1,0:T(8,128)(2,1)S(1)} %collective-permute-done.35.refs_1_.refs_11_, bf16[8,256,1024]{2,1,0:T(8,128)(2,1)S(1)} %bitcast.34, ...), custom_call_target="tpu_custom_call" | custom-call | flops 1048576 | bytes 65536 | tf_op jit(solution)/shard_map/pallas_call | solution.py:496
  237.6 6.4 %shard_map.308 = bf16[8,256,1024]{2,1,0:T(8,128)(2,1)S(1)} custom-call(bf16[256,1024]{1,0:T(8,128)(2,1)} %get-tuple-element.193.refs_0_, bf16[256,1024]{1,0:T(8,128)(2,1)S(1)} %copy-done.37, bf16[256,1024]{1,0:T(8,128)(2,1)} %collective-permute-done.28.refs_0_.refs_2_, bf16[256,1024]{1,0:T(8,128)(2,1)S(1)} %collective-permute-done.29.refs_1_.refs_3_, ...), custom_call_target="tpu_custom_call" | custom-call | flops 1048576 | bytes 65536 | tf_op jit(solution)/shard_map/pallas_call | solution.py:496
  244.0 2.0 copy-done.2
  246.0 4.1 collective-permute-done.37.refs_2_
  251.0 2.1 collective-permute-done.33.refs_1_
  260.6 4.4 shard_map.310
  265.0 8.0 %collective-permute-done.38.refs_0_ = bf16[256,1024]{1,0:T(8,128)(2,1)S(1)} collective-permute-done((bf16[256,1024]{1,0:T(8,128)(2,1)S(1)}, bf16[256,1024]{1,0:T(8,128)(2,1)S(1)}, u32[]{:S(2)}, u32[]{:S(2)}) %collective-permute-start.38) | collective-permute-done | bytes 524320 | tf_op jit(solution)/shard_map/ppermute | solution.py:29
  274.9 5.1 %shard_map.311 = (bf16[512,256]{1,0:T(8,128)(2,1)S(1)}, f32[512,256]{1,0:T(8,128)S(1)}, f32[512,256]{1,0:T(8,128)S(1)}, f32[256,1024]{1,0:T(8,128)S(1)}, bf16[25...) custom-call(s32[9]{0:T(128)S(1)} %pad_add_fusion.3.meta, ...), custom_call_target="tpu_custom_call", output_to_operand_aliasing={{1}: (11, {}), {2}: (12, {}), {3}: (13, {})} | custom-call | flops 1048576 | bytes 65536 | tf_op jit(solution)/shard_map/pallas_call | solution.py:496
  280.0 2.0 collective-permute-done.42.refs_4_
  282.0 1.9 collective-permute-done.43
  285.7 3.3 shard_map.313
  293.3 3.7 shard_map.312
  297.1 3.0 collective-permute-done.45
  303.1 4.7 %shard_map.316 = (bf16[512,256]{1,0:T(8,128)(2,1)S(1)}, f32[1024,256]{1,0:T(8,128)S(1)}, f32[1024,256]{1,0:T(8,128)S(1)}, f32[256,1024]{1,0:T(8,128)S(1)}) custom-call(s32[9]{0:T(128)S(1)} %pad_add_fusion.2.meta, bf16[256,1024]{1,0:T(8,128)(2,1)S(1)} %get-tuple-element.251.refs_0_, bf16[256,1024]{1,0:T(8,128)(2,1)S(1)} %collective-permute-done.47.refs_1_, ...), custom_call_target="tpu_custom_call" | custom-call | flops 1048576 | bytes 65536 | tf_op jit(solution)/shard_map/pallas_call | solution.py:496
  307.8 4.6 %collective-permute-done.48 = bf16[512,256]{1,0:T(8,128)(2,1)S(1)} collective-permute-done((bf16[512,256]{1,0:T(8,128)(2,1)S(1)}, bf16[512,256]{1,0:T(8,128)(2,1)S(1)}, u32[]{:S(2)}, u32[]{:S(2)}) %collective-permute-start.48) | collective-permute-done | bytes 262176 | tf_op jit(solution)/shard_map/ppermute | solution.py:29
  312.4 3.1 collective-permute-done.46.refs_0_
  317.5 6.4 %shard_map.317 = (bf16[512,256]{1,0:T(8,128)(2,1)S(1)}, f32[1024,256]{1,0:T(8,128)S(1)}, f32[1024,256]{1,0:T(8,128)S(1)}, f32[256,1024]{1,0:T(8,128)S(1)}) custom-call(s32[9]{0:T(128)S(1)} %pad_add_fusion.2.meta, bf16[256,1024]{1,0:T(8,128)(2,1)S(1)} %collective-permute-done.46.refs_0_, ...), custom_call_target="tpu_custom_call", output_to_operand_aliasing={{1}: (10, {}), {2}: (11, {}), {3}: (12, {})} | custom-call | flops 1048576 | bytes 65536 | tf_op jit(solution)/shard_map/pallas_call | solution.py:496
  324.2 2.1 collective-permute-done.55
  327.8 8.5 %collective-permute-done.52.refs_5_ = bf16[128,1024]{1,0:T(8,128)(2,1)} collective-permute-done((bf16[128,1024]{1,0:T(8,128)(2,1)S(1)}, bf16[128,1024]{1,0:T(8,128)(2,1)}, u32[]{:S(2)}, u32[]{:S(2)}) %collective-permute-start.52) | collective-permute-done | bytes 262176 | tf_op jit(solution)/shard_map/ppermute | solution.py:29
  336.3 2.6 shard_map.318
  343.1 7.3 %collective-permute-start.68 = (bf16[512,256]{1,0:T(8,128)(2,1)}, bf16[512,256]{1,0:T(8,128)(2,1)}, u32[]{:S(2)}, u32[]{:S(2)}) collective-permute-start(bf16[512,256]{1,0:T(8,128)(2,1)} %add_convert_fusion.12), channel_id=1, source_target_pairs={{0,2},{1,3},{2,0},{3,1},{4,6},{5,7},{6,4},{7,5},{8,10},{9,11},{10,... | collective-permute-start | bytes 786440 | tf_op jit(solution)/shard_map/ppermute | solution.py:29
  351.2 2.0 shard_map.321
  357.6 2.4 collective-permute-done.63
  368.9 5.2 %collective-permute-start.75 = (bf16[512,256]{1,0:T(8,128)(2,1)}, bf16[512,256]{1,0:T(8,128)(2,1)}, u32[]{:S(2)}, u32[]{:S(2)}) collective-permute-start(bf16[512,256]{1,0:T(8,128)(2,1)} %add_convert_fusion.10), channel_id=1, source_target_pairs={{0,2},{1,3},{2,0},{3,1},{4,6},{5,7},{6,4},{7,5},{8,10},{9,11},{10,... | collective-permute-start | bytes 786440 | tf_op jit(solution)/shard_map/ppermute | solution.py:29
  375.7 2.2 collective-permute-start.62
  382.8 4.3 shard_map.323
  387.7 3.4 collective-permute-done.76
  395.6 3.8 shard_map.324
  400.7 4.8 %collective-permute-done.81 = bf16[256,256]{1,0:T(8,128)(2,1)S(1)} collective-permute-done((bf16[256,256]{1,0:T(8,128)(2,1)S(1)}, bf16[256,256]{1,0:T(8,128)(2,1)S(1)}, u32[]{:S(2)}, u32[]{:S(2)}) %collective-permute-start.81) | collective-permute-done | bytes 131104 | tf_op jit(solution)/shard_map/ppermute | solution.py:29
  407.7 2.5 shard_map.325
  410.7 2.6 collective-permute-done.78.refs_2_
  414.9 2.2 collective-permute-done.73
  424.6 2.4 collective-permute-start.92
  431.5 2.4 collective-permute-done.94
  (426 shorter events, 135.6 us)
Async XLA Ops:
  7.2 116.9 %all-gather.3.cloned.1.call-start = ((), (), s32[]{:S(2)}) async-start(), calls=%async_computation.1 | async-start | bytes 2359296 | tf_op jit(solution)/shard_map/all_gather | solution.py:255
  19.8 150.6 %all-gather.5.cloned.1.call-start = ((), (), s32[]{:S(2)}) async-start(), calls=%async_computation.2 | async-start | bytes 4718592 | tf_op jit(solution)/shard_map/all_gather | solution.py:255
  19.8 7.7 %collective-permute-start.5 = (bf16[528,256]{1,0:T(8,128)(2,1)S(1)}, bf16[528,256]{1,0:T(8,128)(2,1)S(1)}, u32[]{:S(2)}, u32[]{:S(2)}) collective-permute-start(bf16[528,256]{1,0:T(8,128)(2,1)S(1)} %shard_map.291.refs_0_), channel_id=1, source_target_pairs={{0,2},{1,3},{2,0},{3,1},{4,6},{5,7},{6,4},{7,5},{8,10},{9,11},{10,... | collective-permute-start | bytes 811016 | tf_op jit(solution)/shard_map/ppermute | solution.py:29
  27.6 328.8 %reduce-scatter.2.cloned.1.call-start = ((), (), s32[]{:S(2)}) async-start(), calls=%async_computation.3 | async-start | bytes 4718592 | tf_op jit(solution)/shard_map/reduce_scatter | solution.py:259
  27.7 12.2 %collective-permute-start.1 = (bf16[256,1024]{1,0:T(8,128)(2,1)S(1)}, bf16[256,1024]{1,0:T(8,128)(2,1)S(1)}, u32[]{:S(2)}, u32[]{:S(2)}) collective-permute-start(bf16[256,1024]{1,0:T(8,128)(2,1)S(1)} %bitcast.42), channel_id=1, source_target_pairs={{0,16},{8,24},{16,0},{24,8},{1,17},{9,25},{17,1},{25,9},{2,18},{10... | collective-permute-start | bytes 1572872 | tf_op jit(solution)/shard_map/ppermute | solution.py:29
  29.1 37.7 %collective-permute-start = (bf16[256,1024]{1,0:T(8,128)(2,1)S(1)}, bf16[256,1024]{1,0:T(8,128)(2,1)S(1)}, u32[]{:S(2)}, u32[]{:S(2)}) collective-permute-start(bf16[256,1024]{1,0:T(8,128)(2,1)S(1)} %bitcast.43), channel_id=1, source_target_pairs={{0,8},{8,0},{16,24},{24,16},{1,9},{9,1},{17,25},{25,17},{2,10},{10... | collective-permute-start | bytes 1572872 | tf_op jit(solution)/shard_map/ppermute | solution.py:29
  31.3 16.4 %collective-permute-start.9 = (bf16[528,256]{1,0:T(8,128)(2,1)S(1)}, bf16[528,256]{1,0:T(8,128)(2,1)S(1)}, u32[]{:S(2)}, u32[]{:S(2)}) collective-permute-start(bf16[528,256]{1,0:T(8,128)(2,1)S(1)} %shard_map.291.refs_0_), channel_id=1, source_target_pairs={{0,6},{1,7},{2,4},{3,5},{4,2},{5,3},{6,0},{7,1},{8,14},{9,15},{10,... | collective-permute-start | bytes 811016 | tf_op jit(solution)/shard_map/ppermute | solution.py:29
  34.9 30.4 %collective-permute-start.7 = (bf16[528,256]{1,0:T(8,128)(2,1)S(1)}, bf16[528,256]{1,0:T(8,128)(2,1)S(1)}, u32[]{:S(2)}, u32[]{:S(2)}) collective-permute-start(bf16[528,256]{1,0:T(8,128)(2,1)S(1)} %shard_map.291.refs_0_), channel_id=1, source_target_pairs={{0,4},{1,5},{2,6},{3,7},{4,0},{5,1},{6,2},{7,3},{8,12},{9,13},{10,... | collective-permute-start | bytes 811016 | tf_op jit(solution)/shard_map/ppermute | solution.py:29
  39.9 27.5 %collective-permute-start.2 = (bf16[256,1024]{1,0:T(8,128)(2,1)S(1)}, bf16[256,1024]{1,0:T(8,128)(2,1)S(1)}, u32[]{:S(2)}, u32[]{:S(2)}) collective-permute-start(bf16[256,1024]{1,0:T(8,128)(2,1)S(1)} %collective-permute-done.1.refs_2_), channel_id=1, source_target_pairs={{0,8},{8,0},{16,24},{24,16},{1,9},{9,1},{17,25},{25,17},{2,10},{10... | collective-permute-start | bytes 1572872 | tf_op jit(solution)/shard_map/ppermute | solution.py:29
  40.2 31.6 %collective-permute-start.4 = (bf16[528,256]{1,0:T(8,128)(2,1)S(1)}, bf16[528,256]{1,0:T(8,128)(2,1)S(1)}, u32[]{:S(2)}, u32[]{:S(2)}) collective-permute-start(bf16[528,256]{1,0:T(8,128)(2,1)S(1)} %shard_map.291.refs_0_), channel_id=1, source_target_pairs={{0,1},{1,0},{2,3},{3,2},{4,5},{5,4},{6,7},{7,6},{8,9},{9,8},{10,11... | collective-permute-start | bytes 811016 | tf_op jit(solution)/shard_map/ppermute | solution.py:29
  47.6 24.1 %collective-permute-start.6 = (bf16[528,256]{1,0:T(8,128)(2,1)S(1)}, bf16[528,256]{1,0:T(8,128)(2,1)S(1)}, u32[]{:S(2)}, u32[]{:S(2)}) collective-permute-start(bf16[528,256]{1,0:T(8,128)(2,1)S(1)} %collective-permute-done.5.refs_2_), channel_id=1, source_target_pairs={{0,1},{1,0},{2,3},{3,2},{4,5},{5,4},{6,7},{7,6},{8,9},{9,8},{10,11... | collective-permute-start | bytes 811016 | tf_op jit(solution)/shard_map/ppermute | solution.py:29
  65.3 15.1 %collective-permute-start.10 = (bf16[528,256]{1,0:T(8,128)(2,1)S(1)}, bf16[528,256]{1,0:T(8,128)(2,1)S(1)}, u32[]{:S(2)}, u32[]{:S(2)}) collective-permute-start(bf16[528,256]{1,0:T(8,128)(2,1)S(1)} %collective-permute-done.9.refs_6_), channel_id=1, source_target_pairs={{0,1},{1,0},{2,3},{3,2},{4,5},{5,4},{6,7},{7,6},{8,9},{9,8},{10,11... | collective-permute-start | bytes 811016 | tf_op jit(solution)/shard_map/ppermute | solution.py:29
  66.8 19.7 %collective-permute-start.8 = (bf16[528,256]{1,0:T(8,128)(2,1)S(1)}, bf16[528,256]{1,0:T(8,128)(2,1)S(1)}, u32[]{:S(2)}, u32[]{:S(2)}) collective-permute-start(bf16[528,256]{1,0:T(8,128)(2,1)S(1)} %collective-permute-done.7.refs_4_), channel_id=1, source_target_pairs={{0,1},{1,0},{2,3},{3,2},{4,5},{5,4},{6,7},{7,6},{8,9},{9,8},{10,11... | collective-permute-start | bytes 811016 | tf_op jit(solution)/shard_map/ppermute | solution.py:29
  102.0 14.8 %collective-permute-start.13 = (bf16[256,1024]{1,0:T(8,128)(2,1)S(1)}, bf16[256,1024]{1,0:T(8,128)(2,1)S(1)}, u32[]{:S(2)}, u32[]{:S(2)}) collective-permute-start(bf16[256,1024]{1,0:T(8,128)(2,1)S(1)} %add_convert_fusion.5), channel_id=1, source_target_pairs={{0,16},{8,24},{16,0},{24,8},{1,17},{9,25},{17,1},{25,9},{2,18},{10... | collective-permute-start | bytes 1572872 | tf_op jit(solution)/shard_map/ppermute | solution.py:29
  103.5 18.3 %collective-permute-start.16 = (bf16[128,1024]{1,0:T(8,128)(2,1)S(1)}, bf16[128,1024]{1,0:T(8,128)(2,1)S(1)}, u32[]{:S(2)}, u32[]{:S(2)}) collective-permute-start(bf16[128,1024]{1,0:T(8,128)(2,1)S(1)} %bitcast.36), channel_id=1, source_target_pairs={{0,16},{8,24},{16,0},{24,8},{1,17},{9,25},{17,1},{25,9},{2,18},{10... | collective-permute-start | bytes 786440 | tf_op jit(solution)/shard_map/ppermute | solution.py:29
  119.1 12.9 %collective-permute-start.14 = (bf16[256,1024]{1,0:T(8,128)(2,1)}, bf16[256,1024]{1,0:T(8,128)(2,1)}, u32[]{:S(2)}, u32[]{:S(2)}) collective-permute-start(bf16[256,1024]{1,0:T(8,128)(2,1)} %get-tuple-element.178.refs_0_), channel_id=1, source_target_pairs={{0,8},{8,0},{16,24},{24,16},{1,9},{9,1},{17,25},{25,17},{2,10},{10... | collective-permute-start | bytes 1572872 | tf_op jit(solution)/shard_map/ppermute | solution.py:29
  119.1 18.4 %collective-permute-start.19 = (bf16[256,1024]{1,0:T(8,128)(2,1)}, bf16[256,1024]{1,0:T(8,128)(2,1)}, u32[]{:S(2)}, u32[]{:S(2)}) collective-permute-start(bf16[256,1024]{1,0:T(8,128)(2,1)} %get-tuple-element.178.refs_0_), channel_id=1, source_target_pairs={{0,16},{8,24},{16,0},{24,8},{1,17},{9,25},{17,1},{25,9},{2,18},{10... | collective-permute-start | bytes 1572872 | tf_op jit(solution)/shard_map/ppermute | solution.py:29
  147.8 14.3 %collective-permute-start.22 = (bf16[256,1024]{1,0:T(8,128)(2,1)S(1)}, bf16[256,1024]{1,0:T(8,128)(2,1)S(1)}, u32[]{:S(2)}, u32[]{:S(2)}) collective-permute-start(bf16[256,1024]{1,0:T(8,128)(2,1)S(1)} %add_convert_fusion.4), channel_id=1, source_target_pairs={{0,16},{8,24},{16,0},{24,8},{1,17},{9,25},{17,1},{25,9},{2,18},{10... | collective-permute-start | bytes 1572872 | tf_op jit(solution)/shard_map/ppermute | solution.py:29
  164.4 16.4 %collective-permute-start.28 = (bf16[256,1024]{1,0:T(8,128)(2,1)}, bf16[256,1024]{1,0:T(8,128)(2,1)}, u32[]{:S(2)}, u32[]{:S(2)}) collective-permute-start(bf16[256,1024]{1,0:T(8,128)(2,1)} %get-tuple-element.193.refs_0_), channel_id=1, source_target_pairs={{0,16},{8,24},{16,0},{24,8},{1,17},{9,25},{17,1},{25,9},{2,18},{10... | collective-permute-start | bytes 1572872 | tf_op jit(solution)/shard_map/ppermute | solution.py:29
  180.9 14.3 %collective-permute-start.24 = (bf16[256,1024]{1,0:T(8,128)(2,1)S(1)}, bf16[256,1024]{1,0:T(8,128)(2,1)S(1)}, u32[]{:S(2)}, u32[]{:S(2)}) collective-permute-start(bf16[256,1024]{1,0:T(8,128)(2,1)S(1)} %bitcast.45), channel_id=1, source_target_pairs={{0,16},{8,24},{16,0},{24,8},{1,17},{9,25},{17,1},{25,9},{2,18},{10... | collective-permute-start | bytes 1572872 | tf_op jit(solution)/shard_map/ppermute | solution.py:29
  190.4 7.1 %collective-permute-start.23 = (bf16[256,1024]{1,0:T(8,128)(2,1)S(1)}, bf16[256,1024]{1,0:T(8,128)(2,1)S(1)}, u32[]{:S(2)}, u32[]{:S(2)}) collective-permute-start(bf16[256,1024]{1,0:T(8,128)(2,1)S(1)} %bitcast.46), channel_id=1, source_target_pairs={{0,8},{8,0},{16,24},{24,16},{1,9},{9,1},{17,25},{25,17},{2,10},{10... | collective-permute-start | bytes 1572872 | tf_op jit(solution)/shard_map/ppermute | solution.py:29
  195.9 13.9 %collective-permute-start.31 = (bf16[256,1024]{1,0:T(8,128)(2,1)S(1)}, bf16[256,1024]{1,0:T(8,128)(2,1)S(1)}, u32[]{:S(2)}, u32[]{:S(2)}) collective-permute-start(bf16[256,1024]{1,0:T(8,128)(2,1)S(1)} %add_convert_fusion.3), channel_id=1, source_target_pairs={{0,16},{8,24},{16,0},{24,8},{1,17},{9,25},{17,1},{25,9},{2,18},{10... | collective-permute-start | bytes 1572872 | tf_op jit(solution)/shard_map/ppermute | solution.py:29
  212.2 14.3 %collective-permute-start.34 = (bf16[256,1024]{1,0:T(8,128)(2,1)S(1)}, bf16[256,1024]{1,0:T(8,128)(2,1)S(1)}, u32[]{:S(2)}, u32[]{:S(2)}) collective-permute-start(bf16[256,1024]{1,0:T(8,128)(2,1)S(1)} %get-tuple-element.203.refs_0_.refs_8_), channel_id=1, source_target_pairs={{0,16},{8,24},{16,0},{24,8},{1,17},{9,25},{17,1},{25,9},{2,18},{10... | collective-permute-start | bytes 1572872 | tf_op jit(solution)/shard_map/ppermute | solution.py:29
  236.1 14.0 %collective-permute-start.37 = (bf16[256,1024]{1,0:T(8,128)(2,1)S(1)}, bf16[256,1024]{1,0:T(8,128)(2,1)S(1)}, u32[]{:S(2)}, u32[]{:S(2)}) collective-permute-start(bf16[256,1024]{1,0:T(8,128)(2,1)S(1)} %add_convert_fusion.2), channel_id=1, source_target_pairs={{0,16},{8,24},{16,0},{24,8},{1,17},{9,25},{17,1},{25,9},{2,18},{10... | collective-permute-start | bytes 1572872 | tf_op jit(solution)/shard_map/ppermute | solution.py:29
  258.8 14.2 %collective-permute-start.38 = (bf16[256,1024]{1,0:T(8,128)(2,1)S(1)}, bf16[256,1024]{1,0:T(8,128)(2,1)S(1)}, u32[]{:S(2)}, u32[]{:S(2)}) collective-permute-start(bf16[256,1024]{1,0:T(8,128)(2,1)S(1)} %get-tuple-element.217.refs_0_), channel_id=1, source_target_pairs={{0,16},{8,24},{16,0},{24,8},{1,17},{9,25},{17,1},{25,9},{2,18},{10... | collective-permute-start | bytes 1572872 | tf_op jit(solution)/shard_map/ppermute | solution.py:29
  273.0 9.0 %collective-permute-start.42 = (bf16[128,1024]{1,0:T(8,128)(2,1)}, bf16[128,1024]{1,0:T(8,128)(2,1)}, u32[]{:S(2)}, u32[]{:S(2)}) collective-permute-start(bf16[128,1024]{1,0:T(8,128)(2,1)} %get-tuple-element.223.refs_0_), channel_id=1, source_target_pairs={{0,16},{8,24},{16,0},{24,8},{1,17},{9,25},{17,1},{25,9},{2,18},{10... | collective-permute-start | bytes 786440 | tf_op jit(solution)/shard_map/ppermute | solution.py:29
  284.1 16.0 %collective-permute-start.44 = (bf16[256,1024]{1,0:T(8,128)(2,1)S(1)}, bf16[256,1024]{1,0:T(8,128)(2,1)S(1)}, u32[]{:S(2)}, u32[]{:S(2)}) collective-permute-start(bf16[256,1024]{1,0:T(8,128)(2,1)S(1)} %add_convert_fusion.1), channel_id=1, source_target_pairs={{0,16},{8,24},{16,0},{24,8},{1,17},{9,25},{17,1},{25,9},{2,18},{10... | collective-permute-start | bytes 1572872 | tf_op jit(solution)/shard_map/ppermute | solution.py:29
  285.7 14.5 %collective-permute-start.40 = (bf16[256,1024]{1,0:T(8,128)(2,1)S(1)}, bf16[256,1024]{1,0:T(8,128)(2,1)S(1)}, u32[]{:S(2)}, u32[]{:S(2)}) collective-permute-start(bf16[256,1024]{1,0:T(8,128)(2,1)S(1)} %get-tuple-element.226), channel_id=1, source_target_pairs={{0,8},{8,0},{16,24},{24,16},{1,9},{9,1},{17,25},{25,17},{2,10},{10... | collective-permute-start | bytes 1572872 | tf_op jit(solution)/shard_map/ppermute | solution.py:29
  289.0 11.1 %collective-permute-start.45 = (bf16[512,256]{1,0:T(8,128)(2,1)S(1)}, bf16[512,256]{1,0:T(8,128)(2,1)S(1)}, u32[]{:S(2)}, u32[]{:S(2)}) collective-permute-start(bf16[512,256]{1,0:T(8,128)(2,1)S(1)} %get-tuple-element.243), channel_id=1, source_target_pairs={{0,1},{1,0},{2,3},{3,2},{4,5},{5,4},{6,7},{7,6},{8,9},{9,8},{10,11... | collective-permute-start | bytes 786440 | tf_op jit(solution)/shard_map/ppermute | solution.py:29
  301.2 14.3 %collective-permute-start.46 = (bf16[256,1024]{1,0:T(8,128)(2,1)S(1)}, bf16[256,1024]{1,0:T(8,128)(2,1)S(1)}, u32[]{:S(2)}, u32[]{:S(2)}) collective-permute-start(bf16[256,1024]{1,0:T(8,128)(2,1)S(1)} %get-tuple-element.251.refs_0_), channel_id=1, source_target_pairs={{0,16},{8,24},{16,0},{24,8},{1,17},{9,25},{17,1},{25,9},{2,18},{10... | collective-permute-start | bytes 1572872 | tf_op jit(solution)/shard_map/ppermute | solution.py:29
  301.2 11.1 %collective-permute-start.48 = (bf16[512,256]{1,0:T(8,128)(2,1)S(1)}, bf16[512,256]{1,0:T(8,128)(2,1)S(1)}, u32[]{:S(2)}, u32[]{:S(2)}) collective-permute-start(bf16[512,256]{1,0:T(8,128)(2,1)S(1)} %get-tuple-element.255), channel_id=1, source_target_pairs={{0,1},{1,0},{2,3},{3,2},{4,5},{5,4},{6,7},{7,6},{8,9},{9,8},{10,11... | collective-permute-start | bytes 786440 | tf_op jit(solution)/shard_map/ppermute | solution.py:29
  315.5 8.7 %collective-permute-start.54 = (bf16[512,256]{1,0:T(8,128)(2,1)S(1)}, bf16[512,256]{1,0:T(8,128)(2,1)S(1)}, u32[]{:S(2)}, u32[]{:S(2)}) collective-permute-start(bf16[512,256]{1,0:T(8,128)(2,1)S(1)} %get-tuple-element.270), channel_id=1, source_target_pairs={{0,1},{1,0},{2,3},{3,2},{4,5},{5,4},{6,7},{7,6},{8,9},{9,8},{10,11... | collective-permute-start | bytes 786440 | tf_op jit(solution)/shard_map/ppermute | solution.py:29
  316.0 10.3 %collective-permute-start.55 = (bf16[512,256]{1,0:T(8,128)(2,1)S(1)}, bf16[512,256]{1,0:T(8,128)(2,1)S(1)}, u32[]{:S(2)}, u32[]{:S(2)}) collective-permute-start(bf16[512,256]{1,0:T(8,128)(2,1)S(1)} %add_convert_fusion.14), channel_id=1, source_target_pairs={{0,6},{1,7},{2,4},{3,5},{4,2},{5,3},{6,0},{7,1},{8,14},{9,15},{10,... | collective-permute-start | bytes 786440 | tf_op jit(solution)/shard_map/ppermute | solution.py:29
  327.4 11.6 %collective-permute-start.56 = (bf16[256,1024]{1,0:T(8,128)(2,1)S(1)}, bf16[256,1024]{1,0:T(8,128)(2,1)S(1)}, u32[]{:S(2)}, u32[]{:S(2)}) collective-permute-start(bf16[256,1024]{1,0:T(8,128)(2,1)S(1)} %get-tuple-element.277), channel_id=1, source_target_pairs={{0,8},{8,0},{16,24},{24,16},{1,9},{9,1},{17,25},{25,17},{2,10},{10... | collective-permute-start | bytes 1572872 | tf_op jit(solution)/shard_map/ppermute | solution.py:29
  327.4 8.8 %collective-permute-start.52 = (bf16[128,1024]{1,0:T(8,128)(2,1)S(1)}, bf16[128,1024]{1,0:T(8,128)(2,1)}, u32[]{:S(2)}, u32[]{:S(2)}) collective-permute-start(bf16[128,1024]{1,0:T(8,128)(2,1)S(1)} %copy-done.61), channel_id=1, source_target_pairs={{0,16},{8,24},{16,0},{24,8},{1,17},{9,25},{17,1},{25,9},{2,18},{10... | collective-permute-start | bytes 786440 | tf_op jit(solution)/shard_map/ppermute | solution.py:29
  339.1 14.1 %collective-permute-start.58 = (bf16[256,1024]{1,0:T(8,128)(2,1)S(1)}, bf16[256,1024]{1,0:T(8,128)(2,1)S(1)}, u32[]{:S(2)}, u32[]{:S(2)}) collective-permute-start(bf16[256,1024]{1,0:T(8,128)(2,1)S(1)} %add_convert_fusion), channel_id=1, source_target_pairs={{0,16},{8,24},{16,0},{24,8},{1,17},{9,25},{17,1},{25,9},{2,18},{10... | collective-permute-start | bytes 1572872 | tf_op jit(solution)/shard_map/ppermute | solution.py:29
  340.5 12.8 %collective-permute-start.57 = (bf16[256,1024]{1,0:T(8,128)(2,1)S(1)}, bf16[256,1024]{1,0:T(8,128)(2,1)S(1)}, u32[]{:S(2)}, u32[]{:S(2)}) collective-permute-start(bf16[256,1024]{1,0:T(8,128)(2,1)S(1)} %get-tuple-element.281), channel_id=1, source_target_pairs={{0,8},{8,0},{16,24},{24,16},{1,9},{9,1},{17,25},{25,17},{2,10},{10... | collective-permute-start | bytes 1572872 | tf_op jit(solution)/shard_map/ppermute | solution.py:29
  340.6 9.9 %collective-permute-start.53 = (bf16[512,256]{1,0:T(8,128)(2,1)S(1)}, bf16[512,256]{1,0:T(8,128)(2,1)S(1)}, u32[]{:S(2)}, u32[]{:S(2)}) collective-permute-start(bf16[512,256]{1,0:T(8,128)(2,1)S(1)} %get-tuple-element.268), channel_id=1, source_target_pairs={{0,1},{1,0},{2,3},{3,2},{4,5},{5,4},{6,7},{7,6},{8,9},{9,8},{10,11... | collective-permute-start | bytes 786440 | tf_op jit(solution)/shard_map/ppermute | solution.py:29
  342.2 14.2 %collective-permute-start.49 = (bf16[128,1024]{1,0:T(8,128)(2,1)}, bf16[128,1024]{1,0:T(8,128)(2,1)S(1)}, u32[]{:S(2)}, u32[]{:S(2)}) collective-permute-start(bf16[128,1024]{1,0:T(8,128)(2,1)} %get-tuple-element.223.refs_0_), channel_id=1, source_target_pairs={{0,8},{8,0},{16,24},{24,16},{1,9},{9,1},{17,25},{25,17},{2,10},{10... | collective-permute-start | bytes 786440 | tf_op jit(solution)/shard_map/ppermute | solution.py:29
  343.1 14.4 %collective-permute-start.68 = (bf16[512,256]{1,0:T(8,128)(2,1)}, bf16[512,256]{1,0:T(8,128)(2,1)}, u32[]{:S(2)}, u32[]{:S(2)}) collective-permute-start(bf16[512,256]{1,0:T(8,128)(2,1)} %add_convert_fusion.12), channel_id=1, source_target_pairs={{0,2},{1,3},{2,0},{3,1},{4,6},{5,7},{6,4},{7,5},{8,10},{9,11},{10,... | collective-permute-start | bytes 786440 | tf_op jit(solution)/shard_map/ppermute | solution.py:29
  350.5 9.5 %collective-permute-start.63 = (bf16[512,256]{1,0:T(8,128)(2,1)}, bf16[512,256]{1,0:T(8,128)(2,1)}, u32[]{:S(2)}, u32[]{:S(2)}) collective-permute-start(bf16[512,256]{1,0:T(8,128)(2,1)} %get-tuple-element.289), channel_id=1, source_target_pairs={{0,1},{1,0},{2,3},{3,2},{4,5},{5,4},{6,7},{7,6},{8,9},{9,8},{10,11... | collective-permute-start | bytes 786440 | tf_op jit(solution)/shard_map/ppermute | solution.py:29
  353.2 9.1 %collective-permute-start.50 = (bf16[128,1024]{1,0:T(8,128)(2,1)S(1)}, bf16[128,1024]{1,0:T(8,128)(2,1)S(1)}, u32[]{:S(2)}, u32[]{:S(2)}) collective-permute-start(bf16[128,1024]{1,0:T(8,128)(2,1)S(1)} %copy-done.61), channel_id=1, source_target_pairs={{0,8},{8,0},{16,24},{24,16},{1,9},{9,1},{17,25},{25,17},{2,10},{10... | collective-permute-start | bytes 786440 | tf_op jit(solution)/shard_map/ppermute | solution.py:29
  353.3 12.1 %collective-permute-start.67 = (bf16[512,256]{1,0:T(8,128)(2,1)}, bf16[512,256]{1,0:T(8,128)(2,1)}, u32[]{:S(2)}, u32[]{:S(2)}) collective-permute-start(bf16[512,256]{1,0:T(8,128)(2,1)} %get-tuple-element.293), channel_id=1, source_target_pairs={{0,1},{1,0},{2,3},{3,2},{4,5},{5,4},{6,7},{7,6},{8,9},{9,8},{10,11... | collective-permute-start | bytes 786440 | tf_op jit(solution)/shard_map/ppermute | solution.py:29
  356.4 11.8 %collective-permute-start.60 = (bf16[128,1024]{1,0:T(8,128)(2,1)}, bf16[128,1024]{1,0:T(8,128)(2,1)S(1)}, u32[]{:S(2)}, u32[]{:S(2)}) collective-permute-start(bf16[128,1024]{1,0:T(8,128)(2,1)} %collective-permute-done.52.refs_5_), channel_id=1, source_target_pairs={{0,8},{8,0},{16,24},{24,16},{1,9},{9,1},{17,25},{25,17},{2,10},{10... | collective-permute-start | bytes 786440 | tf_op jit(solution)/shard_map/ppermute | solution.py:29
  357.6 16.5 %collective-permute-start.59 = (bf16[128,1024]{1,0:T(8,128)(2,1)}, bf16[128,1024]{1,0:T(8,128)(2,1)S(1)}, u32[]{:S(2)}, u32[]{:S(2)}) collective-permute-start(bf16[128,1024]{1,0:T(8,128)(2,1)} %collective-permute-done.42.refs_4_), channel_id=1, source_target_pairs={{0,8},{8,0},{16,24},{24,16},{1,9},{9,1},{17,25},{25,17},{2,10},{10... | collective-permute-start | bytes 786440 | tf_op jit(solution)/shard_map/ppermute | solution.py:29
  359.9 15.8 %collective-permute-start.66 = (bf16[256,1024]{1,0:T(8,128)(2,1)}, bf16[256,1024]{1,0:T(8,128)(2,1)}, u32[]{:S(2)}, u32[]{:S(2)}) collective-permute-start(bf16[256,1024]{1,0:T(8,128)(2,1)} %reduce-scatter.2.cloned.1.call-done.refs_0_), channel_id=1, source_target_pairs={{0,16},{8,24},{16,0},{24,8},{1,17},{9,25},{17,1},{25,9},{2,18},{10... | collective-permute-start | bytes 1572872 | tf_op jit(solution)/shard_map/ppermute | solution.py:29
  363.0 24.1 %collective-permute-start.74 = (bf16[512,256]{1,0:T(8,128)(2,1)}, bf16[512,256]{1,0:T(8,128)(2,1)}, u32[]{:S(2)}, u32[]{:S(2)}) collective-permute-start(bf16[512,256]{1,0:T(8,128)(2,1)} %copy-done.88), channel_id=1, source_target_pairs={{0,1},{1,0},{2,3},{3,2},{4,5},{5,4},{6,7},{7,6},{8,9},{9,8},{10,11... | collective-permute-start | bytes 786440 | tf_op jit(solution)/shard_map/ppermute | solution.py:29
  365.4 21.7 %collective-permute-start.64 = (bf16[512,256]{1,0:T(8,128)(2,1)}, bf16[512,256]{1,0:T(8,128)(2,1)}, u32[]{:S(2)}, u32[]{:S(2)}) collective-permute-start(bf16[512,256]{1,0:T(8,128)(2,1)} %add_convert_fusion.13), channel_id=1, source_target_pairs={{0,6},{1,7},{2,4},{3,5},{4,2},{5,3},{6,0},{7,1},{8,14},{9,15},{10,... | collective-permute-start | bytes 786440 | tf_op jit(solution)/shard_map/ppermute | solution.py:29
  368.9 18.7 %collective-permute-start.75 = (bf16[512,256]{1,0:T(8,128)(2,1)}, bf16[512,256]{1,0:T(8,128)(2,1)}, u32[]{:S(2)}, u32[]{:S(2)}) collective-permute-start(bf16[512,256]{1,0:T(8,128)(2,1)} %add_convert_fusion.10), channel_id=1, source_target_pairs={{0,2},{1,3},{2,0},{3,1},{4,6},{5,7},{6,4},{7,5},{8,10},{9,11},{10,... | collective-permute-start | bytes 786440 | tf_op jit(solution)/shard_map/ppermute | solution.py:29
  374.8 16.2 %collective-permute-start.76 = (bf16[512,256]{1,0:T(8,128)(2,1)}, bf16[512,256]{1,0:T(8,128)(2,1)}, u32[]{:S(2)}, u32[]{:S(2)}) collective-permute-start(bf16[512,256]{1,0:T(8,128)(2,1)} %add_convert_fusion.9), channel_id=1, source_target_pairs={{0,4},{1,5},{2,6},{3,7},{4,0},{5,1},{6,2},{7,3},{8,12},{9,13},{10,... | collective-permute-start | bytes 786440 | tf_op jit(solution)/shard_map/ppermute | solution.py:29
  375.7 23.7 %collective-permute-start.62 = (bf16[272,1024]{1,0:T(8,128)(2,1)S(1)}, bf16[272,1024]{1,0:T(8,128)(2,1)S(1)}, u32[]{:S(2)}, u32[]{:S(2)}) collective-permute-start(bf16[272,1024]{1,0:T(8,128)(2,1)S(1)} %shard_map.322.refs_0_), channel_id=1, source_target_pairs={{0,16},{8,24},{16,0},{24,8},{1,17},{9,25},{17,1},{25,9},{2,18},{10... | collective-permute-start | bytes 1671176 | tf_op jit(solution)/shard_map/ppermute | solution.py:29
  387.1 7.2 %collective-permute-start.65 = (bf16[256,1024]{1,0:T(8,128)(2,1)S(1)}, bf16[256,1024]{1,0:T(8,128)(2,1)}, u32[]{:S(2)}, u32[]{:S(2)}) collective-permute-start(bf16[256,1024]{1,0:T(8,128)(2,1)S(1)} %copy-done.51), channel_id=1, source_target_pairs={{0,8},{8,0},{16,24},{24,16},{1,9},{9,1},{17,25},{25,17},{2,10},{10... | collective-permute-start | bytes 1572872 | tf_op jit(solution)/shard_map/ppermute | solution.py:29
  387.1 8.5 %collective-permute-start.69 = (bf16[256,1024]{1,0:T(8,128)(2,1)}, bf16[256,1024]{1,0:T(8,128)(2,1)}, u32[]{:S(2)}, u32[]{:S(2)}) collective-permute-start(bf16[256,1024]{1,0:T(8,128)(2,1)} %collective-permute-done.66.refs_2_), channel_id=1, source_target_pairs={{0,8},{8,0},{16,24},{24,16},{1,9},{9,1},{17,25},{25,17},{2,10},{10... | collective-permute-start | bytes 1572872 | tf_op jit(solution)/shard_map/ppermute | solution.py:29
  387.6 12.3 %collective-permute-start.72 = (bf16[128,1024]{1,0:T(8,128)(2,1)}, bf16[128,1024]{1,0:T(8,128)(2,1)S(1)}, u32[]{:S(2)}, u32[]{:S(2)}) collective-permute-start(bf16[128,1024]{1,0:T(8,128)(2,1)} %copy-done.87), channel_id=1, source_target_pairs={{0,8},{8,0},{16,24},{24,16},{1,9},{9,1},{17,25},{25,17},{2,10},{10... | collective-permute-start | bytes 786440 | tf_op jit(solution)/shard_map/ppermute | solution.py:29
  394.3 15.9 %collective-permute-start.83 = (bf16[512,256]{1,0:T(8,128)(2,1)}, bf16[512,256]{1,0:T(8,128)(2,1)S(1)}, u32[]{:S(2)}, u32[]{:S(2)}) collective-permute-start(bf16[512,256]{1,0:T(8,128)(2,1)} %copy-done.86), channel_id=1, source_target_pairs={{0,1},{1,0},{2,3},{3,2},{4,5},{5,4},{6,7},{7,6},{8,9},{9,8},{10,11... | collective-permute-start | bytes 786440 | tf_op jit(solution)/shard_map/ppermute | solution.py:29
  395.6 14.7 %collective-permute-start.84 = (bf16[512,256]{1,0:T(8,128)(2,1)S(1)}, bf16[512,256]{1,0:T(8,128)(2,1)S(1)}, u32[]{:S(2)}, u32[]{:S(2)}) collective-permute-start(bf16[512,256]{1,0:T(8,128)(2,1)S(1)} %add_convert_fusion.7), channel_id=1, source_target_pairs={{0,4},{1,5},{2,6},{3,7},{4,0},{5,1},{6,2},{7,3},{8,12},{9,13},{10,... | collective-permute-start | bytes 786440 | tf_op jit(solution)/shard_map/ppermute | solution.py:29
  405.5 7.8 %collective-permute-start.78 = (bf16[384,256]{1,0:T(8,128)(2,1)S(1)}, bf16[384,256]{1,0:T(8,128)(2,1)S(1)}, u32[]{:S(2)}, u32[]{:S(2)}) collective-permute-start(bf16[384,256]{1,0:T(8,128)(2,1)S(1)} %slice.30.refs_0_), channel_id=1, source_target_pairs={{0,16},{8,24},{16,0},{24,8},{1,17},{9,25},{17,1},{25,9},{2,18},{10... | collective-permute-start | bytes 589832 | tf_op jit(solution)/shard_map/ppermute | solution.py:29
  406.2 8.3 %collective-permute-start.71 = (bf16[128,1024]{1,0:T(8,128)(2,1)S(1)}, bf16[128,1024]{1,0:T(8,128)(2,1)S(1)}, u32[]{:S(2)}, u32[]{:S(2)}) collective-permute-start(bf16[128,1024]{1,0:T(8,128)(2,1)S(1)} %copy-done.85), channel_id=1, source_target_pairs={{0,8},{8,0},{16,24},{24,16},{1,9},{9,1},{17,25},{25,17},{2,10},{10... | collective-permute-start | bytes 786440 | tf_op jit(solution)/shard_map/ppermute | solution.py:29
  406.3 10.9 %collective-permute-start.73 = (bf16[128,1024]{1,0:T(8,128)(2,1)S(1)}, bf16[128,1024]{1,0:T(8,128)(2,1)S(1)}, u32[]{:S(2)}, u32[]{:S(2)}) collective-permute-start(bf16[128,1024]{1,0:T(8,128)(2,1)S(1)} %add_convert_fusion.11), channel_id=1, source_target_pairs={{0,16},{8,24},{16,0},{24,8},{1,17},{9,25},{17,1},{25,9},{2,18},{10... | collective-permute-start | bytes 786440 | tf_op jit(solution)/shard_map/ppermute | solution.py:29
  410.2 7.9 %collective-permute-start.77 = (bf16[384,256]{1,0:T(8,128)(2,1)S(1)}, bf16[384,256]{1,0:T(8,128)(2,1)S(1)}, u32[]{:S(2)}, u32[]{:S(2)}) collective-permute-start(bf16[384,256]{1,0:T(8,128)(2,1)S(1)} %slice.30.refs_0_), channel_id=1, source_target_pairs={{0,8},{8,0},{16,24},{24,16},{1,9},{9,1},{17,25},{25,17},{2,10},{10... | collective-permute-start | bytes 589832 | tf_op jit(solution)/shard_map/ppermute | solution.py:29
  410.4 7.7 %collective-permute-start.82 = (bf16[256,256]{1,0:T(8,128)(2,1)S(1)}, bf16[256,256]{1,0:T(8,128)(2,1)S(1)}, u32[]{:S(2)}, u32[]{:S(2)}) collective-permute-start(bf16[256,256]{1,0:T(8,128)(2,1)S(1)} %broadcast_select_fusion.1.refs_4_), channel_id=1, source_target_pairs={{0,8},{8,0},{16,24},{24,16},{1,9},{9,1},{17,25},{25,17},{2,10},{10... | collective-permute-start | bytes 393224 | tf_op jit(solution)/shard_map/ppermute | solution.py:29
  414.5 7.7 %collective-permute-start.88 = (bf16[128,256]{1,0:T(8,128)(2,1)S(1)}, bf16[128,256]{1,0:T(8,128)(2,1)S(1)}, u32[]{:S(2)}, u32[]{:S(2)}) collective-permute-start(bf16[128,256]{1,0:T(8,128)(2,1)S(1)} %slice.33), channel_id=1, source_target_pairs={{0,1},{1,0},{2,3},{3,2},{4,5},{5,4},{6,7},{7,6},{8,9},{9,8},{10,11... | collective-permute-start | bytes 196616 | tf_op jit(solution)/shard_map/ppermute | solution.py:29
  420.0 9.9 %collective-permute-start.86 = (bf16[384,256]{1,0:T(8,128)(2,1)S(1)}, bf16[384,256]{1,0:T(8,128)(2,1)S(1)}, u32[]{:S(2)}, u32[]{:S(2)}) collective-permute-start(bf16[384,256]{1,0:T(8,128)(2,1)S(1)} %slice.32.refs_0_), channel_id=1, source_target_pairs={{0,16},{8,24},{16,0},{24,8},{1,17},{9,25},{17,1},{25,9},{2,18},{10... | collective-permute-start | bytes 589832 | tf_op jit(solution)/shard_map/ppermute | solution.py:29
  420.6 14.5 %collective-permute-start.85 = (bf16[384,256]{1,0:T(8,128)(2,1)S(1)}, bf16[384,256]{1,0:T(8,128)(2,1)S(1)}, u32[]{:S(2)}, u32[]{:S(2)}) collective-permute-start(bf16[384,256]{1,0:T(8,128)(2,1)S(1)} %slice.32.refs_0_), channel_id=1, source_target_pairs={{0,8},{8,0},{16,24},{24,16},{1,9},{9,1},{17,25},{25,17},{2,10},{10... | collective-permute-start | bytes 589832 | tf_op jit(solution)/shard_map/ppermute | solution.py:29
  (130 other events, 738.2 us)
Sparse Core Ops, SparseCore 0:
  19.9 75.2 all-gather.2
  97.9 72.4 all-gather.4
  251.0 99.6 reduce-scatter.1
